TPU v7x, 32 devices: a whole 2x2x4 slice. The times are simulated.
32 devices in a mesh: groups: 2 (over x), rows: 16 (over z, y, core).
Axes of the slice: x: 2, y: 2, z: 4, core: 2. Of those that a mesh axis runs over, the one named last changes fastest.
Arguments:
- samples: bfloat16 [32768, 256], P(('groups', 'rows')), parts along dimension 0
- omega_diag: float32 [256, 128, 128], P(('groups', 'rows')), parts along dimension 0, as said below
- omega_off: float32 [960, 128, 128], P(('groups', 'rows')), parts along dimension 0, as said below
- pattern: int32 [960, 2], P(('groups', 'rows')), parts along dimension 0, may hold values from 0 to 127, as said below
- block_count: int32 [256], P(('groups', 'rows')), parts along dimension 0, may hold values from 0 to 15, as said below
- diag_term: float32 [32768], P(('groups', 'rows')), parts along dimension 0, may hold values from -1 to -0.5
Outputs:
- omega_diag_next: float32 [256, 128, 128], P(('groups', 'rows')), parts along dimension 0
- omega_off_next: float32 [960, 128, 128], P(('groups', 'rows')), parts along dimension 0
- objective: float32 [2], P('groups'), parts along dimension 0
There are 2 independent parts, one for each index of `groups`. A program takes and returns all parts, laid end to end along the dimension named above; each array names one. Nothing has to cross between parts.
Inputs may be any that keep to these rules, and one draw needn't show every extreme that they name: `pattern`: row e names a stored off-diagonal block by its block row i, which lies on the device holding e, and its block column j; for live entries j lies on another device. A device's live entries come first, ordered by block row; the live entries of all devices are symmetric: (j, i) is live wherever (i, j) is, and no pair is named twice. Between the block rows of two devices there are either none or exactly 2 live blocks. Dead entries name the device's first block row twice. The live entries of a device are its first entries, as many as the sum of block_count over its 8 block rows; some device has all 30 entries live. `omega_diag`: each diagonal block is symmetric. Omega is symmetric: for live entries e = (i, j) and f = (j, i), omega_off[f] is the transpose of omega_off[e].
All inputs are finite; a program needn't handle non-finite values.
Results may differ from a plain program's by a relative error of at most 0.0003.
Values may be sent and summed in bfloat16 or wider, within the bound.
No kernel may reach another device: no remote copies, remote signals or barrier semaphores. Data moves between devices by JAX's collectives and lax.ppermute only.
A program may use at most 128 MiB of HBM per device.

v0:
```python
import jax
import jax.numpy as jnp
from jax import lax
from jax.sharding import PartitionSpec as P

SLOTS = 2


STEP_SIZE = 0.5
PENALTY = 0.01


def soften(values, level):
    return values - jnp.clip(values, -level, level)


def scatter_rows(payload, targets, capacity):
    holder = jnp.zeros((capacity,) + payload.shape[1:], payload.dtype)
    return holder.at[targets].set(payload, mode="drop")


def shards(samples, omega_diag, omega_off, pattern, block_count, diag_term):
    devices = lax.axis_size("rows")
    position = lax.axis_index("rows")
    rows_dev = omega_diag.shape[0]
    block_edge = omega_diag.shape[1]
    samples_dev = samples.shape[1]
    entries = omega_off.shape[0]
    block_total = rows_dev * devices
    capacity = devices * SLOTS
    highest = lax.Precision.HIGHEST
    local_samples = samples.reshape(rows_dev, block_edge, samples_dev)
    entry_ids = jnp.arange(entries, dtype=jnp.int32)
    living = entry_ids < jnp.sum(block_count)
    row_glob = pattern[:, 0]
    col_glob = pattern[:, 1]
    row_local = row_glob - position * rows_dev
    owners = col_glob // rows_dev
    send_key = row_glob * block_total + col_glob
    back_key = col_glob * block_total + row_glob
    same_peer = (owners[:, None] == owners[None, :]) & living[None, :]
    send_rank = jnp.sum(same_peer & (send_key[None, :] < send_key[:, None]), axis=1)
    recv_rank = jnp.sum(same_peer & (back_key[None, :] < back_key[:, None]), axis=1)
    send_target = jnp.where(living, owners * SLOTS + send_rank, capacity)
    recv_source = jnp.where(living, owners * SLOTS + recv_rank, 0)
    masked = jnp.where(living[:, None, None], omega_off, 0.0)
    selector = (row_local[None, :] == jnp.arange(rows_dev, dtype=jnp.int32)[:, None]).astype(
        jnp.float32
    )
    arrived = lax.all_to_all(
        scatter_rows(local_samples[row_local], send_target, capacity).reshape(
            devices, SLOTS, block_edge, local_samples.shape[2]
        ),
        "rows",
        split_axis=0,
        concat_axis=0,
        tiled=True,
    )
    columns = local_samples.shape[2]
    fetched = arrived.reshape(capacity, block_edge, columns)[recv_source]
    projected = jnp.einsum(
        "kab,kbn->kan",
        omega_diag,
        local_samples,
        precision=highest,
        preferred_element_type=jnp.float32,
    )
    contributions = jnp.einsum(
        "eab,ebn->ean", masked, fetched, precision=highest, preferred_element_type=jnp.float32
    )
    projected = projected + jnp.einsum("re,ean->ran", selector, contributions, precision=highest)
    off_part = jnp.einsum(
        "ean,ebn->eab",
        projected[row_local],
        fetched,
        precision=highest,
        preferred_element_type=jnp.float32,
    )
    diag_part = jnp.einsum(
        "kan,kbn->kab",
        projected,
        local_samples,
        precision=highest,
        preferred_element_type=jnp.float32,
    )
    squares = jnp.sum(projected * projected)
    flipped_out = scatter_rows(jnp.swapaxes(off_part, 1, 2), send_target, capacity).reshape(
        devices, SLOTS, block_edge, block_edge
    )
    returned = lax.all_to_all(flipped_out, "rows", split_axis=0, concat_axis=0, tiled=True)
    mirrored = returned.reshape(capacity, block_edge, block_edge)[recv_source]
    gradient = (off_part + mirrored) / (2.0 * samples_dev)
    off_next = jnp.where(
        living[:, None, None], soften(omega_off - STEP_SIZE * gradient, STEP_SIZE * PENALTY), 0.0
    )
    identity = jnp.eye(block_edge, dtype=jnp.float32)[None]
    diag_gradient = (diag_part + jnp.swapaxes(diag_part, 1, 2)) / (
        2.0 * samples_dev
    ) + identity * diag_term.reshape(rows_dev, block_edge)[:, :, None]
    moved = omega_diag - STEP_SIZE * diag_gradient
    diag_next = jnp.where(identity > 0.5, moved, soften(moved, STEP_SIZE * PENALTY))
    local_term = squares / (2.0 * samples_dev) - jnp.sum(
        jnp.log(jnp.diagonal(omega_diag, axis1=1, axis2=2))
    )
    total_term = lax.psum(local_term, "rows")
    objective = (total_term / (block_total * block_edge)).reshape(1)
    return (diag_next, off_next, objective)


def solution(mesh):
    return jax.shard_map(
        shards,
        mesh=mesh,
        in_specs=(
            P(("groups", "rows"), None),
            P(("groups", "rows"), None, None),
            P(("groups", "rows"), None, None),
            P(("groups", "rows"), None),
            P(("groups", "rows")),
            P(("groups", "rows")),
        ),
        out_specs=(
            P(("groups", "rows"), None, None),
            P(("groups", "rows"), None, None),
            P("groups"),
        ),
        check_vma=False,
    )
```

profile of v0, /device:TPU:16, one launch (start us, length us, event | category | flops | bytes accessed | tf_op | source)
XLA Modules:
  0.0 181.6 jit_solution(3447105092942988332)
XLA Ops:
  0.6 0.8 fusion.16
  1.4 0.8 bitcast_subtract_fusion
  2.2 1.3 reduce_sum.49
  3.5 0.6 iota_compare_fusion.2
  4.2 0.2 convert_reduce_fusion
  4.3 0.7 fusion.17
  5.0 0.7 gather_fusion
  5.7 1.6 broadcast_in_dim.60
  7.3 5.4 %scatter_fusion = bf16[32,128,256]{2,1,0:T(8,128)(2,1)} fusion(bf16[32,128,256]{2,1,0:T(8,128)(2,1)} %broadcast_in_dim.60, s32[30]{0:T(128)S(1)} %get-tuple-element.14, bf16[30,128,256]{2,1,0:T(8,128)(2,1)S(1)} %gather_fusion), kind=kCustom, calls=%fused_computation.5 | custom fusion | bytes 5898360 | tf_op jit(solution)/shard_map/scatter | solution.py:19
  12.7 6.2 %all-to-all-start = ((bf16[16,2,128,256]{3,2,1,0:T(8,128)(2,1)}), bf16[16,2,128,256]{3,2,1,0:T(8,128)(2,1)S(1)}, u32[]{:S(2)}, u32[]{:S(2)}) async-start(bf16[16,2,128,256]{3,2,1,0:T(8,128)(2,1)} %bitcast.9), calls=%async_computation | async-start | bytes 4194304 | tf_op jit(solution)/shard_map/all_to_all | solution.py:50
  18.9 47.6 %all-to-all-done = bf16[16,2,128,256]{3,2,1,0:T(8,128)(2,1)S(1)} async-done(((bf16[16,2,128,256]{3,2,1,0:T(8,128)(2,1)}), bf16[16,2,128,256]{3,2,1,0:T(8,128)(2,1)S(1)}, u32[]{:S(2)}, u32[]{:S(2)}) %all-to-all-start) | async-done | bytes 2097184 | tf_op jit(solution)/shard_map/all_to_all | solution.py:50
  66.5 1.3 copy-done.2
  67.8 2.3 %gather_fusion.1 = bf16[30,128,256]{2,1,0:T(8,128)(2,1)S(1)} fusion(bf16[32,128,256]{2,1,0:T(8,128)(2,1)} %bitcast.76, s32[1024]{0:T(1024)S(1)} %pad_clamp_fusion), kind=kCustom, calls=%fused_computation.1 | custom fusion | bytes 3932280 | tf_op jit(solution)/shard_map/gather | solution.py:60
  70.1 4.2 %fusion.3 = f32[30,128,256]{2,1,0:T(8,128)S(1)} fusion(bf16[30,128,256]{2,1,0:T(8,128)(2,1)S(1)} %gather_fusion.1, f32[30,128,128]{2,1,0:T(8,128)} %param.8, pred[30]{0:T(512)(128)(4,1)S(1)} %iota_compare_fusion.2), kind=kOutput, calls=%fused_computation.11 | convolution fusion | flops 1510440960 | bytes 7864350 | tf_op jit(solution)/shard_map/eab,ebn->ean/dot_general | solution.py:68
  74.3 3.7 %fusion = f32[8,128,256]{2,0,1:T(8,128)S(1)} fusion(f32[30,128,256]{2,1,0:T(8,128)S(1)} %fusion.3, s32[30]{0:T(128)S(1)} %get-tuple-element.5), kind=kOutput, calls=%fused_computation.7 | convolution fusion | flops 94372080 | bytes 4980856 | tf_op jit(solution)/shard_map/re,ean->ran/dot_general | solution.py:71
  78.0 1.6 multiply_reduce_fusion
  79.6 2.7 %gather_fusion.2 = f32[30,128,256]{2,1,0:T(8,128)} fusion(f32[8,128,256]{2,1,0:T(8,128)S(1)} %get-tuple-element.16, s32[1024]{0:T(1024)S(1)} %pad_clamp_fusion.1), kind=kCustom, calls=%fused_computation.2 | custom fusion | bytes 7864440 | tf_op jit(solution)/shard_map/gather | solution.py:74
  82.3 4.6 %fusion.21 = f32[30,128,128]{2,1,0:T(8,128)S(1)} fusion(f32[30,128,256]{2,1,0:T(8,128)} %gather_fusion.2, bf16[30,128,256]{2,1,0:T(8,128)(2,1)} %copy-done.1), kind=kOutput, calls=%fused_computation.65 | convolution fusion | flops 1509949440 | bytes 7864320 | tf_op jit(solution)/shard_map/ean,ebn->eab/dot_general | solution.py:72
  86.9 1.8 copy.15
  88.7 1.5 broadcast_in_dim.62
  90.3 6.2 %scatter_fusion.1 = f32[32,128,128]{2,1,0:T(8,128)} fusion(f32[32,128,128]{2,1,0:T(8,128)} %broadcast_in_dim.62, s32[30]{0:T(128)S(1)} %get-tuple-element.14, f32[30,128,128]{2,1,0:T(8,128)} %copy.15), kind=kCustom, calls=%fused_computation.6 | custom fusion | bytes 5898360 | tf_op jit(solution)/shard_map/scatter | solution.py:19
  96.4 4.5 %all-to-all-start.1 = ((f32[16,2,128,128]{3,2,1,0:T(8,128)}), f32[16,2,128,128]{3,2,1,0:T(8,128)}, u32[]{:S(2)}, u32[]{:S(2)}) async-start(f32[16,2,128,128]{3,2,1,0:T(8,128)} %bitcast.74), calls=%async_computation.1 | async-start | bytes 4194304 | tf_op jit(solution)/shard_map/all_to_all | solution.py:90
  101.0 5.9 %copy.16 = f32[8,128,128]{0,2,1:T(8,128)} copy(f32[8,128,128]{2,1,0:T(8,128)} %param.7) | data formatting | bytes 1048576 | tf_op args[1]
  106.8 2.4 %gather_fusion.4 = f32[128,8]{1,0:T(8,128)} fusion(f32[8,128,128]{0,2,1:T(8,128)} %copy.16, s32[128]{0:T(128)S(1)} %or_bitcast_fusion), kind=kCustom, calls=%fused_computation.4 | custom fusion | bytes 9216 | tf_op jit(solution)/shard_map/jit(diagonal)/gather | solution.py:103
  109.2 1.5 log_reduce_fusion
  112.0 0.6 fusion.11
  112.6 54.5 %psum.7 = f32[]{:T(128)} all-reduce(f32[]{:T(128)S(6)} %sub.46), channel_id=1, replica_groups=mesh['groups'=2,'rows'=16] {'rows'}, use_global_device_ids=true, to_apply=%region_7.8 | all-reduce | flops 1 | bytes 8 | tf_op jit(solution)/shard_map/psum | solution.py:105
  167.2 1.4 fusion.20
  168.6 1.2 copy.14
  170.5 2.2 %subtract_select_fusion = f32[8,128,128]{2,1,0:T(8,128)} fusion(f32[8,128,128]{2,1,0:T(8,128)} %param.7, f32[8,128,128]{2,1,0:T(8,128)} %fusion.20, f32[8,128,128]{1,2,0:T(8,128)S(1)} %copy.14, f32[8,128]{1,0:T(8,128)} %bitcast.78, f32[128,128]{1,0:T(8,128)} %get-tuple-element.17, pred[128,128]{1,0:T(8,128)(4,1)S(1)} %get-tuple-element.18), kind=kLoop, calls=%fused_computation.17 | loop fusion | flops 1179648 | bytes 2183168 | tf_op jit(solution)/shard_map/jit(_where)/select_n | solution.py:101
  172.7 3.7 %gather_fusion.3 = f32[30,128,128]{2,1,0:T(8,128)} fusion(f32[32,128,128]{2,1,0:T(8,128)} %bitcast.18, s32[1024]{0:T(1024)} %copy-done.4), kind=kCustom, calls=%fused_computation.3 | custom fusion | bytes 3932280 | tf_op jit(solution)/shard_map/gather | solution.py:91
  176.4 4.1 %fusion.2 = f32[30,128,128]{2,1,0:T(8,128)} fusion(f32[30,128,128]{2,1,0:T(8,128)} %param.8, f32[30,128,128]{2,1,0:T(8,128)S(1)} %fusion.21, f32[30,128,128]{2,1,0:T(8,128)} %gather_fusion.3, pred[30]{0:T(512)(128)(4,1)S(1)} %copy-done.6), kind=kLoop, calls=%fused_computation.10 | loop fusion | flops 2949120 | bytes 7864350 | tf_op jit(solution)/shard_map/jit(_where)/select_n | solution.py:93
  (17 shorter events, 0.1 us)
Async XLA Ops:
  0.6 4.4 %copy-start = (bf16[1024,256]{1,0:T(8,128)(2,1)S(1)}, bf16[1024,256]{1,0:T(8,128)(2,1)}, u32[]{:S(2)}) copy-start(bf16[1024,256]{1,0:T(8,128)(2,1)} %param.6) | copy-start | bytes 1572868
  4.1 66.0 %copy-start.5 = (pred[30]{0:T(512)(128)(4,1)}, pred[30]{0:T(512)(128)(4,1)S(1)}, u32[]{:S(2)}) copy-start(pred[30]{0:T(512)(128)(4,1)S(1)} %iota_compare_fusion.2) | copy-start | bytes 94
  12.7 53.8 %all-to-all-start = ((bf16[16,2,128,256]{3,2,1,0:T(8,128)(2,1)}), bf16[16,2,128,256]{3,2,1,0:T(8,128)(2,1)S(1)}, u32[]{:S(2)}, u32[]{:S(2)}) async-start(bf16[16,2,128,256]{3,2,1,0:T(8,128)(2,1)} %bitcast.9), calls=%async_computation | async-start | bytes 4194304 | tf_op jit(solution)/shard_map/all_to_all | solution.py:50
  18.9 55.4 %copy-start.4 = (s32[1024]{0:T(1024)}, s32[1024]{0:T(1024)S(1)}, u32[]{:S(2)}) copy-start(s32[1024]{0:T(1024)S(1)} %pad_clamp_fusion) | copy-start | bytes 12292
  66.5 1.4 copy-start.2
  70.1 4.2 %copy-start.1 = (bf16[30,128,256]{2,1,0:T(8,128)(2,1)}, bf16[30,128,256]{2,1,0:T(8,128)(2,1)S(1)}, u32[]{:S(2)}) copy-start(bf16[30,128,256]{2,1,0:T(8,128)(2,1)S(1)} %gather_fusion.1) | copy-start | bytes 5898244
  74.3 3.7 %copy-start.3 = (f32[8,128,128]{2,1,0:T(8,128)S(1)}, f32[8,128,128]{2,1,0:T(8,128)}, u32[]{:S(2)}) copy-start(f32[8,128,128]{2,1,0:T(8,128)} %param.7) | copy-start | bytes 1572868
  96.4 76.3 %all-to-all-start.1 = ((f32[16,2,128,128]{3,2,1,0:T(8,128)}), f32[16,2,128,128]{3,2,1,0:T(8,128)}, u32[]{:S(2)}, u32[]{:S(2)}) async-start(f32[16,2,128,128]{3,2,1,0:T(8,128)} %bitcast.74), calls=%async_computation.1 | async-start | bytes 4194304 | tf_op jit(solution)/shard_map/all_to_all | solution.py:90
  172.7 3.7 %copy-start.6 = (pred[30]{0:T(512)(128)(4,1)S(1)}, pred[30]{0:T(512)(128)(4,1)}, u32[]{:S(2)}) copy-start(pred[30]{0:T(512)(128)(4,1)} %copy-done.5) | copy-start | bytes 94
where the time goes:
time: 182 us
  blocking collectives  54.5 us (30%)
  waiting for transfers between devices  47.6 us (26%)
  local copies, waits for them, and re-layouts  36.6 us (20%)
  matrix products  15.5 us (9%)
  other arithmetic  12.7 us (7%)
  starting transfers between devices  10.7 us (6%)
  between operations  3.88 us (2%)
    psum x1, blocking collectives, shards(): total_term = lax.psum(local_term, 'rows')  54.5 us
    all_to_all x1, waiting for transfers between devices, shards(): lax.all_to_all(scatter_rows(local_samples[row_local], send_target, capaci...  47.6 us
    scatter x2, local copies, waits for them, and re-layouts, scatter_rows(): return holder.at[targets].set(payload, mode='drop')  11.6 us
    unnamed x15, local copies, waits for them, and re-layouts  7.25 us
    all_to_all x1, starting transfers between devices, shards(): lax.all_to_all(scatter_rows(local_samples[row_local], send_target, capaci...  6.17 us
    dot_general x1, matrix products, shards(): jnp.einsum('ean,ebn->eab', projected[row_local], fetched, precision=highe...  4.62 us
    all_to_all x1, starting transfers between devices, shards(): lax.all_to_all(flipped_out, 'rows', split_axis=0, concat_axis=0, tiled=True)  4.52 us
    dot_general x1, matrix products, shards(): jnp.einsum('eab,ebn->ean', masked, fetched, precision=highest, preferred_...  4.18 us
  transfers between devices with their start and end apart: 2, of which 1 were waited for; matrix products, arithmetic and copies ran while one was open for 8% of the time, Pallas kernels for 0%

commit v1 on v0

v1 whole, which is shorter than its diff:
```python
import functools

import jax
import jax.numpy as jnp
from jax import lax
from jax.experimental import pallas as pl
from jax.experimental.pallas import tpu as pltpu
from jax.sharding import PartitionSpec as P

SLOTS = 2
STAT_ROWS = 8
STEP_SIZE = 0.5
PENALTY = 0.01
LOG_STEPS = 128.0
HEADROOM = 1e-4
FRACTION = 32000.0
VMEM_LIMIT = 60 * 1024 * 1024


def soften(values, level):
    return values - jnp.clip(values, -level, level)


def split_halves(values):
    high = values.astype(jnp.bfloat16)
    low = (values - high.astype(jnp.float32)).astype(jnp.bfloat16)
    return high, low


def unroll_of(entries):
    return max(k for k in range(1, 7) if entries % k == 0)


def live_count(count, rows_dev):
    total = count[0]
    for k in range(1, rows_dev):
        total = total + count[k]
    return total


def pack_kernel(pattern, count, x, send, slots, first, sems, *, rows_dev, devices, entries, block_total):
    live = live_count(count, rows_dev)
    position = pattern[0, 0] // rows_dev
    base = position * rows_dev

    def clear(o, carry):
        first[o] = -1
        return carry

    lax.fori_loop(0, devices, clear, 0)

    def key(e):
        i = pattern[e, 0]
        j = pattern[e, 1]
        return jnp.minimum(i, j) * block_total + jnp.maximum(i, j)

    def copy(e, slot):
        return pltpu.make_async_copy(x.at[pattern[e, 0] - base], send.at[slot], sems.at[e])

    spare = pltpu.make_async_copy(x.at[0], send.at[position * SLOTS], sems.at[entries])
    spare.start()

    def place(e, carry):
        owner = pattern[e, 1] // rows_dev
        earlier = first[owner]

        @pl.when(earlier < 0)
        def _():
            first[owner] = e

        @pl.when(earlier >= 0)
        def _():
            later = jnp.where(key(e) > key(earlier), 1, 0)
            slots[e] = owner * SLOTS + later
            slots[earlier] = owner * SLOTS + 1 - later
            copy(e, owner * SLOTS + later).start()
            copy(earlier, owner * SLOTS + 1 - later).start()

        return carry

    lax.fori_loop(0, live, place, 0)

    def rest(e, carry):
        slots[e] = position * SLOTS
        return carry

    lax.fori_loop(live, entries, rest, 0)
    spare.wait()

    def drain(e, carry):
        copy(e, slots[e]).wait()
        return carry

    lax.fori_loop(0, live, drain, 0)


def own_kernel(x, omega, projected, logs, *, rows_dev, edge):
    on_diagonal = lax.broadcasted_iota(jnp.int32, (edge, edge), 0) == lax.broadcasted_iota(
        jnp.int32, (edge, edge), 1
    )
    total = jnp.zeros((1, edge), jnp.float32)
    for k in range(rows_dev):
        block = omega[k]
        high, low = split_halves(block)
        rows = x[k]
        projected[k] = jnp.dot(
            jnp.concatenate([high, low], axis=1),
            jnp.concatenate([rows, rows], axis=0),
            preferred_element_type=jnp.float32,
        )
        total = total + jnp.log(jnp.sum(jnp.where(on_diagonal, block, 0.0), axis=0, keepdims=True))
    logs[...] = jnp.broadcast_to(total, logs.shape)


def main_kernel(
    pattern,
    count,
    slots,
    own,
    logs,
    arrived,
    omega,
    moved,
    payload,
    projected,
    xs,
    om,
    mv,
    halves,
    stats,
    sem_x,
    sem_o,
    sem_m,
    *,
    rows_dev,
    devices,
    entries,
    edge,
    samples_dev,
):
    live = live_count(count, rows_dev)
    base = (pattern[0, 0] // rows_dev) * rows_dev
    unroll = unroll_of(entries)

    def fetch(e):
        return pltpu.make_async_copy(arrived.at[slots[e]], xs.at[e], sem_x.at[e])

    def fetch_omega(e):
        return pltpu.make_async_copy(omega.at[e], om.at[e], sem_o.at[e])

    def store(e):
        return pltpu.make_async_copy(mv.at[e], moved.at[e], sem_m.at[e])

    def begin(e, carry):
        fetch(e).start()
        fetch_omega(e).start()
        return carry

    lax.fori_loop(0, entries, begin, 0)
    projected[...] = own[...]
    stats[...] = jnp.zeros(stats.shape, jnp.float32)

    def gather(step, carry):
        parts = []
        for k in range(unroll):
            e = step * unroll + k
            fetch(e).wait()
            fetch_omega(e).wait()
            high, low = split_halves(jnp.where(e < live, om[e], 0.0))
            rows = xs[e]
            parts.append(
                jnp.dot(
                    jnp.concatenate([high, low], axis=1),
                    jnp.concatenate([rows, rows], axis=0),
                    preferred_element_type=jnp.float32,
                )
            )
        for k in range(unroll):
            row = pattern[step * unroll + k, 0] - base
            projected[row] = projected[row] + parts[k]
        return carry

    lax.fori_loop(0, entries // unroll, gather, 0)

    squares = jnp.zeros((edge, samples_dev), jnp.float32)
    for k in range(rows_dev):
        values = projected[k]
        squares = squares + values * values
        high, low = split_halves(values)
        halves[k, :edge] = high
        halves[k, edge:] = low

    def products(step, carry):
        for k in range(unroll):
            e = step * unroll + k
            row = pattern[e, 0] - base
            both = lax.dot_general(
                halves[row], xs[e], (((1,), (1,)), ((), ())), preferred_element_type=jnp.float32
            )
            product = both[:edge] + both[edge:]
            mv[e] = om[e] - product * (STEP_SIZE / (2.0 * samples_dev))
            store(e).start()
            largest = jnp.maximum(jnp.max(jnp.abs(product), axis=0, keepdims=True), 1e-30)
            code = jnp.ceil(jnp.log2(largest) * LOG_STEPS + 0.01)
            scaled = product * jnp.exp2(15.0 - HEADROOM - code * (1.0 / LOG_STEPS))
            slot = slots[e]
            owner = slot // SLOTS
            rank = slot - owner * SLOTS
            payload[owner, pl.ds(pl.multiple_of(rank * edge, edge), edge), :] = (
                jnp.round(scaled).astype(jnp.int32).astype(jnp.int16)
            )
            stats[owner, pl.ds(rank, 1), :] = code
        return carry

    lax.fori_loop(0, entries // unroll, products, 0)

    term = jnp.sum(squares) * (1.0 / (2.0 * samples_dev)) - jnp.sum(logs[0:1, :])
    term = jnp.full((1, edge), term, jnp.float32)
    power = jnp.ceil(jnp.log2(jnp.maximum(jnp.abs(term), 1e-30)) + 0.01)
    scaled = term * jnp.exp2(14.0 - power)
    whole = jnp.round(scaled)
    digits = jnp.concatenate(
        [
            jnp.zeros((SLOTS, edge), jnp.float32),
            power,
            whole,
            jnp.round((scaled - whole) * FRACTION),
            jnp.zeros((STAT_ROWS - SLOTS - 3, edge), jnp.float32),
        ],
        axis=0,
    )
    payload[:, SLOTS * edge :, :] = (stats[...] + digits[None]).astype(jnp.int32).astype(jnp.int16)

    def finish(e, carry):
        store(e).wait()
        return carry

    lax.fori_loop(0, entries, finish, 0)


def diagonal_kernel(x, omega, term, projected, result, *, rows_dev, edge, samples_dev):
    on_diagonal = lax.broadcasted_iota(jnp.int32, (edge, edge), 0) == lax.broadcasted_iota(
        jnp.int32, (edge, edge), 1
    )
    for k in range(rows_dev):
        high, low = split_halves(projected[k])
        both = lax.dot_general(
            jnp.concatenate([high, low], axis=0),
            x[k],
            (((1,), (1,)), ((), ())),
            preferred_element_type=jnp.float32,
        )
        product = both[:edge] + both[edge:]
        gradient = (product + product.T) * (1.0 / (2.0 * samples_dev))
        gradient = gradient + jnp.where(on_diagonal, term[k : k + 1, :], 0.0)
        value = omega[k] - STEP_SIZE * gradient
        result[k] = jnp.where(on_diagonal, value, soften(value, STEP_SIZE * PENALTY))


def last_kernel(
    count,
    slots,
    moved,
    returned,
    result,
    objective,
    mv,
    rt,
    rs,
    sem_m,
    sem_r,
    sem_o,
    *,
    rows_dev,
    devices,
    entries,
    edge,
    samples_dev,
):
    live = live_count(count, rows_dev)
    unroll = unroll_of(entries)

    def fetch(e):
        return pltpu.make_async_copy(moved.at[e], mv.at[e], sem_m.at[e])

    def store(e):
        return pltpu.make_async_copy(rs.at[e], result.at[e], sem_o.at[e])

    whole = pltpu.make_async_copy(returned, rt, sem_r.at[0])
    whole.start()

    def begin(e, carry):
        fetch(e).start()
        return carry

    lax.fori_loop(0, entries, begin, 0)
    whole.wait()

    def update(step, carry):
        for k in range(unroll):
            e = step * unroll + k
            fetch(e).wait()
            slot = slots[e]
            owner = slot // SLOTS
            rank = slot - owner * SLOTS
            codes = rt[owner, SLOTS * edge :, :].astype(jnp.int32).astype(jnp.float32)
            code = jnp.where(rank == 0, codes[0:1], codes[1:2])
            digits = rt[owner, pl.ds(pl.multiple_of(rank * edge, edge), edge), :]
            mirrored = digits.astype(jnp.int32).astype(jnp.float32) * jnp.exp2(
                code * (1.0 / LOG_STEPS) - (15.0 - HEADROOM)
            )
            value = mv[e] - mirrored.T * (STEP_SIZE / (2.0 * samples_dev))
            rs[e] = jnp.where(e < live, soften(value, STEP_SIZE * PENALTY), 0.0)
            store(e).start()
        return carry

    lax.fori_loop(0, entries // unroll, update, 0)
    codes = rt[:, SLOTS * edge :, :].astype(jnp.int32).astype(jnp.float32)
    power = codes[:, SLOTS : SLOTS + 1]
    digits = codes[:, SLOTS + 1 : SLOTS + 2] + codes[:, SLOTS + 2 : SLOTS + 3] * (1.0 / FRACTION)
    total = jnp.sum(digits * jnp.exp2(power - 14.0), axis=0)
    objective[...] = jnp.broadcast_to(
        total * (1.0 / (devices * rows_dev * edge)), objective.shape
    )

    def finish(e, carry):
        store(e).wait()
        return carry

    lax.fori_loop(0, entries, finish, 0)


def shards(samples, omega_diag, omega_off, pattern, block_count, diag_term):
    devices = lax.axis_size("rows")
    rows_dev, edge = omega_diag.shape[:2]
    samples_dev = samples.shape[1]
    entries = omega_off.shape[0]
    capacity = devices * SLOTS
    f32 = jnp.float32
    x = samples.reshape(rows_dev, edge, samples_dev)
    term = diag_term.reshape(rows_dev, edge)
    smem = pl.BlockSpec(memory_space=pltpu.SMEM)
    vmem = pl.BlockSpec(memory_space=pltpu.VMEM)
    hbm = pl.BlockSpec(memory_space=pl.ANY)
    dma = pltpu.SemaphoreType.DMA
    params = pltpu.CompilerParams(vmem_limit_bytes=VMEM_LIMIT)

    send, slots = pl.pallas_call(
        functools.partial(
            pack_kernel,
            rows_dev=rows_dev,
            devices=devices,
            entries=entries,
            block_total=rows_dev * devices,
        ),
        out_shape=(
            jax.ShapeDtypeStruct((capacity, edge, samples_dev), samples.dtype),
            jax.ShapeDtypeStruct((entries,), jnp.int32),
        ),
        in_specs=[smem, smem, vmem],
        out_specs=(hbm, smem),
        scratch_shapes=[pltpu.SMEM((devices,), jnp.int32), dma((entries + 1,))],
        compiler_params=params,
        name="pack",
    )(pattern, block_count, x)

    arrived = lax.all_to_all(
        send.reshape(devices, SLOTS, edge, samples_dev),
        "rows",
        split_axis=0,
        concat_axis=0,
        tiled=True,
    ).reshape(capacity, edge, samples_dev)

    own, logs = pl.pallas_call(
        functools.partial(own_kernel, rows_dev=rows_dev, edge=edge),
        out_shape=(
            jax.ShapeDtypeStruct((rows_dev, edge, samples_dev), f32),
            jax.ShapeDtypeStruct((8, edge), f32),
        ),
        in_specs=[vmem, vmem],
        out_specs=(vmem, vmem),
        compiler_params=params,
        cost_estimate=pl.CostEstimate(
            flops=4 * rows_dev * edge * edge * samples_dev, transcendentals=0, bytes_accessed=1 << 21
        ),
        name="own",
    )(x, omega_diag)

    moved, payload, projected = pl.pallas_call(
        functools.partial(
            main_kernel,
            rows_dev=rows_dev,
            devices=devices,
            entries=entries,
            edge=edge,
            samples_dev=samples_dev,
        ),
        out_shape=(
            jax.ShapeDtypeStruct((entries, edge, edge), f32),
            jax.ShapeDtypeStruct((devices, SLOTS * edge + STAT_ROWS, edge), jnp.int16),
            jax.ShapeDtypeStruct((rows_dev, edge, samples_dev), f32),
        ),
        in_specs=[smem, smem, smem, vmem, vmem, hbm, hbm],
        out_specs=(hbm, vmem, vmem),
        scratch_shapes=[
            pltpu.VMEM((entries, edge, samples_dev), samples.dtype),
            pltpu.VMEM((entries, edge, edge), f32),
            pltpu.VMEM((entries, edge, edge), f32),
            pltpu.VMEM((rows_dev, 2 * edge, samples_dev), jnp.bfloat16),
            pltpu.VMEM((devices, STAT_ROWS, edge), f32),
            dma((entries,)),
            dma((entries,)),
            dma((entries,)),
        ],
        compiler_params=params,
        name="main",
    )(pattern, block_count, slots, own, logs, arrived, omega_off)

    returned = lax.all_to_all(payload, "rows", split_axis=0, concat_axis=0, tiled=True)

    diag_next = pl.pallas_call(
        functools.partial(diagonal_kernel, rows_dev=rows_dev, edge=edge, samples_dev=samples_dev),
        out_shape=jax.ShapeDtypeStruct((rows_dev, edge, edge), f32),
        in_specs=[vmem, vmem, vmem, vmem],
        out_specs=vmem,
        compiler_params=params,
        cost_estimate=pl.CostEstimate(
            flops=4 * rows_dev * edge * edge * samples_dev, transcendentals=0, bytes_accessed=1 << 21
        ),
        name="diagonal",
    )(x, omega_diag, term, projected)

    off_next, objective = pl.pallas_call(
        functools.partial(
            last_kernel,
            rows_dev=rows_dev,
            devices=devices,
            entries=entries,
            edge=edge,
            samples_dev=samples_dev,
        ),
        out_shape=(
            jax.ShapeDtypeStruct((entries, edge, edge), f32),
            jax.ShapeDtypeStruct((8, edge), f32),
        ),
        in_specs=[smem, smem, hbm, hbm],
        out_specs=(hbm, vmem),
        scratch_shapes=[
            pltpu.VMEM((entries, edge, edge), f32),
            pltpu.VMEM((devices, SLOTS * edge + STAT_ROWS, edge), jnp.int16),
            pltpu.VMEM((entries, edge, edge), f32),
            dma((entries,)),
            dma((1,)),
            dma((entries,)),
        ],
        compiler_params=params,
        name="last",
    )(block_count, slots, moved, returned)
    return diag_next, off_next, objective[0, :1]


def solution(mesh):
    return jax.shard_map(
        shards,
        mesh=mesh,
        in_specs=(
            P(("groups", "rows"), None),
            P(("groups", "rows"), None, None),
            P(("groups", "rows"), None, None),
            P(("groups", "rows"), None),
            P(("groups", "rows")),
            P(("groups", "rows")),
        ),
        out_specs=(
            P(("groups", "rows"), None, None),
            P(("groups", "rows"), None, None),
            P("groups"),
        ),
        check_vma=False,
    )
```

time: 182 us -> 114 us (0.63)
  blocking collectives: 54.5 us -> 0 us
  local copies, waits for them, and re-layouts: 36.6 us -> 4.89 us
  Pallas kernels: 0 us -> 29.3 us
  waiting for transfers between devices: 47.6 us -> 68.1 us
  matrix products: 15.5 us -> 0 us
  other arithmetic: 12.7 us -> 0 us
  between operations: 3.88 us -> 0.66 us
    psum x1 -> x0, blocking collectives: 54.5 us -> none  [shards(): total_term = lax.psum(local_term, 'rows')]
    pallas_call x0 -> x5, Pallas kernels: none -> 29.3 us  [the longest x1 12.7 us: shards(): pl.pallas_call(functools.partial(main_kernel, rows_dev=rows_dev, devices=...]
    all_to_all x2, waiting for transfers between devices: 47.6 us -> 68.1 us  [the longest x1 45.1 us: shards(): lax.all_to_all(send.reshape(devices, SLOTS, edge, samples_dev), 'rows', s...]
    dot_general x5 -> x0, matrix products: 15.5 us -> none  [the longest x1 4.62 us: shards(): jnp.einsum('ean,ebn->eab', projected[row_local], fetched, precision=highe...]
    gather x5 -> x0, local copies, waits for them, and re-layouts: 11.7 us -> none  [the longest x1 3.66 us: shards(): mirrored = returned.reshape(capacity, block_edge, block_edge)[recv_source]]
    scatter x2 -> x0, local copies, waits for them, and re-layouts: 11.6 us -> none  [scatter_rows(): return holder.at[targets].set(payload, mode='drop')]
    select_n x4 -> x0, other arithmetic: 7.7 us -> none  [the longest x1 4.05 us: shards(): jnp.where(living[:, None, None], soften(omega_off - STEP_SIZE * gradient,...]
    unnamed x15 -> x5, local copies, waits for them, and re-layouts: 7.25 us -> 3.69 us
  transfers between devices with their start and end apart: 2 -> 2, of which waited for: 1 -> 2; matrix products, arithmetic and copies ran while one was open for 8% -> 0% of each run, Pallas kernels for 0% -> 5%
where the time goes in v1:
time: 114 us
  waiting for transfers between devices  68.1 us (60%)
  Pallas kernels  29.3 us (26%)
  starting transfers between devices  10.7 us (9%)
  local copies, waits for them, and re-layouts  4.89 us (4%)
    all_to_all x1, waiting for transfers between devices, shards(): lax.all_to_all(send.reshape(devices, SLOTS, edge, samples_dev), 'rows', s...  45.1 us
    all_to_all x1, waiting for transfers between devices, shards(): lax.all_to_all(payload, 'rows', split_axis=0, concat_axis=0, tiled=True)  23 us
    pallas_call x1, Pallas kernels, shards(): pl.pallas_call(functools.partial(main_kernel, rows_dev=rows_dev, devices=...  12.7 us
    pallas_call x1, Pallas kernels, shards(): pl.pallas_call(functools.partial(last_kernel, rows_dev=rows_dev, devices=...  7.46 us
    all_to_all x1, starting transfers between devices, shards(): lax.all_to_all(send.reshape(devices, SLOTS, edge, samples_dev), 'rows', s...  6.08 us
    all_to_all x1, starting transfers between devices, shards(): lax.all_to_all(payload, 'rows', split_axis=0, concat_axis=0, tiled=True)  4.6 us
    pallas_call x1, Pallas kernels, shards(): pl.pallas_call(functools.partial(pack_kernel, rows_dev=rows_dev, devices=...  3.78 us
    unnamed x5, local copies, waits for them, and re-layouts  3.69 us
  transfers between devices with their start and end apart: 2, of which 2 were waited for; matrix products, arithmetic and copies ran while one was open for 0% of the time, Pallas kernels for 5%

profile of v1, /device:TPU:16, one launch (start us, length us, event | category | flops | bytes accessed | tf_op | source)
XLA Modules:
  0.0 113.7 jit_solution(1235938575140547150)
XLA Ops:
  0.6 1.4 %copy.10.pattern = s32[30,2]{1,0:T(8,128)} copy(s32[30,2]{0,1:T(2,128)} %param.9) | data formatting | bytes 480 | tf_op args[3]
  2.0 3.8 %pack.1 = (bf16[32,128,256]{2,1,0:T(8,128)(2,1)}, s32[30]{0:T(128)}) custom-call(s32[30,2]{1,0:T(8,128)} %copy.10.pattern, s32[8]{0:T(128)} %count.5, bf16[8,128,256]{2,1,0:T(8,128)(2,1)} %bitcast.6), custom_call_target="tpu_custom_call" | custom-call | tf_op jit(solution)/shard_map/pack/pallas_call | solution.py:348
  5.8 6.1 %all-to-all-start = ((bf16[16,2,128,256]{3,2,1,0:T(8,128)(2,1)}), bf16[16,2,128,256]{3,2,1,0:T(8,128)(2,1)S(1)}, u32[]{:S(2)}, u32[]{:S(2)}) async-start(bf16[16,2,128,256]{3,2,1,0:T(8,128)(2,1)} %bitcast.9), calls=%async_computation | async-start | bytes 4194304 | tf_op jit(solution)/shard_map/all_to_all | solution.py:367
  11.9 2.5 %own.1 = (f32[8,128,256]{2,1,0:T(8,128)}, f32[8,128]{1,0:T(8,128)}) custom-call(bf16[8,128,256]{2,1,0:T(8,128)(2,1)} %bitcast.7, f32[8,128,128]{2,1,0:T(8,128)} %omega.5), custom_call_target="tpu_custom_call" | custom-call | flops 134217728 | bytes 2097152 | tf_op jit(solution)/shard_map/own/pallas_call | solution.py:375
  14.3 45.1 %all-to-all-done = bf16[16,2,128,256]{3,2,1,0:T(8,128)(2,1)S(1)} async-done(((bf16[16,2,128,256]{3,2,1,0:T(8,128)(2,1)}), bf16[16,2,128,256]{3,2,1,0:T(8,128)(2,1)S(1)}, u32[]{:S(2)}, u32[]{:S(2)}) %all-to-all-start) | async-done | bytes 2097184 | tf_op jit(solution)/shard_map/all_to_all | solution.py:367
  59.5 0.0 copy-start
  59.5 1.3 %copy-done = bf16[16,2,128,256]{3,2,1,0:T(8,128)(2,1)} copy-done((bf16[16,2,128,256]{3,2,1,0:T(8,128)(2,1)}, bf16[16,2,128,256]{3,2,1,0:T(8,128)(2,1)S(1)}, u32[]{:S(2)}) %copy-start) | copy-done | bytes 2097176
  60.8 12.7 %main.1 = (f32[30,128,128]{2,1,0:T(8,128)}, s16[16,264,128]{2,1,0:T(8,128)(2,1)}, f32[8,128,256]{2,1,0:T(8,128)}) custom-call(s32[30,2]{1,0:T(8,128)} %copy.10.pattern, s32[8]{0:T(128)} %count.5, s32[30]{0:T(128)} %get-tuple-element.12.slots, f32[8,128,256]{2,1,0:T(8,128)} %get-tuple-element.13.own, f32[8,128]{1,0:T(8,128)} %get-tuple-element.14.logs, ...), custom_call_target="tpu_custom_call" | custom-call | tf_op jit(solution)/shard_map/main/pallas_call | solution.py:390
  73.6 4.6 %all-to-all-start.1 = ((s16[16,264,128]{2,1,0:T(8,128)(2,1)}), s16[16,264,128]{2,1,0:T(8,128)(2,1)S(1)}, u32[]{:S(2)}, u32[]{:S(2)}) async-start(s16[16,264,128]{2,1,0:T(8,128)(2,1)} %get-tuple-element.18), calls=%async_computation.1 | async-start | bytes 2162688 | tf_op jit(solution)/shard_map/all_to_all | solution.py:420
  78.2 2.9 %diagonal.1 = f32[8,128,128]{2,1,0:T(8,128)} custom-call(bf16[8,128,256]{2,1,0:T(8,128)(2,1)} %bitcast.8, f32[8,128,128]{2,1,0:T(8,128)} %omega.5, f32[8,128]{1,0:T(8,128)} %bitcast.10, f32[8,128,256]{2,1,0:T(8,128)} %get-tuple-element.16.projected), custom_call_target="tpu_custom_call" | custom-call | flops 134217728 | bytes 2097152 | tf_op jit(solution)/shard_map/diagonal/pallas_call | solution.py:422
  81.1 23.0 %all-to-all-done.1.returned = s16[16,264,128]{2,1,0:T(8,128)(2,1)S(1)} async-done(((s16[16,264,128]{2,1,0:T(8,128)(2,1)}), s16[16,264,128]{2,1,0:T(8,128)(2,1)S(1)}, u32[]{:S(2)}, u32[]{:S(2)}) %all-to-all-start.1) | async-done | bytes 1081376 | tf_op jit(solution)/shard_map/all_to_all | solution.py:420
  104.0 0.0 copy-start.1
  104.0 1.0 copy-done.1
  105.0 7.5 %last.1 = (f32[30,128,128]{2,1,0:T(8,128)}, f32[8,128]{1,0:T(8,128)}) custom-call(s32[8]{0:T(128)} %count.5, s32[30]{0:T(128)} %get-tuple-element.12.slots, f32[30,128,128]{2,1,0:T(8,128)} %get-tuple-element.17.moved, s16[16,264,128]{2,1,0:T(8,128)(2,1)} %copy-done.1), custom_call_target="tpu_custom_call" | custom-call | tf_op jit(solution)/shard_map/last/pallas_call | solution.py:434
  112.5 1.2 %slice.3 = f32[1,1]{1,0:T(1,128)} slice(f32[8,128]{1,0:T(8,128)} %get-tuple-element.20), slice={[0:1], [0:1]} | slice | bytes 8 | tf_op jit(solution)/shard_map/slice | solution.py:460
Async XLA Ops:
  5.8 53.7 %all-to-all-start = ((bf16[16,2,128,256]{3,2,1,0:T(8,128)(2,1)}), bf16[16,2,128,256]{3,2,1,0:T(8,128)(2,1)S(1)}, u32[]{:S(2)}, u32[]{:S(2)}) async-start(bf16[16,2,128,256]{3,2,1,0:T(8,128)(2,1)} %bitcast.9), calls=%async_computation | async-start | bytes 4194304 | tf_op jit(solution)/shard_map/all_to_all | solution.py:367
  59.5 1.3 %copy-start = (bf16[16,2,128,256]{3,2,1,0:T(8,128)(2,1)}, bf16[16,2,128,256]{3,2,1,0:T(8,128)(2,1)S(1)}, u32[]{:S(2)}) copy-start(bf16[16,2,128,256]{3,2,1,0:T(8,128)(2,1)S(1)} %all-to-all-done) | copy-start | bytes 6291460
  73.6 30.4 %all-to-all-start.1 = ((s16[16,264,128]{2,1,0:T(8,128)(2,1)}), s16[16,264,128]{2,1,0:T(8,128)(2,1)S(1)}, u32[]{:S(2)}, u32[]{:S(2)}) async-start(s16[16,264,128]{2,1,0:T(8,128)(2,1)} %get-tuple-element.18), calls=%async_computation.1 | async-start | bytes 2162688 | tf_op jit(solution)/shard_map/all_to_all | solution.py:420
  104.0 1.0 copy-start.1

commit v2 on v1

v2 whole, which is shorter than its diff:
```python
import functools

import jax
import jax.numpy as jnp
from jax import lax
from jax.experimental import pallas as pl
from jax.experimental.pallas import tpu as pltpu
from jax.sharding import PartitionSpec as P

SLOTS = 2
STAT_ROWS = 8
STEP_SIZE = 0.5
PENALTY = 0.01
LOG_STEPS = 128.0
HEADROOM = 1e-4
FRACTION = 32000.0
VMEM_LIMIT = 40 * 1024 * 1024
VMEM_ALONE = 60 * 1024 * 1024


def soften(values, level):
    return values - jnp.clip(values, -level, level)


def split_halves(values):
    high = values.astype(jnp.bfloat16)
    low = (values - high.astype(jnp.float32)).astype(jnp.bfloat16)
    return high, low


def divide(value, by):
    if by & (by - 1):
        return value // by
    return lax.shift_right_logical(value, by.bit_length() - 1)


def parts_of(entries, head):
    first = max(1, entries // 5)
    first = first if head else entries - first
    return ((0, first), (first, entries - first))


def live_count(count, rows_dev):
    total = count[0]
    for k in range(1, rows_dev):
        total = total + count[k]
    return total


def pack_kernel(pattern, count, x, send, slots, sums, sems, *, rows_dev, devices, entries, block_total):
    live = live_count(count, rows_dev)
    position = divide(pattern[0, 0], rows_dev)
    base = position * rows_dev

    def key(e):
        i = pattern[0, e]
        j = pattern[1, e]
        return jnp.minimum(i, j) * block_total + jnp.maximum(i, j)

    def copy(e):
        return pltpu.make_async_copy(x.at[pattern[0, e] - base], send.at[slots[e]], sems.at[e])

    spare = pltpu.make_async_copy(x.at[0], send.at[position * SLOTS], sems.at[entries])
    spare.start()
    for o in range(devices):
        sums[o] = 0
    for e in range(entries):
        owner = divide(pattern[1, e], rows_dev)
        sums[owner] = sums[owner] + key(e)
    for e in range(entries):
        owner = divide(pattern[1, e], rows_dev)
        later = jnp.where((2 * key(e) > sums[owner]) & (e < live), 1, 0)
        slots[e] = owner * SLOTS + later

    def begin(e, carry):
        copy(e).start()
        return carry

    def finish(e, carry):
        copy(e).wait()
        return carry

    lax.fori_loop(0, live, begin, 0)
    spare.wait()
    lax.fori_loop(0, live, finish, 0)


def own_kernel(count, x, omega, off, projected, logs, wide, *, rows_dev, entries, edge):
    live = live_count(count, rows_dev)
    on_diagonal = lax.broadcasted_iota(jnp.int32, (edge, edge), 0) == lax.broadcasted_iota(
        jnp.int32, (edge, edge), 1
    )
    total = jnp.zeros((1, edge), jnp.float32)
    for k in range(rows_dev):
        block = omega[k]
        high, low = split_halves(block)
        rows = x[k]
        projected[k] = jnp.dot(
            jnp.concatenate([high, low], axis=1),
            jnp.concatenate([rows, rows], axis=0),
            preferred_element_type=jnp.float32,
        )
        total = total + jnp.log(jnp.sum(jnp.where(on_diagonal, block, 0.0), axis=0, keepdims=True))
    logs[...] = jnp.broadcast_to(total, logs.shape)

    def widen(e, carry):
        high, low = split_halves(jnp.where(e < live, off[e], 0.0))
        wide[e, :, :edge] = high
        wide[e, :, edge:] = low
        return carry

    lax.fori_loop(0, entries, widen, 0)


def main_kernel(
    pattern,
    count,
    slots,
    logs,
    arrived,
    own,
    wide,
    payload,
    projected,
    held_wide,
    held_own,
    held_rows,
    halves,
    coded,
    stats,
    tail,
    sem_wide,
    sem_own,
    sem_rows,
    sem_code,
    *,
    rows_dev,
    devices,
    entries,
    edge,
    samples_dev,
):
    live = live_count(count, rows_dev)
    base = divide(pattern[0, 0], rows_dev) * rows_dev
    fetches = []
    for at, (start, size) in enumerate(parts_of(entries, True)):
        part = pl.ds(start, size)
        fetches.append(pltpu.make_async_copy(wide.at[part], held_wide.at[part], sem_wide.at[at]))
        fetches[-1].start()
    fetch_own = pltpu.make_async_copy(own, held_own, sem_own.at[0])
    fetch_own.start()
    held_rows[...] = jnp.zeros(held_rows.shape, jnp.float32)
    stats[...] = jnp.zeros(stats.shape, jnp.float32)

    for at, (start, size) in enumerate(parts_of(entries, True)):
        fetches[at].wait()
        for e in range(start, start + size):
            rows = arrived[slots[e]]
            part = jnp.dot(
                held_wide[e],
                jnp.concatenate([rows, rows], axis=0),
                preferred_element_type=jnp.float32,
            )
            row = pattern[0, e] - base
            held_rows[row] = held_rows[row] + part

    fetch_own.wait()
    squares = jnp.zeros((8, samples_dev), jnp.float32)
    for k in range(rows_dev):
        values = held_rows[k] + held_own[k]
        held_own[k] = values
        squares = squares + jnp.sum((values * values).reshape(edge // 8, 8, samples_dev), axis=0)
        high, low = split_halves(values)
        halves[k, :edge] = high
        halves[k, edge:] = low
    store_rows = pltpu.make_async_copy(held_own, projected, sem_rows.at[0])
    store_rows.start()

    def store(e):
        slot = slots[e]
        owner = divide(slot, SLOTS)
        rank = slot - owner * SLOTS
        return pltpu.make_async_copy(
            coded.at[e],
            payload.at[owner, pl.ds(pl.multiple_of(rank * edge, edge), edge), :],
            sem_code.at[e],
        )

    for start, size in parts_of(entries, False):
        for e in range(start, start + size):
            row = pattern[0, e] - base
            slot = slots[e]
            both = lax.dot_general(
                arrived[slot],
                halves[row],
                (((1,), (1,)), ((), ())),
                preferred_element_type=jnp.float32,
            )
            product = both[:, :edge] + both[:, edge:]
            largest = jnp.maximum(jnp.max(jnp.abs(product), axis=0, keepdims=True), 1e-30)
            code = jnp.ceil(jnp.log2(largest) * LOG_STEPS + 0.01)
            scaled = product * jnp.exp2(15.0 - HEADROOM - code * (1.0 / LOG_STEPS))
            owner = divide(slot, SLOTS)
            rank = slot - owner * SLOTS
            coded[e] = jnp.round(scaled).astype(jnp.int32).astype(jnp.int16)
            stats[owner, pl.ds(rank, 1), :] = code

        def begin(e, carry):
            store(e).start()
            return carry

        lax.fori_loop(start, jnp.clip(live, start, start + size), begin, 0)

    term = jnp.sum(squares) * (1.0 / (2.0 * samples_dev)) - jnp.sum(logs[0:1, :])
    term = jnp.full((1, edge), term, jnp.float32)
    power = jnp.ceil(jnp.log2(jnp.maximum(jnp.abs(term), 1e-30)) + 0.01)
    scaled = term * jnp.exp2(14.0 - power)
    whole = jnp.round(scaled)
    digits = jnp.concatenate(
        [
            jnp.zeros((SLOTS, edge), jnp.float32),
            power,
            whole,
            jnp.round((scaled - whole) * FRACTION),
            jnp.zeros((STAT_ROWS - SLOTS - 3, edge), jnp.float32),
        ],
        axis=0,
    )
    tail[...] = (stats[...] + digits[None]).astype(jnp.int32).astype(jnp.int16)
    store_tail = pltpu.make_async_copy(
        tail, payload.at[:, pl.ds(SLOTS * edge, STAT_ROWS), :], sem_code.at[entries]
    )
    store_tail.start()

    def finish(e, carry):
        store(e).wait()
        return carry

    lax.fori_loop(0, live, finish, 0)
    store_rows.wait()
    store_tail.wait()


def side_kernel(
    pattern,
    count,
    slots,
    x,
    omega,
    term,
    projected,
    off,
    arrived,
    result,
    moved,
    halves,
    *,
    rows_dev,
    entries,
    edge,
    samples_dev,
):
    live = live_count(count, rows_dev)
    base = divide(pattern[0, 0], rows_dev) * rows_dev
    on_diagonal = lax.broadcasted_iota(jnp.int32, (edge, edge), 0) == lax.broadcasted_iota(
        jnp.int32, (edge, edge), 1
    )

    def against(row, other):
        both = lax.dot_general(
            halves[row], other, (((1,), (1,)), ((), ())), preferred_element_type=jnp.float32
        )
        return both[:edge] + both[edge:]

    for k in range(rows_dev):
        high, low = split_halves(projected[k])
        halves[k, :edge] = high
        halves[k, edge:] = low
        product = against(k, x[k])
        gradient = (product + product.T) * (1.0 / (2.0 * samples_dev))
        gradient = gradient + jnp.where(on_diagonal, term[k : k + 1, :], 0.0)
        value = omega[k] - STEP_SIZE * gradient
        result[k] = jnp.where(on_diagonal, value, soften(value, STEP_SIZE * PENALTY))

    def move(e, carry):
        product = against(pattern[0, e] - base, arrived[slots[e]])
        value = off[e] - product * (STEP_SIZE / (2.0 * samples_dev))
        moved[e] = jnp.where(e < live, value, 0.0)
        return carry

    lax.fori_loop(0, entries, move, 0)


def last_kernel(
    count,
    slots,
    moved,
    returned,
    result,
    objective,
    held,
    rs,
    sem_in,
    sem_out,
    *,
    rows_dev,
    devices,
    entries,
    edge,
    samples_dev,
):
    live = live_count(count, rows_dev)

    def fetch(at, part):
        return pltpu.make_async_copy(moved.at[part], held.at[part], sem_in.at[at])

    def store(at, part):
        return pltpu.make_async_copy(rs.at[part], result.at[part], sem_out.at[at])

    width = max(k for k in range(1, 11) if entries % k == 0)
    parts = [(at, pl.ds(at * width, width)) for at in range(entries // width)]
    for at, part in parts:
        fetch(at, part).start()
    codes = returned[:, SLOTS * edge :, :].astype(jnp.int32).astype(jnp.float32)
    power = codes[:, SLOTS : SLOTS + 1]
    digits = codes[:, SLOTS + 1 : SLOTS + 2] + codes[:, SLOTS + 2 : SLOTS + 3] * (1.0 / FRACTION)
    total = jnp.sum(digits * jnp.exp2(power - 14.0), axis=0)
    objective[0] = jnp.max(total) * (1.0 / (devices * rows_dev * edge))
    for at, part in parts:
        fetch(at, part).wait()
        for e in range(at * width, (at + 1) * width):
            slot = slots[e]
            owner = divide(slot, SLOTS)
            rank = slot - owner * SLOTS
            codes = returned[owner, SLOTS * edge :, :].astype(jnp.int32).astype(jnp.float32)
            code = jnp.where(rank == 0, codes[0:1], codes[1:2])
            weight = jnp.exp2(code * (1.0 / LOG_STEPS) - (15.0 - HEADROOM)) * (
                STEP_SIZE / (2.0 * samples_dev)
            )
            weight = jnp.where(e < live, weight, 0.0)
            digits = returned[owner, pl.ds(pl.multiple_of(rank * edge, edge), edge), :]
            value = held[e] - digits.astype(jnp.int32).astype(jnp.float32) * weight
            rs[e] = soften(value, STEP_SIZE * PENALTY)
        store(at, part).start()
    for at, part in parts:
        store(at, part).wait()


def shards(samples, omega_diag, omega_off, pattern, block_count, diag_term):
    devices = lax.axis_size("rows")
    rows_dev, edge = omega_diag.shape[:2]
    samples_dev = samples.shape[1]
    entries = omega_off.shape[0]
    capacity = devices * SLOTS
    f32 = jnp.float32
    x = samples.reshape(rows_dev, edge, samples_dev)
    term = diag_term.reshape(rows_dev, edge)
    pattern = pattern.T
    smem = pl.BlockSpec(memory_space=pltpu.SMEM)
    vmem = pl.BlockSpec(memory_space=pltpu.VMEM)
    hbm = pl.BlockSpec(memory_space=pltpu.HBM)
    params = pltpu.CompilerParams(vmem_limit_bytes=VMEM_LIMIT)
    alone = pltpu.CompilerParams(vmem_limit_bytes=VMEM_ALONE)
    sizes = dict(rows_dev=rows_dev, entries=entries, edge=edge)
    every = dict(sizes, devices=devices, samples_dev=samples_dev)
    held = functools.partial(pltpu.with_memory_space_constraint, memory_space=pltpu.VMEM)
    kept = functools.partial(pltpu.with_memory_space_constraint, memory_space=pltpu.HBM)

    dma = pltpu.SemaphoreType.DMA

    send, slots = pl.pallas_call(
        functools.partial(
            pack_kernel,
            rows_dev=rows_dev,
            devices=devices,
            entries=entries,
            block_total=rows_dev * devices,
        ),
        out_shape=(
            jax.ShapeDtypeStruct((capacity, edge, samples_dev), samples.dtype),
            jax.ShapeDtypeStruct((entries,), jnp.int32),
        ),
        in_specs=[smem, smem, hbm],
        out_specs=(hbm, smem),
        scratch_shapes=[pltpu.SMEM((devices,), jnp.int32), dma((entries + 1,))],
        compiler_params=alone,
        name="pack",
    )(pattern, block_count, x)

    arrived = lax.all_to_all(
        send.reshape(devices, SLOTS, edge, samples_dev),
        "rows",
        split_axis=0,
        concat_axis=0,
        tiled=True,
    ).reshape(capacity, edge, samples_dev)

    own, logs, wide = pl.pallas_call(
        functools.partial(own_kernel, **sizes),
        out_shape=(
            pltpu.HBM((rows_dev, edge, samples_dev), f32),
            jax.ShapeDtypeStruct((8, edge), f32),
            pltpu.HBM((entries, edge, 2 * edge), jnp.bfloat16),
        ),
        in_specs=[smem, vmem, vmem, vmem],
        out_specs=(vmem, vmem, vmem),
        compiler_params=params,
        cost_estimate=pl.CostEstimate(
            flops=4 * rows_dev * edge * edge * samples_dev, transcendentals=0, bytes_accessed=1 << 23
        ),
        name="own",
    )(block_count, x, omega_diag, omega_off)

    payload, projected = pl.pallas_call(
        functools.partial(main_kernel, **every),
        out_shape=(
            pltpu.HBM((devices, SLOTS * edge + STAT_ROWS, edge), jnp.int16),
            pltpu.HBM((rows_dev, edge, samples_dev), f32),
        ),
        in_specs=[smem, smem, smem, vmem, vmem, hbm, hbm],
        out_specs=(hbm, hbm),
        scratch_shapes=[
            pltpu.VMEM((entries, edge, 2 * edge), jnp.bfloat16),
            pltpu.VMEM((rows_dev, edge, samples_dev), f32),
            pltpu.VMEM((rows_dev, edge, samples_dev), f32),
            pltpu.VMEM((rows_dev, 2 * edge, samples_dev), jnp.bfloat16),
            pltpu.VMEM((entries, edge, edge), jnp.int16),
            pltpu.VMEM((devices, STAT_ROWS, edge), f32),
            pltpu.VMEM((devices, STAT_ROWS, edge), jnp.int16),
            dma((2,)),
            dma((1,)),
            dma((1,)),
            dma((entries + 1,)),
        ],
        compiler_params=params,
        name="main",
    )(pattern, block_count, slots, logs, held(arrived), kept(own), kept(wide))

    returned = lax.all_to_all(kept(payload), "rows", split_axis=0, concat_axis=0, tiled=True)

    diag_next, moved = pl.pallas_call(
        functools.partial(side_kernel, samples_dev=samples_dev, **sizes),
        out_shape=(
            jax.ShapeDtypeStruct((rows_dev, edge, edge), f32),
            pltpu.HBM((entries, edge, edge), f32),
        ),
        in_specs=[smem] * 3 + [vmem] * 6,
        out_specs=(vmem, vmem),
        scratch_shapes=[pltpu.VMEM((rows_dev, 2 * edge, samples_dev), jnp.bfloat16)],
        compiler_params=params,
        cost_estimate=pl.CostEstimate(
            flops=4 * rows_dev * edge * edge * samples_dev, transcendentals=0, bytes_accessed=1 << 23
        ),
        name="side",
    )(pattern, block_count, slots, x, omega_diag, term, projected, omega_off, arrived)

    off_next, objective = pl.pallas_call(
        functools.partial(last_kernel, **every),
        out_shape=(
            jax.ShapeDtypeStruct((entries, edge, edge), f32),
            jax.ShapeDtypeStruct((1,), f32),
        ),
        in_specs=[smem, smem, hbm, vmem],
        out_specs=(hbm, smem),
        scratch_shapes=[
            pltpu.VMEM((entries, edge, edge), f32),
            pltpu.VMEM((entries, edge, edge), f32),
            dma((entries,)),
            dma((entries,)),
        ],
        compiler_params=params,
        name="last",
    )(block_count, slots, kept(moved), held(returned))
    return diag_next, off_next, objective


def solution(mesh):
    return jax.shard_map(
        shards,
        mesh=mesh,
        in_specs=(
            P(("groups", "rows"), None),
            P(("groups", "rows"), None, None),
            P(("groups", "rows"), None, None),
            P(("groups", "rows"), None),
            P(("groups", "rows")),
            P(("groups", "rows")),
        ),
        out_specs=(
            P(("groups", "rows"), None, None),
            P(("groups", "rows"), None, None),
            P("groups"),
        ),
        check_vma=False,
    )
```

time: 114 us -> 161 us (1.41)
  Pallas kernels: 29.3 us -> 78.2 us
  waiting for transfers between devices: 68.1 us -> 58 us
  starting transfers between devices: 10.7 us -> 18.9 us
    pallas_call x1, Pallas kernels: 3.78 us -> 56.2 us  [shards(): pl.pallas_call(functools.partial(pack_kernel, rows_dev=rows_dev, devices=...]
    all_to_all x1, starting transfers between devices: 6.08 us -> 14.3 us  [shards(): lax.all_to_all(send.reshape(devices, SLOTS, edge, samples_dev), 'rows', s...]
    all_to_all x1, waiting for transfers between devices: 23 us -> 14.9 us  [shards(): lax.all_to_all(kept(payload), 'rows', split_axis=0, concat_axis=0, tiled=...]
    pallas_call x4, Pallas kernels: 25.6 us -> 22 us  [the longest x1 8.24 us: shards(): pl.pallas_call(functools.partial(side_kernel, samples_dev=samples_dev, **...]
    all_to_all x1, waiting for transfers between devices: 45.1 us -> 43.1 us  [shards(): lax.all_to_all(send.reshape(devices, SLOTS, edge, samples_dev), 'rows', s...]
    unnamed x5 -> x18, local copies, waits for them, and re-layouts: 3.69 us -> 4.34 us
  transfers between devices with their start and end apart: 2 -> 2, of which waited for: 2 -> 2; matrix products, arithmetic and copies ran while one was open for 0% -> 0% of each run, Pallas kernels for 5% -> 7%
where the time goes in v2:
time: 161 us; the launch traced here: 160 us
  Pallas kernels  78.2 us (49%)
  waiting for transfers between devices  58 us (36%)
  starting transfers between devices  18.9 us (12%)
  local copies, waits for them, and re-layouts  4.34 us (3%)
    pallas_call x1, Pallas kernels, shards(): pl.pallas_call(functools.partial(pack_kernel, rows_dev=rows_dev, devices=...  56.2 us
    all_to_all x1, waiting for transfers between devices, shards(): lax.all_to_all(send.reshape(devices, SLOTS, edge, samples_dev), 'rows', s...  43.1 us
    all_to_all x1, waiting for transfers between devices, shards(): lax.all_to_all(kept(payload), 'rows', split_axis=0, concat_axis=0, tiled=...  14.9 us
    all_to_all x1, starting transfers between devices, shards(): lax.all_to_all(send.reshape(devices, SLOTS, edge, samples_dev), 'rows', s...  14.3 us
    pallas_call x1, Pallas kernels, shards(): pl.pallas_call(functools.partial(side_kernel, samples_dev=samples_dev, **...  8.24 us
    pallas_call x1, Pallas kernels, shards(): pl.pallas_call(functools.partial(main_kernel, **every), out_shape=(pltpu....  6.04 us
    pallas_call x1, Pallas kernels, shards(): pl.pallas_call(functools.partial(last_kernel, **every), out_shape=(jax.Sh...  4.82 us
    all_to_all x1, starting transfers between devices, shards(): lax.all_to_all(kept(payload), 'rows', split_axis=0, concat_axis=0, tiled=...  4.62 us
  transfers between devices with their start and end apart: 2, of which 2 were waited for; matrix products, arithmetic and copies ran while one was open for 0% of the time, Pallas kernels for 7%

profile of v2, /device:TPU:16, one launch (start us, length us, event | category | flops | bytes accessed | tf_op | source)
XLA Modules:
  0.0 160.2 jit_solution(10999250279973824578)
XLA Ops:
  0.6 56.2 %pack.1 = (bf16[32,128,256]{2,1,0:T(8,128)(2,1)}, s32[30]{0:T(128)}) custom-call(s32[2,30]{1,0:T(2,128)} %bitcast.10, s32[8]{0:T(128)} %count.9, bf16[8,128,256]{2,1,0:T(8,128)(2,1)} %bitcast.7), custom_call_target="tpu_custom_call" | custom-call | tf_op jit(solution)/shard_map/pack/pallas_call | solution.py:371
  56.8 0.0 copy-start.2
  56.8 0.0 copy-start.3
  56.9 0.0 copy-start.5
  56.9 14.3 %all-to-all-start = ((bf16[16,2,128,256]{3,2,1,0:T(8,128)(2,1)}), bf16[16,2,128,256]{3,2,1,0:T(8,128)(2,1)S(1)}, u32[]{:S(2)}, u32[]{:S(2)}) async-start(bf16[16,2,128,256]{3,2,1,0:T(8,128)(2,1)} %bitcast.14), calls=%async_computation | async-start | bytes 4194304 | tf_op jit(solution)/shard_map/all_to_all | solution.py:390
  71.1 0.0 copy-done.2
  71.1 0.0 copy-done.3
  71.2 0.0 copy-done.5
  71.2 0.0 copy-start
  71.2 1.5 copy-done
  72.7 0.0 copy-start.6
  72.7 0.0 copy-start.7
  72.7 2.9 %own.1 = (f32[8,128,256]{2,1,0:T(8,128)}, f32[8,128]{1,0:T(8,128)S(1)}, bf16[30,128,256]{2,1,0:T(8,128)(2,1)}) custom-call(s32[8]{0:T(128)S(1)} %copy-done.5, bf16[8,128,256]{2,1,0:T(8,128)(2,1)S(1)} %bitcast.8, f32[8,128,128]{2,1,0:T(8,128)S(1)} %copy-done.3, f32[30,128,128]{2,1,0:T(8,128)S(1)} %copy-done), custom_call_target="tpu_custom_call" | custom-call | flops 134217728 | bytes 8388608 | tf_op jit(solution)/shard_map/own/pallas_call | solution.py:398
  75.6 43.1 %all-to-all-done = bf16[16,2,128,256]{3,2,1,0:T(8,128)(2,1)S(1)} async-done(((bf16[16,2,128,256]{3,2,1,0:T(8,128)(2,1)}), bf16[16,2,128,256]{3,2,1,0:T(8,128)(2,1)S(1)}, u32[]{:S(2)}, u32[]{:S(2)}) %all-to-all-start) | async-done | bytes 2097184 | tf_op jit(solution)/shard_map/all_to_all | solution.py:390
  118.8 0.0 copy-done.6
  118.8 0.0 copy-done.7
  118.8 6.0 %main.1 = (s16[16,264,128]{2,1,0:T(8,128)(2,1)}, f32[8,128,256]{2,1,0:T(8,128)}) custom-call(s32[2,30]{1,0:T(2,128)S(1)} %bitcast.11, s32[8]{0:T(128)S(1)} %copy-done.5, s32[30]{0:T(128)S(1)} %copy-done.7, f32[8,128]{1,0:T(8,128)S(1)} %get-tuple-element.15.logs, bf16[32,128,256]{2,1,0:T(8,128)(2,1)S(1)} %bitcast.5, f32[8,128,256]{2,1,0:T(8,128)} %get-tuple-element.17.own, ...), custom_call_target="tpu_custom_call" | custom-call | tf_op jit(solution)/shard_map/main/pallas_call | solution.py:414
  124.8 0.0 copy-start.8
  124.8 4.6 %all-to-all-start.1 = ((s16[16,264,128]{2,1,0:T(8,128)(2,1)}), s16[16,264,128]{2,1,0:T(8,128)(2,1)}, u32[]{:S(2)}, u32[]{:S(2)}) async-start(s16[16,264,128]{2,1,0:T(8,128)(2,1)} %get-tuple-element.22), calls=%async_computation.1 | async-start | bytes 2162688 | tf_op jit(solution)/shard_map/all_to_all | solution.py:439
  129.4 0.0 copy-done.8
  129.4 0.0 copy-start.1
  129.5 1.5 copy-done.1
  131.0 0.0 copy-start.4
  131.0 1.2 copy-done.4
  132.2 8.2 %side.1 = (f32[8,128,128]{2,1,0:T(8,128)}, f32[30,128,128]{2,1,0:T(8,128)}) custom-call(s32[2,30]{1,0:T(2,128)S(1)} %bitcast.12, s32[8]{0:T(128)S(1)} %copy-done.5, s32[30]{0:T(128)S(1)} %copy-done.7, bf16[8,128,256]{2,1,0:T(8,128)(2,1)S(1)} %bitcast.9, f32[8,128,128]{2,1,0:T(8,128)S(1)} %copy-done.3, f32[8,128]{1,0:T(8,128)S(1)} %bitcast.13, ...), custom_call_target="tpu_custom_call" | custom-call | flops 134217728 | bytes 8388608 | tf_op jit(solution)/shard_map/side/pallas_call | solution.py:441
  140.5 14.9 %all-to-all-done.1.returned = s16[16,264,128]{2,1,0:T(8,128)(2,1)} async-done(((s16[16,264,128]{2,1,0:T(8,128)(2,1)}), s16[16,264,128]{2,1,0:T(8,128)(2,1)}, u32[]{:S(2)}, u32[]{:S(2)}) %all-to-all-start.1) | async-done | bytes 1081376 | tf_op jit(solution)/shard_map/all_to_all | solution.py:439
  155.4 4.8 %last.1 = (f32[30,128,128]{2,1,0:T(8,128)}, f32[1]{0:T(128)}) custom-call(s32[8]{0:T(128)S(1)} %copy-done.5, s32[30]{0:T(128)S(1)} %copy-done.7, f32[30,128,128]{2,1,0:T(8,128)} %get-tuple-element.21.moved, s16[16,264,128]{2,1,0:T(8,128)(2,1)} %all-to-all-done.1.returned), custom_call_target="tpu_custom_call" | custom-call | tf_op jit(solution)/shard_map/last/pallas_call | solution.py:457
Async XLA Ops:
  56.8 14.3 %copy-start.2 = (bf16[1024,256]{1,0:T(8,128)(2,1)S(1)}, bf16[1024,256]{1,0:T(8,128)(2,1)}, u32[]{:S(2)}) copy-start(bf16[1024,256]{1,0:T(8,128)(2,1)} %param.6) | copy-start | bytes 1572868
  56.8 14.3 %copy-start.3 = (f32[8,128,128]{2,1,0:T(8,128)S(1)}, f32[8,128,128]{2,1,0:T(8,128)}, u32[]{:S(2)}) copy-start(f32[8,128,128]{2,1,0:T(8,128)} %omega.3) | copy-start | bytes 1572868
  56.9 14.3 %copy-start.5 = (s32[8]{0:T(128)S(1)}, s32[8]{0:T(128)}, u32[]{:S(2)}) copy-start(s32[8]{0:T(128)} %count.9) | copy-start | bytes 100
  56.9 61.9 %all-to-all-start = ((bf16[16,2,128,256]{3,2,1,0:T(8,128)(2,1)}), bf16[16,2,128,256]{3,2,1,0:T(8,128)(2,1)S(1)}, u32[]{:S(2)}, u32[]{:S(2)}) async-start(bf16[16,2,128,256]{3,2,1,0:T(8,128)(2,1)} %bitcast.14), calls=%async_computation | async-start | bytes 4194304 | tf_op jit(solution)/shard_map/all_to_all | solution.py:390
  71.2 1.5 copy-start
  72.7 46.0 %copy-start.6 = (s32[30,2]{0,1:T(2,128)S(1)}, s32[30,2]{0,1:T(2,128)}, u32[]{:S(2)}) copy-start(s32[30,2]{0,1:T(2,128)} %param.9) | copy-start | bytes 724
  72.7 46.0 %copy-start.7 = (s32[30]{0:T(128)S(1)}, s32[30]{0:T(128)}, u32[]{:S(2)}) copy-start(s32[30]{0:T(128)} %get-tuple-element.14.slots) | copy-start | bytes 364
  124.8 4.6 %copy-start.8 = (f32[1024]{0:T(1024)S(1)}, f32[1024]{0:T(1024)}, u32[]{:S(2)}) copy-start(f32[1024]{0:T(1024)} %param.11) | copy-start | bytes 12292
  124.8 30.6 %all-to-all-start.1 = ((s16[16,264,128]{2,1,0:T(8,128)(2,1)}), s16[16,264,128]{2,1,0:T(8,128)(2,1)}, u32[]{:S(2)}, u32[]{:S(2)}) async-start(s16[16,264,128]{2,1,0:T(8,128)(2,1)} %get-tuple-element.22), calls=%async_computation.1 | async-start | bytes 2162688 | tf_op jit(solution)/shard_map/all_to_all | solution.py:439
  129.4 1.5 copy-start.1
  131.0 1.2 copy-start.4

commit v3 on v2

--- a/solution.py
+++ b/solution.py
@@ -47,7 +47,9 @@
     return total
 
 
-def pack_kernel(pattern, count, x, send, slots, sums, sems, *, rows_dev, devices, entries, block_total):
+def pack_kernel(
+    pattern, count, x, send, slots, sums, held, sem_x, sems, *, rows_dev, devices, entries, block_total
+):
     live = live_count(count, rows_dev)
     position = divide(pattern[0, 0], rows_dev)
     base = position * rows_dev
@@ -58,10 +60,11 @@
         return jnp.minimum(i, j) * block_total + jnp.maximum(i, j)
 
     def copy(e):
-        return pltpu.make_async_copy(x.at[pattern[0, e] - base], send.at[slots[e]], sems.at[e])
-
-    spare = pltpu.make_async_copy(x.at[0], send.at[position * SLOTS], sems.at[entries])
-    spare.start()
+        return pltpu.make_async_copy(held.at[pattern[0, e] - base], send.at[slots[e]], sems.at[e])
+
+    fetch = pltpu.make_async_copy(x, held, sem_x.at[0])
+    fetch.start()
+    spare = pltpu.make_async_copy(held.at[0], send.at[position * SLOTS], sems.at[entries])
     for o in range(devices):
         sums[o] = 0
     for e in range(entries):
@@ -80,6 +83,8 @@
         copy(e).wait()
         return carry
 
+    fetch.wait()
+    spare.start()
     lax.fori_loop(0, live, begin, 0)
     spare.wait()
     lax.fori_loop(0, live, finish, 0)
@@ -299,8 +304,10 @@
     result,
     objective,
     held,
+    rt,
     rs,
     sem_in,
+    sem_rt,
     sem_out,
     *,
     rows_dev,
@@ -319,9 +326,12 @@
 
     width = max(k for k in range(1, 11) if entries % k == 0)
     parts = [(at, pl.ds(at * width, width)) for at in range(entries // width)]
+    whole = pltpu.make_async_copy(returned, rt, sem_rt.at[0])
+    whole.start()
     for at, part in parts:
         fetch(at, part).start()
-    codes = returned[:, SLOTS * edge :, :].astype(jnp.int32).astype(jnp.float32)
+    whole.wait()
+    codes = rt[:, SLOTS * edge :, :].astype(jnp.int32).astype(jnp.float32)
     power = codes[:, SLOTS : SLOTS + 1]
     digits = codes[:, SLOTS + 1 : SLOTS + 2] + codes[:, SLOTS + 2 : SLOTS + 3] * (1.0 / FRACTION)
     total = jnp.sum(digits * jnp.exp2(power - 14.0), axis=0)
@@ -332,13 +342,13 @@
             slot = slots[e]
             owner = divide(slot, SLOTS)
             rank = slot - owner * SLOTS
-            codes = returned[owner, SLOTS * edge :, :].astype(jnp.int32).astype(jnp.float32)
+            codes = rt[owner, SLOTS * edge :, :].astype(jnp.int32).astype(jnp.float32)
             code = jnp.where(rank == 0, codes[0:1], codes[1:2])
             weight = jnp.exp2(code * (1.0 / LOG_STEPS) - (15.0 - HEADROOM)) * (
                 STEP_SIZE / (2.0 * samples_dev)
             )
             weight = jnp.where(e < live, weight, 0.0)
-            digits = returned[owner, pl.ds(pl.multiple_of(rank * edge, edge), edge), :]
+            digits = rt[owner, pl.ds(pl.multiple_of(rank * edge, edge), edge), :]
             value = held[e] - digits.astype(jnp.int32).astype(jnp.float32) * weight
             rs[e] = soften(value, STEP_SIZE * PENALTY)
         store(at, part).start()
@@ -382,7 +392,12 @@
         ),
         in_specs=[smem, smem, hbm],
         out_specs=(hbm, smem),
-        scratch_shapes=[pltpu.SMEM((devices,), jnp.int32), dma((entries + 1,))],
+        scratch_shapes=[
+            pltpu.SMEM((devices,), jnp.int32),
+            pltpu.VMEM((rows_dev, edge, samples_dev), samples.dtype),
+            dma((1,)),
+            dma((entries + 1,)),
+        ],
         compiler_params=alone,
         name="pack",
     )(pattern, block_count, x)
@@ -460,17 +475,19 @@
             jax.ShapeDtypeStruct((entries, edge, edge), f32),
             jax.ShapeDtypeStruct((1,), f32),
         ),
-        in_specs=[smem, smem, hbm, vmem],
+        in_specs=[smem, smem, hbm, hbm],
         out_specs=(hbm, smem),
         scratch_shapes=[
             pltpu.VMEM((entries, edge, edge), f32),
+            pltpu.VMEM((devices, SLOTS * edge + STAT_ROWS, edge), jnp.int16),
             pltpu.VMEM((entries, edge, edge), f32),
             dma((entries,)),
+            dma((1,)),
             dma((entries,)),
         ],
-        compiler_params=params,
+        compiler_params=alone,
         name="last",
-    )(block_count, slots, kept(moved), held(returned))
+    )(block_count, slots, kept(moved), kept(returned))
     return diag_next, off_next, objective
 
 

time: 161 us -> 101 us (0.63)
  Pallas kernels: 78.2 us -> 26 us
  starting transfers between devices: 18.9 us -> 10.9 us
    pallas_call x1, Pallas kernels: 56.2 us -> 3.86 us  [shards(): pl.pallas_call(functools.partial(pack_kernel, rows_dev=rows_dev, devices=...]
    all_to_all x1, starting transfers between devices: 14.3 us -> 6.27 us  [shards(): lax.all_to_all(send.reshape(devices, SLOTS, edge, samples_dev), 'rows', s...]
  transfers between devices with their start and end apart: 2 -> 2, of which waited for: 2 -> 2; matrix products, arithmetic and copies ran while one was open for 0% -> 0% of each run, Pallas kernels for 7% -> 11%
where the time goes in v3:
time: 101 us; the launch traced here: 100 us
  waiting for transfers between devices  58 us (57%)
  Pallas kernels  26 us (26%)
  starting transfers between devices  10.9 us (11%)
  local copies, waits for them, and re-layouts  4.34 us (4%)
    all_to_all x1, waiting for transfers between devices, shards(): lax.all_to_all(send.reshape(devices, SLOTS, edge, samples_dev), 'rows', s...  43.1 us
    all_to_all x1, waiting for transfers between devices, shards(): lax.all_to_all(kept(payload), 'rows', split_axis=0, concat_axis=0, tiled=...  14.9 us
    pallas_call x1, Pallas kernels, shards(): pl.pallas_call(functools.partial(side_kernel, samples_dev=samples_dev, **...  8.23 us
    all_to_all x1, starting transfers between devices, shards(): lax.all_to_all(send.reshape(devices, SLOTS, edge, samples_dev), 'rows', s...  6.27 us
    pallas_call x1, Pallas kernels, shards(): pl.pallas_call(functools.partial(main_kernel, **every), out_shape=(pltpu....  6.03 us
    pallas_call x1, Pallas kernels, shards(): pl.pallas_call(functools.partial(last_kernel, **every), out_shape=(jax.Sh...  4.95 us
    all_to_all x1, starting transfers between devices, shards(): lax.all_to_all(kept(payload), 'rows', split_axis=0, concat_axis=0, tiled=...  4.61 us
    unnamed x18, local copies, waits for them, and re-layouts  4.34 us
  transfers between devices with their start and end apart: 2, of which 2 were waited for; matrix products, arithmetic and copies ran while one was open for 0% of the time, Pallas kernels for 11%

profile of v3, /device:TPU:16, one launch (start us, length us, event | category | flops | bytes accessed | tf_op | source)
XLA Modules:
  0.0 100.0 jit_solution(9209342958855699725)
XLA Ops:
  0.6 3.9 %pack.1 = (bf16[32,128,256]{2,1,0:T(8,128)(2,1)}, s32[30]{0:T(128)}) custom-call(s32[2,30]{1,0:T(2,128)} %bitcast.10, s32[8]{0:T(128)} %count.9, bf16[8,128,256]{2,1,0:T(8,128)(2,1)} %bitcast.7), custom_call_target="tpu_custom_call" | custom-call | tf_op jit(solution)/shard_map/pack/pallas_call | solution.py:381
  4.5 0.0 copy-start.2
  4.5 0.0 copy-start.3
  4.5 0.0 copy-start.5
  4.5 6.3 %all-to-all-start = ((bf16[16,2,128,256]{3,2,1,0:T(8,128)(2,1)}), bf16[16,2,128,256]{3,2,1,0:T(8,128)(2,1)S(1)}, u32[]{:S(2)}, u32[]{:S(2)}) async-start(bf16[16,2,128,256]{3,2,1,0:T(8,128)(2,1)} %bitcast.14), calls=%async_computation | async-start | bytes 4194304 | tf_op jit(solution)/shard_map/all_to_all | solution.py:405
  10.8 0.0 copy-done.2
  10.8 0.0 copy-done.3
  10.8 0.0 copy-done.5
  10.8 0.0 copy-start
  10.8 1.5 %copy-done = f32[30,128,128]{2,1,0:T(8,128)S(1)} copy-done((f32[30,128,128]{2,1,0:T(8,128)S(1)}, f32[30,128,128]{2,1,0:T(8,128)}, u32[]{:S(2)}) %copy-start) | copy-done | bytes 1966104
  12.4 0.0 copy-start.6
  12.4 0.0 copy-start.7
  12.4 2.9 %own.1 = (f32[8,128,256]{2,1,0:T(8,128)}, f32[8,128]{1,0:T(8,128)S(1)}, bf16[30,128,256]{2,1,0:T(8,128)(2,1)}) custom-call(s32[8]{0:T(128)S(1)} %copy-done.5, bf16[8,128,256]{2,1,0:T(8,128)(2,1)S(1)} %bitcast.8, f32[8,128,128]{2,1,0:T(8,128)S(1)} %copy-done.3, f32[30,128,128]{2,1,0:T(8,128)S(1)} %copy-done), custom_call_target="tpu_custom_call" | custom-call | flops 134217728 | bytes 8388608 | tf_op jit(solution)/shard_map/own/pallas_call | solution.py:413
  15.3 43.1 %all-to-all-done = bf16[16,2,128,256]{3,2,1,0:T(8,128)(2,1)S(1)} async-done(((bf16[16,2,128,256]{3,2,1,0:T(8,128)(2,1)}), bf16[16,2,128,256]{3,2,1,0:T(8,128)(2,1)S(1)}, u32[]{:S(2)}, u32[]{:S(2)}) %all-to-all-start) | async-done | bytes 2097184 | tf_op jit(solution)/shard_map/all_to_all | solution.py:405
  58.4 0.0 copy-done.6
  58.4 0.0 copy-done.7
  58.4 6.0 %main.1 = (s16[16,264,128]{2,1,0:T(8,128)(2,1)}, f32[8,128,256]{2,1,0:T(8,128)}) custom-call(s32[2,30]{1,0:T(2,128)S(1)} %bitcast.11, s32[8]{0:T(128)S(1)} %copy-done.5, s32[30]{0:T(128)S(1)} %copy-done.7, f32[8,128]{1,0:T(8,128)S(1)} %get-tuple-element.15.logs, bf16[32,128,256]{2,1,0:T(8,128)(2,1)S(1)} %bitcast.5, f32[8,128,256]{2,1,0:T(8,128)} %get-tuple-element.17.own, ...), custom_call_target="tpu_custom_call" | custom-call | tf_op jit(solution)/shard_map/main/pallas_call | solution.py:429
  64.5 0.0 copy-start.8
  64.5 4.6 %all-to-all-start.1 = ((s16[16,264,128]{2,1,0:T(8,128)(2,1)}), s16[16,264,128]{2,1,0:T(8,128)(2,1)}, u32[]{:S(2)}, u32[]{:S(2)}) async-start(s16[16,264,128]{2,1,0:T(8,128)(2,1)} %get-tuple-element.22), calls=%async_computation.1 | async-start | bytes 2162688 | tf_op jit(solution)/shard_map/all_to_all | solution.py:454
  69.1 0.0 copy-done.8
  69.1 0.0 copy-start.1
  69.1 1.5 %copy-done.1 = f32[30,128,128]{2,1,0:T(8,128)S(1)} copy-done((f32[30,128,128]{2,1,0:T(8,128)S(1)}, f32[30,128,128]{2,1,0:T(8,128)}, u32[]{:S(2)}) %copy-start.1) | copy-done | bytes 1966104
  70.6 0.0 copy-start.4
  70.6 1.2 %copy-done.4 = f32[8,128,256]{2,1,0:T(8,128)S(1)} copy-done((f32[8,128,256]{2,1,0:T(8,128)S(1)}, f32[8,128,256]{2,1,0:T(8,128)}, u32[]{:S(2)}) %copy-start.4) | copy-done | bytes 1048600
  71.9 8.2 %side.1 = (f32[8,128,128]{2,1,0:T(8,128)}, f32[30,128,128]{2,1,0:T(8,128)}) custom-call(s32[2,30]{1,0:T(2,128)S(1)} %bitcast.12, s32[8]{0:T(128)S(1)} %copy-done.5, s32[30]{0:T(128)S(1)} %copy-done.7, bf16[8,128,256]{2,1,0:T(8,128)(2,1)S(1)} %bitcast.9, f32[8,128,128]{2,1,0:T(8,128)S(1)} %copy-done.3, f32[8,128]{1,0:T(8,128)S(1)} %bitcast.13, ...), custom_call_target="tpu_custom_call" | custom-call | flops 134217728 | bytes 8388608 | tf_op jit(solution)/shard_map/side/pallas_call | solution.py:456
  80.1 14.9 %all-to-all-done.1.returned = s16[16,264,128]{2,1,0:T(8,128)(2,1)} async-done(((s16[16,264,128]{2,1,0:T(8,128)(2,1)}), s16[16,264,128]{2,1,0:T(8,128)(2,1)}, u32[]{:S(2)}, u32[]{:S(2)}) %all-to-all-start.1) | async-done | bytes 1081376 | tf_op jit(solution)/shard_map/all_to_all | solution.py:454
  95.0 5.0 %last.1 = (f32[30,128,128]{2,1,0:T(8,128)}, f32[1]{0:T(128)}) custom-call(s32[8]{0:T(128)} %count.9, s32[30]{0:T(128)} %get-tuple-element.14.slots, f32[30,128,128]{2,1,0:T(8,128)} %get-tuple-element.21.moved, s16[16,264,128]{2,1,0:T(8,128)(2,1)} %all-to-all-done.1.returned), custom_call_target="tpu_custom_call" | custom-call | tf_op jit(solution)/shard_map/last/pallas_call | solution.py:472
Async XLA Ops:
  4.5 6.3 %copy-start.2 = (bf16[1024,256]{1,0:T(8,128)(2,1)S(1)}, bf16[1024,256]{1,0:T(8,128)(2,1)}, u32[]{:S(2)}) copy-start(bf16[1024,256]{1,0:T(8,128)(2,1)} %param.6) | copy-start | bytes 1572868
  4.5 6.3 %copy-start.3 = (f32[8,128,128]{2,1,0:T(8,128)S(1)}, f32[8,128,128]{2,1,0:T(8,128)}, u32[]{:S(2)}) copy-start(f32[8,128,128]{2,1,0:T(8,128)} %omega.3) | copy-start | bytes 1572868
  4.5 6.3 %copy-start.5 = (s32[8]{0:T(128)S(1)}, s32[8]{0:T(128)}, u32[]{:S(2)}) copy-start(s32[8]{0:T(128)} %count.9) | copy-start | bytes 100
  4.5 53.9 %all-to-all-start = ((bf16[16,2,128,256]{3,2,1,0:T(8,128)(2,1)}), bf16[16,2,128,256]{3,2,1,0:T(8,128)(2,1)S(1)}, u32[]{:S(2)}, u32[]{:S(2)}) async-start(bf16[16,2,128,256]{3,2,1,0:T(8,128)(2,1)} %bitcast.14), calls=%async_computation | async-start | bytes 4194304 | tf_op jit(solution)/shard_map/all_to_all | solution.py:405
  10.8 1.5 %copy-start = (f32[30,128,128]{2,1,0:T(8,128)S(1)}, f32[30,128,128]{2,1,0:T(8,128)}, u32[]{:S(2)}) copy-start(f32[30,128,128]{2,1,0:T(8,128)} %off.3) | copy-start | bytes 5898244
  12.4 46.0 %copy-start.6 = (s32[30,2]{0,1:T(2,128)S(1)}, s32[30,2]{0,1:T(2,128)}, u32[]{:S(2)}) copy-start(s32[30,2]{0,1:T(2,128)} %param.9) | copy-start | bytes 724
  12.4 46.0 %copy-start.7 = (s32[30]{0:T(128)S(1)}, s32[30]{0:T(128)}, u32[]{:S(2)}) copy-start(s32[30]{0:T(128)} %get-tuple-element.14.slots) | copy-start | bytes 364
  64.5 4.6 %copy-start.8 = (f32[1024]{0:T(1024)S(1)}, f32[1024]{0:T(1024)}, u32[]{:S(2)}) copy-start(f32[1024]{0:T(1024)} %param.11) | copy-start | bytes 12292
  64.5 30.6 %all-to-all-start.1 = ((s16[16,264,128]{2,1,0:T(8,128)(2,1)}), s16[16,264,128]{2,1,0:T(8,128)(2,1)}, u32[]{:S(2)}, u32[]{:S(2)}) async-start(s16[16,264,128]{2,1,0:T(8,128)(2,1)} %get-tuple-element.22), calls=%async_computation.1 | async-start | bytes 2162688 | tf_op jit(solution)/shard_map/all_to_all | solution.py:454
  69.1 1.5 %copy-start.1 = (f32[30,128,128]{2,1,0:T(8,128)S(1)}, f32[30,128,128]{2,1,0:T(8,128)}, u32[]{:S(2)}) copy-start(f32[30,128,128]{2,1,0:T(8,128)} %off.3) | copy-start | bytes 5898244
  70.6 1.2 %copy-start.4 = (f32[8,128,256]{2,1,0:T(8,128)S(1)}, f32[8,128,256]{2,1,0:T(8,128)}, u32[]{:S(2)}) copy-start(f32[8,128,256]{2,1,0:T(8,128)} %get-tuple-element.19.projected) | copy-start | bytes 3145732

commit v4 on v3

v4 whole, which is shorter than its diff:
```python
import functools

import jax
import jax.numpy as jnp
from jax import lax
from jax.experimental import pallas as pl
from jax.experimental.pallas import tpu as pltpu
from jax.sharding import PartitionSpec as P


SLOTS = 2
STAT_ROWS = 8
STEP_SIZE = 0.5
PENALTY = 0.01
LOG_STEPS = 128.0
HEADROOM = 1e-4
FRACTION = 32000.0
VMEM_LIMIT = 40 * 1024 * 1024
VMEM_ALONE = 60 * 1024 * 1024


def soften(values, level):
    return values - jnp.clip(values, -level, level)


def split_halves(values):
    high = values.astype(jnp.bfloat16)
    low = (values - high.astype(jnp.float32)).astype(jnp.bfloat16)
    return high, low


def divide(value, by):
    if by & (by - 1):
        return value // by
    return lax.shift_right_logical(value, by.bit_length() - 1)


def limits(entries, devices):
    half = devices // 2
    return min(entries, SLOTS * half), min(entries, SLOTS * (half - 1))


def live_count(count, rows_dev):
    total = count[0]
    for k in range(1, rows_dev):
        total = total + count[k]
    return total


def pack_kernel(
    pattern,
    count,
    x,
    send,
    slots,
    lists,
    wanted,
    sums,
    keys,
    held,
    sem_x,
    sems,
    *,
    rows_dev,
    devices,
    entries,
    block_total,
):
    live = live_count(count, rows_dev)
    half = devices // 2
    far_limit, near_limit = limits(entries, devices)
    position = divide(pattern[0, 0], rows_dev)
    base = position * rows_dev
    side = divide(position, half)
    spot = (position - side * half) * SLOTS

    fetch = pltpu.make_async_copy(x, held, sem_x.at[0])
    fetch.start()
    spare = pltpu.make_async_copy(held.at[0], send.at[spot], sems.at[near_limit])
    for o in range(devices):
        sums[o] = 0
    for q in range(SLOTS * half):
        wanted[q] = 0
    for k in range(far_limit + near_limit):
        lists[0, k] = entries
        lists[1, k] = rows_dev
        lists[2, k] = spot if k >= far_limit else 0
        lists[3, k] = position * SLOTS
    for e in range(entries):
        i = pattern[0, e]
        j = pattern[1, e]
        owner = divide(j, rows_dev)
        key = jnp.minimum(i * block_total + j, j * block_total + i)
        keys[e] = key
        sums[owner] = sums[owner] + key
    fars = jnp.int32(0)
    nears = jnp.int32(far_limit)
    for e in range(entries):
        row = pattern[0, e] - base
        owner = divide(pattern[1, e], rows_dev)
        alive = e < live
        later = jnp.where((2 * keys[e] > sums[owner]) & alive, 1, 0)
        slot = owner * SLOTS + later
        slots[e] = slot
        away = divide(owner, half)
        place = slot - away * (SLOTS * half)
        near = away == side
        wanted[jnp.where(alive & ~near, place, SLOTS * half)] = row
        at = jnp.where(alive, jnp.where(near, nears, fars), far_limit + near_limit)
        lists[0, at] = e
        lists[1, at] = row
        lists[2, at] = place
        lists[3, at] = slot
        fars = fars + jnp.where(alive & ~near, 1, 0)
        nears = nears + jnp.where(alive & near, 1, 0)

    def copy(k):
        return pltpu.make_async_copy(
            held.at[lists[1, k]], send.at[lists[2, k]], sems.at[k - far_limit]
        )

    def begin(k, carry):
        copy(k).start()
        return carry

    def finish(k, carry):
        copy(k).wait()
        return carry

    fetch.wait()
    spare.start()
    lax.fori_loop(far_limit, nears, begin, 0)
    lists[0, far_limit + near_limit + 1] = fars
    lists[0, far_limit + near_limit + 2] = nears
    spare.wait()
    lax.fori_loop(far_limit, nears, finish, 0)


def relay_kernel(wanted, x, send, sems, *, devices):
    copies = [
        pltpu.make_async_copy(x.at[wanted[q]], send.at[q], sems.at[q])
        for q in range(SLOTS * (devices // 2))
    ]
    for copy in copies:
        copy.start()
    for copy in copies:
        copy.wait()


def own_kernel(lists, x, omega, off, near, projected, logs, wide, *, rows_dev, devices, entries, edge):
    far_limit, near_limit = limits(entries, devices)
    on_diagonal = lax.broadcasted_iota(jnp.int32, (edge, edge), 0) == lax.broadcasted_iota(
        jnp.int32, (edge, edge), 1
    )

    def apply(block, rows):
        high, low = split_halves(block)
        return jnp.dot(
            jnp.concatenate([high, low], axis=1),
            jnp.concatenate([rows, rows], axis=0),
            preferred_element_type=jnp.float32,
        )

    total = jnp.zeros((1, edge), jnp.float32)
    for k in range(rows_dev):
        projected[k] = apply(omega[k], x[k])
        total = total + jnp.log(
            jnp.sum(jnp.where(on_diagonal, omega[k], 0.0), axis=0, keepdims=True)
        )
    projected[rows_dev] = jnp.zeros(projected.shape[1:], jnp.float32)
    logs[...] = jnp.broadcast_to(total, logs.shape)

    def add(k, carry):
        row = lists[1, k]
        block = off[jnp.minimum(lists[0, k], entries - 1)]
        projected[row] = projected[row] + apply(block, near[lists[2, k]])
        return carry

    lax.fori_loop(far_limit, far_limit + near_limit, add, 0)

    def widen(k, carry):
        high, low = split_halves(off[jnp.minimum(lists[0, k], entries - 1)])
        wide[k, :, :edge] = high
        wide[k, :, edge:] = low
        return carry

    lax.fori_loop(0, far_limit, widen, 0)


def main_kernel(
    lists,
    logs,
    far,
    near,
    own,
    wide,
    payload,
    projected,
    held_near,
    held_wide,
    held_own,
    held_rows,
    halves,
    coded,
    stats,
    tail,
    sem_near,
    sem_wide,
    sem_own,
    sem_rows,
    sem_code,
    *,
    rows_dev,
    devices,
    entries,
    edge,
    samples_dev,
):
    far_limit, near_limit = limits(entries, devices)
    limit = far_limit + near_limit
    split = far_limit // 4
    parts = (pl.ds(0, split), pl.ds(split, far_limit - split))
    fetches = [
        pltpu.make_async_copy(wide.at[part], held_wide.at[part], sem_wide.at[at])
        for at, part in enumerate(parts)
    ]
    fetch_own = pltpu.make_async_copy(own.at[pl.ds(0, rows_dev)], held_own, sem_own.at[0])
    fetch_near = pltpu.make_async_copy(near, held_near, sem_near.at[0])
    for fetch in (*fetches, fetch_own, fetch_near):
        fetch.start()
    held_rows[...] = jnp.zeros(held_rows.shape, jnp.float32)
    stats[...] = jnp.zeros(stats.shape, jnp.float32)
    halves[rows_dev] = jnp.zeros(halves.shape[1:], halves.dtype)

    total = jnp.zeros((edge, samples_dev), jnp.float32)
    for k in range(far_limit):
        if k == 0:
            fetches[0].wait()
        if k == split:
            fetches[1].wait()
        rows = far[lists[2, k]]
        part = jnp.dot(
            held_wide[k],
            jnp.concatenate([rows, rows], axis=0),
            preferred_element_type=jnp.float32,
        )
        row = lists[1, k]
        total = part if k == 0 else jnp.where(row == lists[1, k - 1], total, 0.0) + part
        held_rows[row] = total

    fetch_own.wait()
    squares = jnp.zeros((8, samples_dev), jnp.float32)
    for k in range(rows_dev):
        values = held_rows[k] + held_own[k]
        held_own[k] = values
        squares = squares + jnp.sum((values * values).reshape(edge // 8, 8, samples_dev), axis=0)
        high, low = split_halves(values)
        halves[k, :edge] = high
        halves[k, edge:] = low
    store_rows = pltpu.make_async_copy(held_own, projected, sem_rows.at[0])
    store_rows.start()
    fetch_near.wait()

    def store(k):
        slot = lists[3, k]
        owner = divide(slot, SLOTS)
        rank = slot - owner * SLOTS
        return pltpu.make_async_copy(
            coded.at[k],
            payload.at[owner, pl.ds(pl.multiple_of(rank * edge, edge), edge), :],
            sem_code.at[k],
        )

    def begin(k, carry):
        store(k).start()
        return carry

    def finish(k, carry):
        store(k).wait()
        return carry

    def encode(k, rows):
        slot = lists[3, k]
        both = lax.dot_general(
            rows,
            halves[lists[1, k]],
            (((1,), (1,)), ((), ())),
            preferred_element_type=jnp.float32,
        )
        product = both[:, :edge] + both[:, edge:]
        largest = jnp.maximum(jnp.max(jnp.abs(product), axis=0, keepdims=True), 1e-30)
        code = jnp.ceil(jnp.log2(largest) * LOG_STEPS + 0.01)
        scaled = product * jnp.exp2(15.0 - HEADROOM - code * (1.0 / LOG_STEPS))
        owner = divide(slot, SLOTS)
        coded[k] = jnp.round(scaled).astype(jnp.int32).astype(jnp.int16)
        stats[owner, pl.ds(slot - owner * SLOTS, 1), :] = code

    fars = lists[0, limit + 1]
    nears = lists[0, limit + 2]
    for k in range(far_limit):
        encode(k, far[lists[2, k]])
    lax.fori_loop(0, fars, begin, 0)
    for k in range(far_limit, limit):
        encode(k, held_near[lists[2, k]])
    lax.fori_loop(far_limit, nears, begin, 0)

    term = jnp.sum(squares) * (1.0 / (2.0 * samples_dev)) - jnp.sum(logs[0:1, :])
    term = jnp.full((1, edge), term, jnp.float32)
    power = jnp.ceil(jnp.log2(jnp.maximum(jnp.abs(term), 1e-30)) + 0.01)
    scaled = term * jnp.exp2(14.0 - power)
    whole = jnp.round(scaled)
    digits = jnp.concatenate(
        [
            jnp.zeros((SLOTS, edge), jnp.float32),
            power,
            whole,
            jnp.round((scaled - whole) * FRACTION),
            jnp.zeros((STAT_ROWS - SLOTS - 3, edge), jnp.float32),
        ],
        axis=0,
    )
    tail[...] = (stats[...] + digits[None]).astype(jnp.int32).astype(jnp.int16)
    store_tail = pltpu.make_async_copy(
        tail, payload.at[:, pl.ds(SLOTS * edge, STAT_ROWS), :], sem_code.at[limit]
    )
    store_tail.start()
    lax.fori_loop(0, fars, finish, 0)
    lax.fori_loop(far_limit, nears, finish, 0)
    store_rows.wait()
    store_tail.wait()


def side_kernel(
    lists,
    x,
    omega,
    term,
    projected,
    off,
    far,
    near,
    result,
    moved,
    halves,
    *,
    rows_dev,
    devices,
    entries,
    edge,
    samples_dev,
):
    far_limit, near_limit = limits(entries, devices)
    on_diagonal = lax.broadcasted_iota(jnp.int32, (edge, edge), 0) == lax.broadcasted_iota(
        jnp.int32, (edge, edge), 1
    )

    def against(row, other):
        both = lax.dot_general(
            halves[row], other, (((1,), (1,)), ((), ())), preferred_element_type=jnp.float32
        )
        return both[:edge] + both[edge:]

    moved[...] = jnp.zeros(moved.shape, jnp.float32)
    halves[rows_dev] = jnp.zeros(halves.shape[1:], halves.dtype)
    for k in range(rows_dev):
        high, low = split_halves(projected[k])
        halves[k, :edge] = high
        halves[k, edge:] = low
        product = against(k, x[k])
        gradient = (product + product.T) * (1.0 / (2.0 * samples_dev))
        gradient = gradient + jnp.where(on_diagonal, term[k : k + 1, :], 0.0)
        value = omega[k] - STEP_SIZE * gradient
        result[k] = jnp.where(on_diagonal, value, soften(value, STEP_SIZE * PENALTY))

    def move(source, k, carry):
        e = lists[0, k]
        product = against(lists[1, k], source[lists[2, k]])
        moved[e] = off[jnp.minimum(e, entries - 1)] - product * (STEP_SIZE / (2.0 * samples_dev))
        return carry

    lax.fori_loop(0, far_limit, functools.partial(move, far), 0)
    lax.fori_loop(far_limit, far_limit + near_limit, functools.partial(move, near), 0)


def last_kernel(
    count,
    slots,
    moved,
    returned,
    result,
    objective,
    held,
    rt,
    rs,
    sem_in,
    sem_rt,
    sem_out,
    *,
    rows_dev,
    devices,
    entries,
    edge,
    samples_dev,
):
    live = live_count(count, rows_dev)

    def fetch(at, part):
        return pltpu.make_async_copy(moved.at[part], held.at[part], sem_in.at[at])

    def store(at, part):
        return pltpu.make_async_copy(rs.at[part], result.at[part], sem_out.at[at])

    width = max(k for k in range(1, 11) if entries % k == 0)
    parts = [(at, pl.ds(at * width, width)) for at in range(entries // width)]
    whole = pltpu.make_async_copy(returned, rt, sem_rt.at[0])
    whole.start()
    for at, part in parts:
        fetch(at, part).start()
    whole.wait()
    codes = rt[:, SLOTS * edge :, :].astype(jnp.int32).astype(jnp.float32)
    power = codes[:, SLOTS : SLOTS + 1]
    digits = codes[:, SLOTS + 1 : SLOTS + 2] + codes[:, SLOTS + 2 : SLOTS + 3] * (1.0 / FRACTION)
    total = jnp.sum(digits * jnp.exp2(power - 14.0), axis=0)
    objective[0] = jnp.max(total) * (1.0 / (devices * rows_dev * edge))
    for at, part in parts:
        fetch(at, part).wait()
        for e in range(at * width, (at + 1) * width):
            slot = slots[e]
            owner = divide(slot, SLOTS)
            rank = slot - owner * SLOTS
            codes = rt[owner, SLOTS * edge :, :].astype(jnp.int32).astype(jnp.float32)
            code = jnp.where(rank == 0, codes[0:1], codes[1:2])
            weight = jnp.exp2(code * (1.0 / LOG_STEPS) - (15.0 - HEADROOM)) * (
                STEP_SIZE / (2.0 * samples_dev)
            )
            weight = jnp.where(e < live, weight, 0.0)
            digits = rt[owner, pl.ds(pl.multiple_of(rank * edge, edge), edge), :]
            value = held[e] - digits.astype(jnp.int32).astype(jnp.float32) * weight
            rs[e] = soften(value, STEP_SIZE * PENALTY)
        store(at, part).start()
    for at, part in parts:
        store(at, part).wait()


def shards(samples, omega_diag, omega_off, pattern, block_count, diag_term):
    devices = lax.axis_size("rows")
    rows_dev, edge = omega_diag.shape[:2]
    samples_dev = samples.shape[1]
    entries = omega_off.shape[0]
    f32 = jnp.float32
    x = samples.reshape(rows_dev, edge, samples_dev)
    term = diag_term.reshape(rows_dev, edge)
    pattern = pattern.T
    smem = pl.BlockSpec(memory_space=pltpu.SMEM)
    vmem = pl.BlockSpec(memory_space=pltpu.VMEM)
    hbm = pl.BlockSpec(memory_space=pltpu.HBM)
    params = pltpu.CompilerParams(vmem_limit_bytes=VMEM_LIMIT)
    alone = pltpu.CompilerParams(vmem_limit_bytes=VMEM_ALONE)
    sizes = dict(rows_dev=rows_dev, entries=entries, edge=edge)
    every = dict(sizes, devices=devices, samples_dev=samples_dev)
    held = functools.partial(pltpu.with_memory_space_constraint, memory_space=pltpu.VMEM)
    kept = functools.partial(pltpu.with_memory_space_constraint, memory_space=pltpu.HBM)

    dma = pltpu.SemaphoreType.DMA

    half = devices // 2
    far_limit, near_limit = limits(entries, devices)
    limit = far_limit + near_limit
    across = [(o, (o + half) % devices) for o in range(devices)]
    halves = [list(range(half)), list(range(half, devices))]

    other = lax.ppermute(kept(x), "rows", across)

    send, slots, lists, wanted = pl.pallas_call(
        functools.partial(
            pack_kernel,
            rows_dev=rows_dev,
            devices=devices,
            entries=entries,
            block_total=rows_dev * devices,
        ),
        out_shape=(
            pltpu.HBM((SLOTS * half, edge, samples_dev), samples.dtype),
            jax.ShapeDtypeStruct((entries,), jnp.int32),
            jax.ShapeDtypeStruct((4, limit + 3), jnp.int32),
            jax.ShapeDtypeStruct((SLOTS * half + 1,), jnp.int32),
        ),
        in_specs=[smem, smem, hbm],
        out_specs=(hbm, smem, smem, smem),
        scratch_shapes=[
            pltpu.SMEM((devices,), jnp.int32),
            pltpu.SMEM((entries,), jnp.int32),
            pltpu.VMEM((rows_dev, edge, samples_dev), samples.dtype),
            dma((1,)),
            dma((near_limit + 1,)),
        ],
        compiler_params=params,
        name="pack",
    )(pattern, block_count, kept(x))

    def within(blocks):
        return lax.all_to_all(
            blocks.reshape(half, SLOTS, edge, samples_dev),
            "rows",
            split_axis=0,
            concat_axis=0,
            axis_index_groups=halves,
            tiled=True,
        ).reshape(SLOTS * half, edge, samples_dev)

    wanted = lax.ppermute(wanted, "rows", across)
    near = within(send)

    passed = pl.pallas_call(
        functools.partial(relay_kernel, devices=devices),
        out_shape=pltpu.HBM((SLOTS * half, edge, samples_dev), samples.dtype),
        in_specs=[smem, vmem],
        out_specs=hbm,
        scratch_shapes=[dma((SLOTS * half,))],
        compiler_params=params,
        name="relay",
    )(wanted, held(other))
    far = within(passed)

    own, logs, wide = pl.pallas_call(
        functools.partial(own_kernel, devices=devices, **sizes),
        out_shape=(
            pltpu.HBM((rows_dev + 1, edge, samples_dev), f32),
            jax.ShapeDtypeStruct((8, edge), f32),
            pltpu.HBM((far_limit, edge, 2 * edge), jnp.bfloat16),
        ),
        in_specs=[smem] + [vmem] * 4,
        out_specs=(vmem, vmem, vmem),
        compiler_params=params,
        cost_estimate=pl.CostEstimate(
            flops=12 * rows_dev * edge * edge * samples_dev, transcendentals=0, bytes_accessed=1 << 23
        ),
        name="own",
    )(lists, x, omega_diag, omega_off, near)

    payload, projected = pl.pallas_call(
        functools.partial(main_kernel, **every),
        out_shape=(
            pltpu.HBM((devices, SLOTS * edge + STAT_ROWS, edge), jnp.int16),
            pltpu.HBM((rows_dev, edge, samples_dev), f32),
        ),
        in_specs=[smem, vmem, vmem, hbm, hbm, hbm],
        out_specs=(hbm, hbm),
        scratch_shapes=[
            pltpu.VMEM((SLOTS * half, edge, samples_dev), samples.dtype),
            pltpu.VMEM((far_limit, edge, 2 * edge), jnp.bfloat16),
            pltpu.VMEM((rows_dev, edge, samples_dev), f32),
            pltpu.VMEM((rows_dev + 1, edge, samples_dev), f32),
            pltpu.VMEM((rows_dev + 1, 2 * edge, samples_dev), jnp.bfloat16),
            pltpu.VMEM((limit, edge, edge), jnp.int16),
            pltpu.VMEM((devices, STAT_ROWS, edge), f32),
            pltpu.VMEM((devices, STAT_ROWS, edge), jnp.int16),
            dma((1,)),
            dma((2,)),
            dma((1,)),
            dma((1,)),
            dma((limit + 1,)),
        ],
        compiler_params=params,
        name="main",
    )(lists, logs, held(far), kept(near), kept(own), kept(wide))

    returned = lax.all_to_all(kept(payload), "rows", split_axis=0, concat_axis=0, tiled=True)

    diag_next, moved = pl.pallas_call(
        functools.partial(side_kernel, **every),
        out_shape=(
            jax.ShapeDtypeStruct((rows_dev, edge, edge), f32),
            pltpu.HBM((entries + 1, edge, edge), f32),
        ),
        in_specs=[smem] + [vmem] * 7,
        out_specs=(vmem, vmem),
        scratch_shapes=[pltpu.VMEM((rows_dev + 1, 2 * edge, samples_dev), jnp.bfloat16)],
        compiler_params=params,
        cost_estimate=pl.CostEstimate(
            flops=12 * rows_dev * edge * edge * samples_dev, transcendentals=0, bytes_accessed=1 << 23
        ),
        name="side",
    )(lists, x, omega_diag, term, projected, omega_off, far, near)

    off_next, objective = pl.pallas_call(
        functools.partial(last_kernel, **every),
        out_shape=(
            jax.ShapeDtypeStruct((entries, edge, edge), f32),
            jax.ShapeDtypeStruct((1,), f32),
        ),
        in_specs=[smem, smem, hbm, hbm],
        out_specs=(hbm, smem),
        scratch_shapes=[
            pltpu.VMEM((entries, edge, edge), f32),
            pltpu.VMEM((devices, SLOTS * edge + STAT_ROWS, edge), jnp.int16),
            pltpu.VMEM((entries, edge, edge), f32),
            dma((entries,)),
            dma((1,)),
            dma((entries,)),
        ],
        compiler_params=alone,
        name="last",
    )(block_count, slots, kept(moved), kept(returned))
    return diag_next, off_next, objective


def solution(mesh):
    return jax.shard_map(
        shards,
        mesh=mesh,
        in_specs=(
            P(("groups", "rows"), None),
            P(("groups", "rows"), None, None),
            P(("groups", "rows"), None, None),
            P(("groups", "rows"), None),
            P(("groups", "rows")),
            P(("groups", "rows")),
        ),
        out_specs=(
            P(("groups", "rows"), None, None),
            P(("groups", "rows"), None, None),
            P("groups"),
        ),
        check_vma=False,
    )
```

time: 101 us -> 98.7 us (0.977)
  waiting for transfers between devices: 58 us -> 44.5 us
  starting transfers between devices: 10.9 us -> 18 us
  Pallas kernels: 26 us -> 28.5 us
  local copies, waits for them, and re-layouts: 4.34 us -> 6.3 us
    all_to_all x1 -> x2, waiting for transfers between devices: 43.1 us -> 8.04 us  [within(): lax.all_to_all(blocks.reshape(half, SLOTS, edge, samples_dev), 'rows', sp...]
    ppermute x0 -> x2, waiting for transfers between devices: none -> 21.6 us  [the longest x1 21.6 us: shards(): wanted = lax.ppermute(wanted, 'rows', across)]
    pallas_call x2 -> x3, Pallas kernels: 11.2 us -> 14.9 us  [the longest x1 8.32 us: shards(): pl.pallas_call(functools.partial(side_kernel, **every), out_shape=(jax.Sh...]
    all_to_all x1 -> x2, starting transfers between devices: 6.27 us -> 9.75 us  [within(): lax.all_to_all(blocks.reshape(half, SLOTS, edge, samples_dev), 'rows', sp...]
    ppermute x0 -> x2, starting transfers between devices: none -> 2.99 us  [the longest x1 2.59 us: shards(): wanted = lax.ppermute(wanted, 'rows', across)]
    unnamed x18 -> x22, local copies, waits for them, and re-layouts: 4.34 us -> 6.3 us
  transfers between devices with their start and end apart: 2 -> 5, of which waited for: 2 -> 3; matrix products, arithmetic and copies ran while one was open for 0% -> 0% of each run, Pallas kernels for 11% -> 15%
where the time goes in v4:
time: 98.7 us; the launch traced here: 98 us
  waiting for transfers between devices  44.5 us (45%)
  Pallas kernels  28.5 us (29%)
  starting transfers between devices  18 us (18%)
  local copies, waits for them, and re-layouts  6.3 us (6%)
    ppermute x1, waiting for transfers between devices, shards(): wanted = lax.ppermute(wanted, 'rows', across)  21.6 us
    all_to_all x1, waiting for transfers between devices, shards(): lax.all_to_all(kept(payload), 'rows', split_axis=0, concat_axis=0, tiled=...  14.8 us
    all_to_all x2, starting transfers between devices, within(): lax.all_to_all(blocks.reshape(half, SLOTS, edge, samples_dev), 'rows', sp...  9.75 us
    pallas_call x1, Pallas kernels, shards(): pl.pallas_call(functools.partial(side_kernel, **every), out_shape=(jax.Sh...  8.32 us
    all_to_all x2, waiting for transfers between devices, within(): lax.all_to_all(blocks.reshape(half, SLOTS, edge, samples_dev), 'rows', sp...  8.04 us
    unnamed x22, local copies, waits for them, and re-layouts  6.3 us
    pallas_call x1, Pallas kernels, shards(): pl.pallas_call(functools.partial(main_kernel, **every), out_shape=(pltpu....  5.41 us
    all_to_all x1, starting transfers between devices, shards(): lax.all_to_all(kept(payload), 'rows', split_axis=0, concat_axis=0, tiled=...  5.26 us
  transfers between devices with their start and end apart: 5, of which 3 were waited for; matrix products, arithmetic and copies ran while one was open for 0% of the time, Pallas kernels for 15%

profile of v4, /device:TPU:16, one launch (start us, length us, event | category | flops | bytes accessed | tf_op | source)
XLA Modules:
  0.0 98.0 jit_solution(11084570979345051902)
XLA Ops:
  0.6 0.0 copy-start.4
  0.6 0.0 copy-start.8
  0.7 0.7 copy-done.8
  1.4 0.7 copy-done.9
  2.0 3.3 %pack.1 = (bf16[16,128,256]{2,1,0:T(8,128)(2,1)}, s32[30]{0:T(128)S(1)}, s32[4,33]{1,0:T(4,128)S(1)}, s32[17]{0:T(128)S(1)}) custom-call(s32[2,30]{1,0:T(2,128)S(1)} %bitcast.17, s32[8]{0:T(128)S(1)} %copy-done.8, bf16[8,128,256]{2,1,0:T(8,128)(2,1)} %bitcast.12), custom_call_target="tpu_custom_call" | custom-call | tf_op jit(solution)/shard_map/pack/pallas_call | solution.py:474
  5.3 0.0 copy-start.10
  5.3 0.6 copy-done.10
  5.9 3.9 %all-to-all-start = ((bf16[8,2,128,256]{3,2,1,0:T(8,128)(2,1)}), bf16[8,2,128,256]{3,2,1,0:T(8,128)(2,1)S(1)}, u32[]{:S(2)}, u32[]{:S(2)}) async-start(bf16[8,2,128,256]{3,2,1,0:T(8,128)(2,1)} %bitcast.19), calls=%async_computation | async-start | bytes 2097152 | tf_op jit(solution)/shard_map/all_to_all | solution.py:502
  9.7 0.0 copy-done.4
  9.7 0.0 copy-start.5
  9.8 0.4 collective-permute-start.1
  10.2 2.6 %collective-permute-start = (s32[17]{0:T(128)S(1)}, s32[17]{0:T(128)S(1)}, u32[]{:S(2)}, u32[]{:S(2)}) collective-permute-start(s32[17]{0:T(128)S(1)} %get-tuple-element.19), channel_id=1, source_target_pairs={{0,8},{1,9},{2,10},{3,11},{4,12},{5,13},{6,14},{7,15},{8,0},{9,1},... | collective-permute-start | bytes 212 | tf_op jit(solution)/shard_map/ppermute | solution.py:511
  12.7 21.6 %collective-permute-done.wanted = s32[17]{0:T(128)S(1)} collective-permute-done((s32[17]{0:T(128)S(1)}, s32[17]{0:T(128)S(1)}, u32[]{:S(2)}, u32[]{:S(2)}) %collective-permute-start) | collective-permute-done | bytes 100 | tf_op jit(solution)/shard_map/ppermute | solution.py:511
  34.3 0.0 collective-permute-done.1.x
  34.3 1.7 %relay.1 = bf16[16,128,256]{2,1,0:T(8,128)(2,1)} custom-call(s32[17]{0:T(128)S(1)} %collective-permute-done.wanted, bf16[8,128,256]{2,1,0:T(8,128)(2,1)S(1)} %collective-permute-done.1.x), custom_call_target="tpu_custom_call" | custom-call | tf_op jit(solution)/shard_map/relay/pallas_call | solution.py:514
  36.0 0.0 all-to-all-done
  36.0 0.0 copy-start
  36.0 5.9 %all-to-all-start.1 = ((bf16[8,2,128,256]{3,2,1,0:T(8,128)(2,1)}), bf16[8,2,128,256]{3,2,1,0:T(8,128)(2,1)S(1)}, u32[]{:S(2)}, u32[]{:S(2)}) async-start(bf16[8,2,128,256]{3,2,1,0:T(8,128)(2,1)} %bitcast.18), calls=%async_computation.1 | async-start | bytes 2097152 | tf_op jit(solution)/shard_map/all_to_all | solution.py:502
  41.9 0.0 copy-done.5
  41.9 0.0 copy-start.2
  42.0 1.5 %copy-done.2 = f32[30,128,128]{2,1,0:T(8,128)S(1)} copy-done((f32[30,128,128]{2,1,0:T(8,128)S(1)}, f32[30,128,128]{2,1,0:T(8,128)}, u32[]{:S(2)}) %copy-start.2) | copy-done | bytes 1966104
  43.5 4.9 %own.1 = (f32[9,128,256]{2,1,0:T(8,128)}, f32[8,128]{1,0:T(8,128)S(1)}, bf16[16,128,256]{2,1,0:T(8,128)(2,1)}) custom-call(s32[4,33]{1,0:T(4,128)S(1)} %get-tuple-element.16.lists, bf16[8,128,256]{2,1,0:T(8,128)(2,1)S(1)} %bitcast.14, f32[8,128,128]{2,1,0:T(8,128)S(1)} %copy-done.5, f32[30,128,128]{2,1,0:T(8,128)S(1)} %copy-done.2, ...), custom_call_target="tpu_custom_call" | custom-call | flops 402653184 | bytes 8388608 | tf_op jit(solution)/shard_map/own/pallas_call | solution.py:525
  48.4 8.0 %all-to-all-done.1 = bf16[8,2,128,256]{3,2,1,0:T(8,128)(2,1)S(1)} async-done(((bf16[8,2,128,256]{3,2,1,0:T(8,128)(2,1)}), bf16[8,2,128,256]{3,2,1,0:T(8,128)(2,1)S(1)}, u32[]{:S(2)}, u32[]{:S(2)}) %all-to-all-start.1) | async-done | bytes 1048608 | tf_op jit(solution)/shard_map/all_to_all | solution.py:502
  56.4 5.4 %main.1 = (s16[16,264,128]{2,1,0:T(8,128)(2,1)}, f32[8,128,256]{2,1,0:T(8,128)}) custom-call(s32[4,33]{1,0:T(4,128)S(1)} %get-tuple-element.16.lists, f32[8,128]{1,0:T(8,128)S(1)} %get-tuple-element.18.logs, bf16[16,128,256]{2,1,0:T(8,128)(2,1)S(1)} %bitcast.10, bf16[16,128,256]{2,1,0:T(8,128)(2,1)} %bitcast.8, f32[9,128,256]{2,1,0:T(8,128)} %get-tuple-element.20.own, ...), custom_call_target="tpu_custom_call" | custom-call | tf_op jit(solution)/shard_map/main/pallas_call | solution.py:541
  61.8 0.0 copy-start.7
  61.9 5.3 %all-to-all-start.2 = ((s16[16,264,128]{2,1,0:T(8,128)(2,1)}), s16[16,264,128]{2,1,0:T(8,128)(2,1)}, u32[]{:S(2)}, u32[]{:S(2)}) async-start(s16[16,264,128]{2,1,0:T(8,128)(2,1)} %get-tuple-element.26), calls=%async_computation.2 | async-start | bytes 2162688 | tf_op jit(solution)/shard_map/all_to_all | solution.py:568
  67.1 0.0 copy-start.3
  67.1 1.5 %copy-done.3 = f32[30,128,128]{2,1,0:T(8,128)S(1)} copy-done((f32[30,128,128]{2,1,0:T(8,128)S(1)}, f32[30,128,128]{2,1,0:T(8,128)}, u32[]{:S(2)}) %copy-start.3) | copy-done | bytes 1966104
  68.7 1.2 %copy-done.6 = f32[8,128,256]{2,1,0:T(8,128)S(1)} copy-done((f32[8,128,256]{2,1,0:T(8,128)S(1)}, f32[8,128,256]{2,1,0:T(8,128)}, u32[]{:S(2)}) %copy-start.6) | copy-done | bytes 1048600
  69.9 8.3 %side.1 = (f32[8,128,128]{2,1,0:T(8,128)}, f32[31,128,128]{2,1,0:T(8,128)}) custom-call(s32[4,33]{1,0:T(4,128)S(1)} %get-tuple-element.16.lists, bf16[8,128,256]{2,1,0:T(8,128)(2,1)S(1)} %bitcast.15, f32[8,128,128]{2,1,0:T(8,128)S(1)} %copy-done.5, f32[8,128]{1,0:T(8,128)S(1)} %bitcast.16, f32[8,128,256]{2,1,0:T(8,128)S(1)} %copy-done.6, ...), custom_call_target="tpu_custom_call" | custom-call | flops 402653184 | bytes 8388608 | tf_op jit(solution)/shard_map/side/pallas_call | solution.py:570
  78.2 14.8 %all-to-all-done.2.returned = s16[16,264,128]{2,1,0:T(8,128)(2,1)} async-done(((s16[16,264,128]{2,1,0:T(8,128)(2,1)}), s16[16,264,128]{2,1,0:T(8,128)(2,1)}, u32[]{:S(2)}, u32[]{:S(2)}) %all-to-all-start.2) | async-done | bytes 1081376 | tf_op jit(solution)/shard_map/all_to_all | solution.py:568
  93.1 5.0 %last.1 = (f32[30,128,128]{2,1,0:T(8,128)}, f32[1]{0:T(128)}) custom-call(s32[8]{0:T(128)} %count.3, s32[30]{0:T(128)} %copy-done.10, f32[31,128,128]{2,1,0:T(8,128)} %get-tuple-element.25.moved, s16[16,264,128]{2,1,0:T(8,128)(2,1)} %all-to-all-done.2.returned), custom_call_target="tpu_custom_call" | custom-call | tf_op jit(solution)/shard_map/last/pallas_call | solution.py:586
  (6 shorter events, 0.0 us)
Async XLA Ops:
  0.6 9.1 %copy-start.4 = (bf16[1024,256]{1,0:T(8,128)(2,1)S(1)}, bf16[1024,256]{1,0:T(8,128)(2,1)}, u32[]{:S(2)}) copy-start(bf16[1024,256]{1,0:T(8,128)(2,1)} %param.6) | copy-start | bytes 1572868
  0.6 0.7 copy-start.8
  1.4 0.7 copy-start.9
  5.3 0.6 copy-start.10
  5.9 30.1 %all-to-all-start = ((bf16[8,2,128,256]{3,2,1,0:T(8,128)(2,1)}), bf16[8,2,128,256]{3,2,1,0:T(8,128)(2,1)S(1)}, u32[]{:S(2)}, u32[]{:S(2)}) async-start(bf16[8,2,128,256]{3,2,1,0:T(8,128)(2,1)} %bitcast.19), calls=%async_computation | async-start | bytes 2097152 | tf_op jit(solution)/shard_map/all_to_all | solution.py:502
  9.7 32.2 %copy-start.5 = (f32[8,128,128]{2,1,0:T(8,128)S(1)}, f32[8,128,128]{2,1,0:T(8,128)}, u32[]{:S(2)}) copy-start(f32[8,128,128]{2,1,0:T(8,128)} %omega.3) | copy-start | bytes 1572868
  9.8 24.6 %collective-permute-start.1 = (bf16[8,128,256]{2,1,0:T(8,128)(2,1)S(1)}, bf16[8,128,256]{2,1,0:T(8,128)(2,1)S(1)}, u32[]{:S(2)}, u32[]{:S(2)}) collective-permute-start(bf16[8,128,256]{2,1,0:T(8,128)(2,1)S(1)} %bitcast.13), channel_id=1, source_target_pairs={{0,8},{1,9},{2,10},{3,11},{4,12},{5,13},{6,14},{7,15},{8,0},{9,1},... | collective-permute-start | bytes 1572872 | tf_op jit(solution)/shard_map/ppermute | solution.py:472
  10.2 24.2 %collective-permute-start = (s32[17]{0:T(128)S(1)}, s32[17]{0:T(128)S(1)}, u32[]{:S(2)}, u32[]{:S(2)}) collective-permute-start(s32[17]{0:T(128)S(1)} %get-tuple-element.19), channel_id=1, source_target_pairs={{0,8},{1,9},{2,10},{3,11},{4,12},{5,13},{6,14},{7,15},{8,0},{9,1},... | collective-permute-start | bytes 212 | tf_op jit(solution)/shard_map/ppermute | solution.py:511
  36.0 12.3 %copy-start = (bf16[8,2,128,256]{3,2,1,0:T(8,128)(2,1)}, bf16[8,2,128,256]{3,2,1,0:T(8,128)(2,1)S(1)}, u32[]{:S(2)}) copy-start(bf16[8,2,128,256]{3,2,1,0:T(8,128)(2,1)S(1)} %all-to-all-done) | copy-start | bytes 3145732
  36.0 20.4 %all-to-all-start.1 = ((bf16[8,2,128,256]{3,2,1,0:T(8,128)(2,1)}), bf16[8,2,128,256]{3,2,1,0:T(8,128)(2,1)S(1)}, u32[]{:S(2)}, u32[]{:S(2)}) async-start(bf16[8,2,128,256]{3,2,1,0:T(8,128)(2,1)} %bitcast.18), calls=%async_computation.1 | async-start | bytes 2097152 | tf_op jit(solution)/shard_map/all_to_all | solution.py:502
  41.9 1.5 %copy-start.2 = (f32[30,128,128]{2,1,0:T(8,128)S(1)}, f32[30,128,128]{2,1,0:T(8,128)}, u32[]{:S(2)}) copy-start(f32[30,128,128]{2,1,0:T(8,128)} %off.3) | copy-start | bytes 5898244
  61.8 5.3 %copy-start.1 = (bf16[8,2,128,256]{3,2,1,0:T(8,128)(2,1)S(1)}, bf16[8,2,128,256]{3,2,1,0:T(8,128)(2,1)}, u32[]{:S(2)}) copy-start(bf16[8,2,128,256]{3,2,1,0:T(8,128)(2,1)} %copy-done) | copy-start | bytes 3145732
  61.8 5.3 %copy-start.7 = (f32[1024]{0:T(1024)S(1)}, f32[1024]{0:T(1024)}, u32[]{:S(2)}) copy-start(f32[1024]{0:T(1024)} %param.11) | copy-start | bytes 12292
  61.9 31.2 %all-to-all-start.2 = ((s16[16,264,128]{2,1,0:T(8,128)(2,1)}), s16[16,264,128]{2,1,0:T(8,128)(2,1)}, u32[]{:S(2)}, u32[]{:S(2)}) async-start(s16[16,264,128]{2,1,0:T(8,128)(2,1)} %get-tuple-element.26), calls=%async_computation.2 | async-start | bytes 2162688 | tf_op jit(solution)/shard_map/all_to_all | solution.py:568
  67.1 1.5 %copy-start.3 = (f32[30,128,128]{2,1,0:T(8,128)S(1)}, f32[30,128,128]{2,1,0:T(8,128)}, u32[]{:S(2)}) copy-start(f32[30,128,128]{2,1,0:T(8,128)} %off.3) | copy-start | bytes 5898244
  68.7 1.2 %copy-start.6 = (f32[8,128,256]{2,1,0:T(8,128)S(1)}, f32[8,128,256]{2,1,0:T(8,128)}, u32[]{:S(2)}) copy-start(f32[8,128,256]{2,1,0:T(8,128)} %get-tuple-element.22.projected) | copy-start | bytes 3145732

commit v5 on v4

--- a/solution.py
+++ b/solution.py
@@ -136,7 +136,9 @@
     lax.fori_loop(far_limit, nears, finish, 0)
 
 
-def relay_kernel(wanted, x, send, sems, *, devices):
+def relay_kernel(wanted, early, late, send, x, sems, *, devices):
+    x[: early.shape[0]] = early[...]
+    x[early.shape[0] :] = late[...]
     copies = [
         pltpu.make_async_copy(x.at[wanted[q]], send.at[q], sems.at[q])
         for q in range(SLOTS * (devices // 2))
@@ -469,7 +471,8 @@
     across = [(o, (o + half) % devices) for o in range(devices)]
     halves = [list(range(half)), list(range(half, devices))]
 
-    other = lax.ppermute(kept(x), "rows", across)
+    early = max(1, rows_dev // 4)
+    other_early = lax.ppermute(x[:early], "rows", across)
 
     send, slots, lists, wanted = pl.pallas_call(
         functools.partial(
@@ -510,16 +513,20 @@
 
     wanted = lax.ppermute(wanted, "rows", across)
     near = within(send)
+    other_late = lax.ppermute(x[early:], "rows", across)
 
     passed = pl.pallas_call(
         functools.partial(relay_kernel, devices=devices),
         out_shape=pltpu.HBM((SLOTS * half, edge, samples_dev), samples.dtype),
-        in_specs=[smem, vmem],
+        in_specs=[smem, vmem, vmem],
         out_specs=hbm,
-        scratch_shapes=[dma((SLOTS * half,))],
+        scratch_shapes=[
+            pltpu.VMEM((rows_dev, edge, samples_dev), samples.dtype),
+            dma((SLOTS * half,)),
+        ],
         compiler_params=params,
         name="relay",
-    )(wanted, held(other))
+    )(wanted, held(other_early), held(other_late))
     far = within(passed)
 
     own, logs, wide = pl.pallas_call(

time: 98.7 us -> 98.7 us (level)
    ppermute x1 -> x2, starting transfers between devices: 0.4 us -> 3.06 us  [the longest x1 2.65 us: shards(): other_early = lax.ppermute(x[:early], 'rows', across)]
    ppermute x1, starting transfers between devices: 2.59 us -> 0.34 us  [shards(): wanted = lax.ppermute(wanted, 'rows', across)]
  transfers between devices with their start and end apart: 5 -> 6, of which waited for: 3 -> 3; matrix products, arithmetic and copies ran while one was open for 0% -> 0% of each run, Pallas kernels for 15% -> 15%
where the time goes in v5:
time: 98.7 us; the launch traced here: 98 us
  waiting for transfers between devices  44 us (45%)
  Pallas kernels  28.5 us (29%)
  starting transfers between devices  18.5 us (19%)
  local copies, waits for them, and re-layouts  6.25 us (6%)
    ppermute x1, waiting for transfers between devices, shards(): wanted = lax.ppermute(wanted, 'rows', across)  21.1 us
    all_to_all x1, waiting for transfers between devices, shards(): lax.all_to_all(kept(payload), 'rows', split_axis=0, concat_axis=0, tiled=...  14.8 us
    all_to_all x2, starting transfers between devices, within(): lax.all_to_all(blocks.reshape(half, SLOTS, edge, samples_dev), 'rows', sp...  9.8 us
    pallas_call x1, Pallas kernels, shards(): pl.pallas_call(functools.partial(side_kernel, **every), out_shape=(jax.Sh...  8.31 us
    all_to_all x2, waiting for transfers between devices, within(): lax.all_to_all(blocks.reshape(half, SLOTS, edge, samples_dev), 'rows', sp...  8.04 us
    unnamed x22, local copies, waits for them, and re-layouts  6.21 us
    pallas_call x1, Pallas kernels, shards(): pl.pallas_call(functools.partial(main_kernel, **every), out_shape=(pltpu....  5.41 us
    all_to_all x1, starting transfers between devices, shards(): lax.all_to_all(kept(payload), 'rows', split_axis=0, concat_axis=0, tiled=...  5.26 us
  transfers between devices with their start and end apart: 6, of which 3 were waited for; matrix products, arithmetic and copies ran while one was open for 0% of the time, Pallas kernels for 15%

profile of v5, /device:TPU:16, one launch (start us, length us, event | category | flops | bytes accessed | tf_op | source)
XLA Modules:
  0.0 98.0 jit_solution(12583938120230219279)
XLA Ops:
  0.6 0.0 copy-start.2
  0.6 0.0 copy-start.8
  0.7 0.7 copy-done.8
  1.4 0.7 copy-done.9
  2.0 3.3 %pack.1 = (bf16[16,128,256]{2,1,0:T(8,128)(2,1)}, s32[30]{0:T(128)S(1)}, s32[4,33]{1,0:T(4,128)S(1)}, s32[17]{0:T(128)S(1)}) custom-call(s32[2,30]{1,0:T(2,128)S(1)} %bitcast.18, s32[8]{0:T(128)S(1)} %copy-done.8, bf16[8,128,256]{2,1,0:T(8,128)(2,1)} %bitcast.14), custom_call_target="tpu_custom_call" | custom-call | tf_op jit(solution)/shard_map/pack/pallas_call | solution.py:477
  5.3 0.0 copy-start.10
  5.3 0.5 copy-done.10
  5.8 3.9 %all-to-all-start = ((bf16[8,2,128,256]{3,2,1,0:T(8,128)(2,1)}), bf16[8,2,128,256]{3,2,1,0:T(8,128)(2,1)S(1)}, u32[]{:S(2)}, u32[]{:S(2)}) async-start(bf16[8,2,128,256]{3,2,1,0:T(8,128)(2,1)} %bitcast.20), calls=%async_computation | async-start | bytes 2097152 | tf_op jit(solution)/shard_map/all_to_all | solution.py:505
  9.7 0.0 copy-done.2
  9.7 0.0 copy-start.5
  9.7 0.4 collective-permute-start.2
  10.1 2.7 %collective-permute-start.1 = (bf16[2,128,256]{2,1,0:T(8,128)(2,1)S(1)}, bf16[2,128,256]{2,1,0:T(8,128)(2,1)S(1)}, u32[]{:S(2)}, u32[]{:S(2)}) collective-permute-start(bf16[2,128,256]{2,1,0:T(8,128)(2,1)S(1)} %bitcast.22), channel_id=1, source_target_pairs={{0,8},{1,9},{2,10},{3,11},{4,12},{5,13},{6,14},{7,15},{8,0},{9,1},... | collective-permute-start | bytes 393224 | tf_op jit(solution)/shard_map/ppermute | solution.py:475
  12.8 0.3 collective-permute-start
  13.1 21.1 %collective-permute-done.wanted = s32[17]{0:T(128)S(1)} collective-permute-done((s32[17]{0:T(128)S(1)}, s32[17]{0:T(128)S(1)}, u32[]{:S(2)}, u32[]{:S(2)}) %collective-permute-start) | collective-permute-done | bytes 100 | tf_op jit(solution)/shard_map/ppermute | solution.py:514
  34.3 0.0 collective-permute-done.1.early
  34.3 0.0 collective-permute-done.2.late
  34.3 1.7 %relay.1 = bf16[16,128,256]{2,1,0:T(8,128)(2,1)} custom-call(s32[17]{0:T(128)S(1)} %collective-permute-done.wanted, bf16[2,128,256]{2,1,0:T(8,128)(2,1)S(1)} %collective-permute-done.1.early, bf16[6,128,256]{2,1,0:T(8,128)(2,1)S(1)} %collective-permute-done.2.late), custom_call_target="tpu_custom_call" | custom-call | tf_op jit(solution)/shard_map/relay/pallas_call | solution.py:518
  36.0 0.0 all-to-all-done
  36.0 5.9 %all-to-all-start.1 = ((bf16[8,2,128,256]{3,2,1,0:T(8,128)(2,1)}), bf16[8,2,128,256]{3,2,1,0:T(8,128)(2,1)S(1)}, u32[]{:S(2)}, u32[]{:S(2)}) async-start(bf16[8,2,128,256]{3,2,1,0:T(8,128)(2,1)} %bitcast.19), calls=%async_computation.1 | async-start | bytes 2097152 | tf_op jit(solution)/shard_map/all_to_all | solution.py:505
  42.0 0.0 copy-start.3
  42.0 1.5 %copy-done.3 = f32[30,128,128]{2,1,0:T(8,128)S(1)} copy-done((f32[30,128,128]{2,1,0:T(8,128)S(1)}, f32[30,128,128]{2,1,0:T(8,128)}, u32[]{:S(2)}) %copy-start.3) | copy-done | bytes 1966104
  43.5 4.9 %own.1 = (f32[9,128,256]{2,1,0:T(8,128)}, f32[8,128]{1,0:T(8,128)S(1)}, bf16[16,128,256]{2,1,0:T(8,128)(2,1)}) custom-call(s32[4,33]{1,0:T(4,128)S(1)} %get-tuple-element.16.lists, bf16[8,128,256]{2,1,0:T(8,128)(2,1)S(1)} %bitcast.15, f32[8,128,128]{2,1,0:T(8,128)S(1)} %copy-done.5, f32[30,128,128]{2,1,0:T(8,128)S(1)} %copy-done.3, ...), custom_call_target="tpu_custom_call" | custom-call | flops 402653184 | bytes 8388608 | tf_op jit(solution)/shard_map/own/pallas_call | solution.py:532
  48.4 8.0 %all-to-all-done.1 = bf16[8,2,128,256]{3,2,1,0:T(8,128)(2,1)S(1)} async-done(((bf16[8,2,128,256]{3,2,1,0:T(8,128)(2,1)}), bf16[8,2,128,256]{3,2,1,0:T(8,128)(2,1)S(1)}, u32[]{:S(2)}, u32[]{:S(2)}) %all-to-all-start.1) | async-done | bytes 1048608 | tf_op jit(solution)/shard_map/all_to_all | solution.py:505
  56.4 5.4 %main.1 = (s16[16,264,128]{2,1,0:T(8,128)(2,1)}, f32[8,128,256]{2,1,0:T(8,128)}) custom-call(s32[4,33]{1,0:T(4,128)S(1)} %get-tuple-element.16.lists, f32[8,128]{1,0:T(8,128)S(1)} %get-tuple-element.18.logs, bf16[16,128,256]{2,1,0:T(8,128)(2,1)S(1)} %bitcast.12, bf16[16,128,256]{2,1,0:T(8,128)(2,1)} %bitcast.10, f32[9,128,256]{2,1,0:T(8,128)} %get-tuple-element.20.own, ...), custom_call_target="tpu_custom_call" | custom-call | tf_op jit(solution)/shard_map/main/pallas_call | solution.py:548
  61.9 0.0 copy-start.7
  61.9 5.3 %all-to-all-start.2 = ((s16[16,264,128]{2,1,0:T(8,128)(2,1)}), s16[16,264,128]{2,1,0:T(8,128)(2,1)}, u32[]{:S(2)}, u32[]{:S(2)}) async-start(s16[16,264,128]{2,1,0:T(8,128)(2,1)} %get-tuple-element.26), calls=%async_computation.2 | async-start | bytes 2162688 | tf_op jit(solution)/shard_map/all_to_all | solution.py:575
  67.1 0.0 copy-start.4
  67.2 1.5 %copy-done.4 = f32[30,128,128]{2,1,0:T(8,128)S(1)} copy-done((f32[30,128,128]{2,1,0:T(8,128)S(1)}, f32[30,128,128]{2,1,0:T(8,128)}, u32[]{:S(2)}) %copy-start.4) | copy-done | bytes 1966104
  68.7 1.2 %copy-done.6 = f32[8,128,256]{2,1,0:T(8,128)S(1)} copy-done((f32[8,128,256]{2,1,0:T(8,128)S(1)}, f32[8,128,256]{2,1,0:T(8,128)}, u32[]{:S(2)}) %copy-start.6) | copy-done | bytes 1048600
  69.9 8.3 %side.1 = (f32[8,128,128]{2,1,0:T(8,128)}, f32[31,128,128]{2,1,0:T(8,128)}) custom-call(s32[4,33]{1,0:T(4,128)S(1)} %get-tuple-element.16.lists, bf16[8,128,256]{2,1,0:T(8,128)(2,1)S(1)} %bitcast.16, f32[8,128,128]{2,1,0:T(8,128)S(1)} %copy-done.5, f32[8,128]{1,0:T(8,128)S(1)} %bitcast.17, f32[8,128,256]{2,1,0:T(8,128)S(1)} %copy-done.6, ...), custom_call_target="tpu_custom_call" | custom-call | flops 402653184 | bytes 8388608 | tf_op jit(solution)/shard_map/side/pallas_call | solution.py:577
  78.2 14.8 %all-to-all-done.2.returned = s16[16,264,128]{2,1,0:T(8,128)(2,1)} async-done(((s16[16,264,128]{2,1,0:T(8,128)(2,1)}), s16[16,264,128]{2,1,0:T(8,128)(2,1)}, u32[]{:S(2)}, u32[]{:S(2)}) %all-to-all-start.2) | async-done | bytes 1081376 | tf_op jit(solution)/shard_map/all_to_all | solution.py:575
  93.1 5.0 %last.1 = (f32[30,128,128]{2,1,0:T(8,128)}, f32[1]{0:T(128)}) custom-call(s32[8]{0:T(128)} %count.3, s32[30]{0:T(128)} %copy-done.10, f32[31,128,128]{2,1,0:T(8,128)} %get-tuple-element.25.moved, s16[16,264,128]{2,1,0:T(8,128)(2,1)} %all-to-all-done.2.returned), custom_call_target="tpu_custom_call" | custom-call | tf_op jit(solution)/shard_map/last/pallas_call | solution.py:593
  (10 shorter events, 0.1 us)
Async XLA Ops:
  0.6 9.0 %copy-start.2 = (bf16[1024,256]{1,0:T(8,128)(2,1)S(1)}, bf16[1024,256]{1,0:T(8,128)(2,1)}, u32[]{:S(2)}) copy-start(bf16[1024,256]{1,0:T(8,128)(2,1)} %param.6) | copy-start | bytes 1572868
  0.6 0.7 copy-start.8
  1.4 0.7 copy-start.9
  5.3 0.5 copy-start.10
  5.8 30.2 %all-to-all-start = ((bf16[8,2,128,256]{3,2,1,0:T(8,128)(2,1)}), bf16[8,2,128,256]{3,2,1,0:T(8,128)(2,1)S(1)}, u32[]{:S(2)}, u32[]{:S(2)}) async-start(bf16[8,2,128,256]{3,2,1,0:T(8,128)(2,1)} %bitcast.20), calls=%async_computation | async-start | bytes 2097152 | tf_op jit(solution)/shard_map/all_to_all | solution.py:505
  9.7 32.3 %copy-start.5 = (f32[8,128,128]{2,1,0:T(8,128)S(1)}, f32[8,128,128]{2,1,0:T(8,128)}, u32[]{:S(2)}) copy-start(f32[8,128,128]{2,1,0:T(8,128)} %omega.3) | copy-start | bytes 1572868
  9.7 24.6 %collective-permute-start.2 = (bf16[6,128,256]{2,1,0:T(8,128)(2,1)S(1)}, bf16[6,128,256]{2,1,0:T(8,128)(2,1)S(1)}, u32[]{:S(2)}, u32[]{:S(2)}) collective-permute-start(bf16[6,128,256]{2,1,0:T(8,128)(2,1)S(1)} %bitcast.21), channel_id=1, source_target_pairs={{0,8},{1,9},{2,10},{3,11},{4,12},{5,13},{6,14},{7,15},{8,0},{9,1},... | collective-permute-start | bytes 1179656 | tf_op jit(solution)/shard_map/ppermute | solution.py:516
  10.1 24.1 %collective-permute-start.1 = (bf16[2,128,256]{2,1,0:T(8,128)(2,1)S(1)}, bf16[2,128,256]{2,1,0:T(8,128)(2,1)S(1)}, u32[]{:S(2)}, u32[]{:S(2)}) collective-permute-start(bf16[2,128,256]{2,1,0:T(8,128)(2,1)S(1)} %bitcast.22), channel_id=1, source_target_pairs={{0,8},{1,9},{2,10},{3,11},{4,12},{5,13},{6,14},{7,15},{8,0},{9,1},... | collective-permute-start | bytes 393224 | tf_op jit(solution)/shard_map/ppermute | solution.py:475
  12.8 21.5 %collective-permute-start = (s32[17]{0:T(128)S(1)}, s32[17]{0:T(128)S(1)}, u32[]{:S(2)}, u32[]{:S(2)}) collective-permute-start(s32[17]{0:T(128)S(1)} %get-tuple-element.19), channel_id=1, source_target_pairs={{0,8},{1,9},{2,10},{3,11},{4,12},{5,13},{6,14},{7,15},{8,0},{9,1},... | collective-permute-start | bytes 212 | tf_op jit(solution)/shard_map/ppermute | solution.py:514
  36.0 12.4 %copy-start = (bf16[8,2,128,256]{3,2,1,0:T(8,128)(2,1)}, bf16[8,2,128,256]{3,2,1,0:T(8,128)(2,1)S(1)}, u32[]{:S(2)}) copy-start(bf16[8,2,128,256]{3,2,1,0:T(8,128)(2,1)S(1)} %all-to-all-done) | copy-start | bytes 3145732
  36.0 20.4 %all-to-all-start.1 = ((bf16[8,2,128,256]{3,2,1,0:T(8,128)(2,1)}), bf16[8,2,128,256]{3,2,1,0:T(8,128)(2,1)S(1)}, u32[]{:S(2)}, u32[]{:S(2)}) async-start(bf16[8,2,128,256]{3,2,1,0:T(8,128)(2,1)} %bitcast.19), calls=%async_computation.1 | async-start | bytes 2097152 | tf_op jit(solution)/shard_map/all_to_all | solution.py:505
  42.0 1.5 %copy-start.3 = (f32[30,128,128]{2,1,0:T(8,128)S(1)}, f32[30,128,128]{2,1,0:T(8,128)}, u32[]{:S(2)}) copy-start(f32[30,128,128]{2,1,0:T(8,128)} %off.3) | copy-start | bytes 5898244
  61.8 5.3 %copy-start.1 = (bf16[8,2,128,256]{3,2,1,0:T(8,128)(2,1)S(1)}, bf16[8,2,128,256]{3,2,1,0:T(8,128)(2,1)}, u32[]{:S(2)}) copy-start(bf16[8,2,128,256]{3,2,1,0:T(8,128)(2,1)} %copy-done) | copy-start | bytes 3145732
  61.9 5.3 %copy-start.7 = (f32[1024]{0:T(1024)S(1)}, f32[1024]{0:T(1024)}, u32[]{:S(2)}) copy-start(f32[1024]{0:T(1024)} %param.11) | copy-start | bytes 12292
  61.9 31.2 %all-to-all-start.2 = ((s16[16,264,128]{2,1,0:T(8,128)(2,1)}), s16[16,264,128]{2,1,0:T(8,128)(2,1)}, u32[]{:S(2)}, u32[]{:S(2)}) async-start(s16[16,264,128]{2,1,0:T(8,128)(2,1)} %get-tuple-element.26), calls=%async_computation.2 | async-start | bytes 2162688 | tf_op jit(solution)/shard_map/all_to_all | solution.py:575
  67.1 1.5 %copy-start.4 = (f32[30,128,128]{2,1,0:T(8,128)S(1)}, f32[30,128,128]{2,1,0:T(8,128)}, u32[]{:S(2)}) copy-start(f32[30,128,128]{2,1,0:T(8,128)} %off.3) | copy-start | bytes 5898244
  68.7 1.2 %copy-start.6 = (f32[8,128,256]{2,1,0:T(8,128)S(1)}, f32[8,128,256]{2,1,0:T(8,128)}, u32[]{:S(2)}) copy-start(f32[8,128,256]{2,1,0:T(8,128)} %get-tuple-element.22.projected) | copy-start | bytes 3145732

commit v6 on v5

--- a/solution.py
+++ b/solution.py
@@ -30,9 +30,13 @@
 
 
 def divide(value, by):
-    if by & (by - 1):
+    if isinstance(value, int) or by & (by - 1):
         return value // by
     return lax.shift_right_logical(value, by.bit_length() - 1)
+
+
+def mirror(o, devices, layer):
+    return o + (devices - layer) - 2 * layer * divide(o, layer)
 
 
 def limits(entries, devices):
@@ -63,6 +67,7 @@
     *,
     rows_dev,
     devices,
+    layer,
     entries,
     block_total,
 ):
@@ -109,7 +114,9 @@
         at = jnp.where(alive, jnp.where(near, nears, fars), far_limit + near_limit)
         lists[0, at] = e
         lists[1, at] = row
-        lists[2, at] = place
+        across = mirror(owner, devices, layer)
+        across = across - divide(across, half) * half
+        lists[2, at] = jnp.where(near, place, across * SLOTS + later)
         lists[3, at] = slot
         fars = fars + jnp.where(alive & ~near, 1, 0)
         nears = nears + jnp.where(alive & near, 1, 0)
@@ -136,9 +143,8 @@
     lax.fori_loop(far_limit, nears, finish, 0)
 
 
-def relay_kernel(wanted, early, late, send, x, sems, *, devices):
-    x[: early.shape[0]] = early[...]
-    x[early.shape[0] :] = late[...]
+def relay_kernel(wanted, outer, inner, send, x, sems, *, devices):
+    x[...] = outer[...] + inner[...]
     copies = [
         pltpu.make_async_copy(x.at[wanted[q]], send.at[q], sems.at[q])
         for q in range(SLOTS * (devices // 2))
@@ -444,7 +450,19 @@
         store(at, part).wait()
 
 
-def shards(samples, omega_diag, omega_off, pattern, block_count, diag_term):
+def layer_of(mesh):
+    spots = [getattr(d, "coords", None) for d in mesh.devices.reshape(-1, mesh.shape["rows"])[0]]
+    best = 1
+    for axis in range(3) if None not in spots else ():
+        places = [spot[axis] for spot in spots]
+        count = len(set(places))
+        runs = 1 + sum(a != b for a, b in zip(places, places[1:]))
+        if runs == count and count % 2 == 0:
+            best = max(best, len(places) // count)
+    return best
+
+
+def shards(samples, omega_diag, omega_off, pattern, block_count, diag_term, *, layer):
     devices = lax.axis_size("rows")
     rows_dev, edge = omega_diag.shape[:2]
     samples_dev = samples.shape[1]
@@ -468,17 +486,20 @@
     half = devices // 2
     far_limit, near_limit = limits(entries, devices)
     limit = far_limit + near_limit
-    across = [(o, (o + half) % devices) for o in range(devices)]
+    across = [(o, mirror(o, devices, layer)) for o in range(devices)]
+    steps = devices // layer
+    outer = [(o, m) for o, m in across if 4 * abs(2 * (o // layer) + 1 - steps) > 2 * steps]
+    inner = [pair for pair in across if pair not in outer]
     halves = [list(range(half)), list(range(half, devices))]
 
-    early = max(1, rows_dev // 4)
-    other_early = lax.ppermute(x[:early], "rows", across)
+    from_outer = lax.ppermute(kept(x), "rows", outer)
 
     send, slots, lists, wanted = pl.pallas_call(
         functools.partial(
             pack_kernel,
             rows_dev=rows_dev,
             devices=devices,
+            layer=layer,
             entries=entries,
             block_total=rows_dev * devices,
         ),
@@ -513,7 +534,7 @@
 
     wanted = lax.ppermute(wanted, "rows", across)
     near = within(send)
-    other_late = lax.ppermute(x[early:], "rows", across)
+    from_inner = lax.ppermute(kept(x), "rows", inner)
 
     passed = pl.pallas_call(
         functools.partial(relay_kernel, devices=devices),
@@ -526,7 +547,7 @@
         ],
         compiler_params=params,
         name="relay",
-    )(wanted, held(other_early), held(other_late))
+    )(wanted, held(from_outer), held(from_inner))
     far = within(passed)
 
     own, logs, wide = pl.pallas_call(
@@ -614,7 +635,7 @@
 
 def solution(mesh):
     return jax.shard_map(
-        shards,
+        functools.partial(shards, layer=layer_of(mesh)),
         mesh=mesh,
         in_specs=(
             P(("groups", "rows"), None),

time: 98.7 us -> 99.3 us (level)
  waiting for transfers between devices: 44 us -> 45.6 us
  starting transfers between devices: 18.5 us -> 17.4 us
    all_to_all x2, starting transfers between devices: 9.8 us -> 7.42 us  [within(): lax.all_to_all(blocks.reshape(half, SLOTS, edge, samples_dev), 'rows', sp...]
    ppermute x1, waiting for transfers between devices: 21.1 us -> 22.8 us  [shards(): wanted = lax.ppermute(wanted, 'rows', across)]
where the time goes in v6:
time: 99.3 us; the launch traced here: 98.6 us
  waiting for transfers between devices  45.6 us (46%)
  Pallas kernels  28.5 us (29%)
  starting transfers between devices  17.4 us (18%)
  local copies, waits for them, and re-layouts  6.21 us (6%)
    ppermute x1, waiting for transfers between devices, shards(): wanted = lax.ppermute(wanted, 'rows', across)  22.8 us
    all_to_all x1, waiting for transfers between devices, shards(): lax.all_to_all(kept(payload), 'rows', split_axis=0, concat_axis=0, tiled=...  14.8 us
    pallas_call x1, Pallas kernels, shards(): pl.pallas_call(functools.partial(side_kernel, **every), out_shape=(jax.Sh...  8.32 us
    all_to_all x2, waiting for transfers between devices, within(): lax.all_to_all(blocks.reshape(half, SLOTS, edge, samples_dev), 'rows', sp...  7.96 us
    all_to_all x2, starting transfers between devices, within(): lax.all_to_all(blocks.reshape(half, SLOTS, edge, samples_dev), 'rows', sp...  7.42 us
    unnamed x22, local copies, waits for them, and re-layouts  6.21 us
    pallas_call x1, Pallas kernels, shards(): pl.pallas_call(functools.partial(main_kernel, **every), out_shape=(pltpu....  5.41 us
    all_to_all x1, starting transfers between devices, shards(): lax.all_to_all(kept(payload), 'rows', split_axis=0, concat_axis=0, tiled=...  5.25 us
  transfers between devices with their start and end apart: 6, of which 3 were waited for; matrix products, arithmetic and copies ran while one was open for 0% of the time, Pallas kernels for 15%

profile of v6, /device:TPU:16, one launch (start us, length us, event | category | flops | bytes accessed | tf_op | source)
XLA Modules:
  0.0 98.6 jit_solution(4934933935971697038)
XLA Ops:
  0.6 0.0 copy-start.4
  0.6 0.0 copy-start.8
  0.7 0.7 copy-done.8
  1.4 0.7 copy-done.9
  2.0 3.3 %pack.1 = (bf16[16,128,256]{2,1,0:T(8,128)(2,1)}, s32[30]{0:T(128)S(1)}, s32[4,33]{1,0:T(4,128)S(1)}, s32[17]{0:T(128)S(1)}) custom-call(s32[2,30]{1,0:T(2,128)S(1)} %bitcast.18, s32[8]{0:T(128)S(1)} %copy-done.8, bf16[8,128,256]{2,1,0:T(8,128)(2,1)} %bitcast.12), custom_call_target="tpu_custom_call" | custom-call | tf_op jit(solution)/shard_map/pack/pallas_call | solution.py:497
  5.3 0.5 copy-done.10
  5.8 3.9 %all-to-all-start = ((bf16[8,2,128,256]{3,2,1,0:T(8,128)(2,1)}), bf16[8,2,128,256]{3,2,1,0:T(8,128)(2,1)S(1)}, u32[]{:S(2)}, u32[]{:S(2)}) async-start(bf16[8,2,128,256]{3,2,1,0:T(8,128)(2,1)} %bitcast.20), calls=%async_computation | async-start | bytes 2097152 | tf_op jit(solution)/shard_map/all_to_all | solution.py:526
  9.7 0.0 copy-done.4
  9.7 2.8 %collective-permute-start.2 = (bf16[8,128,256]{2,1,0:T(8,128)(2,1)S(1)}, bf16[8,128,256]{2,1,0:T(8,128)(2,1)S(1)}, u32[]{:S(2)}, u32[]{:S(2)}) collective-permute-start(bf16[8,128,256]{2,1,0:T(8,128)(2,1)S(1)} %bitcast.13), channel_id=1, source_target_pairs={{4,8},{5,9},{6,10},{7,11},{8,4},{9,5},{10,6},{11,7},{20,24},{21,25... | collective-permute-start | bytes 1572872 | tf_op jit(solution)/shard_map/ppermute | solution.py:537
  12.5 0.7 collective-permute-start.1
  13.2 0.0 copy-start.5
  13.2 1.2 %collective-permute-start = (s32[17]{0:T(128)S(1)}, s32[17]{0:T(128)S(1)}, u32[]{:S(2)}, u32[]{:S(2)}) collective-permute-start(s32[17]{0:T(128)S(1)} %get-tuple-element.19), channel_id=1, source_target_pairs={{0,12},{1,13},{2,14},{3,15},{4,8},{5,9},{6,10},{7,11},{8,4},{9,5},... | collective-permute-start | bytes 212 | tf_op jit(solution)/shard_map/ppermute | solution.py:535
  14.4 22.8 %collective-permute-done.wanted = s32[17]{0:T(128)S(1)} collective-permute-done((s32[17]{0:T(128)S(1)}, s32[17]{0:T(128)S(1)}, u32[]{:S(2)}, u32[]{:S(2)}) %collective-permute-start) | collective-permute-done | bytes 100 | tf_op jit(solution)/shard_map/ppermute | solution.py:535
  37.2 0.0 collective-permute-done.2.inner
  37.2 0.0 collective-permute-done.1.outer
  37.2 1.7 %relay.1 = bf16[16,128,256]{2,1,0:T(8,128)(2,1)} custom-call(s32[17]{0:T(128)S(1)} %collective-permute-done.wanted, bf16[8,128,256]{2,1,0:T(8,128)(2,1)S(1)} %collective-permute-done.1.outer, bf16[8,128,256]{2,1,0:T(8,128)(2,1)S(1)} %collective-permute-done.2.inner), custom_call_target="tpu_custom_call" | custom-call | tf_op jit(solution)/shard_map/relay/pallas_call | solution.py:539
  39.0 0.0 all-to-all-done
  39.0 3.6 %all-to-all-start.1 = ((bf16[8,2,128,256]{3,2,1,0:T(8,128)(2,1)}), bf16[8,2,128,256]{3,2,1,0:T(8,128)(2,1)S(1)}, u32[]{:S(2)}, u32[]{:S(2)}) async-start(bf16[8,2,128,256]{3,2,1,0:T(8,128)(2,1)} %bitcast.19), calls=%async_computation.1 | async-start | bytes 2097152 | tf_op jit(solution)/shard_map/all_to_all | solution.py:526
  42.6 0.0 copy-start.2
  42.6 1.5 %copy-done.2 = f32[30,128,128]{2,1,0:T(8,128)S(1)} copy-done((f32[30,128,128]{2,1,0:T(8,128)S(1)}, f32[30,128,128]{2,1,0:T(8,128)}, u32[]{:S(2)}) %copy-start.2) | copy-done | bytes 1966104
  44.1 4.9 %own.1 = (f32[9,128,256]{2,1,0:T(8,128)}, f32[8,128]{1,0:T(8,128)S(1)}, bf16[16,128,256]{2,1,0:T(8,128)(2,1)}) custom-call(s32[4,33]{1,0:T(4,128)S(1)} %get-tuple-element.16.lists, bf16[8,128,256]{2,1,0:T(8,128)(2,1)S(1)} %bitcast.15, f32[8,128,128]{2,1,0:T(8,128)S(1)} %copy-done.5, f32[30,128,128]{2,1,0:T(8,128)S(1)} %copy-done.2, ...), custom_call_target="tpu_custom_call" | custom-call | flops 402653184 | bytes 8388608 | tf_op jit(solution)/shard_map/own/pallas_call | solution.py:553
  49.0 8.0 %all-to-all-done.1 = bf16[8,2,128,256]{3,2,1,0:T(8,128)(2,1)S(1)} async-done(((bf16[8,2,128,256]{3,2,1,0:T(8,128)(2,1)}), bf16[8,2,128,256]{3,2,1,0:T(8,128)(2,1)S(1)}, u32[]{:S(2)}, u32[]{:S(2)}) %all-to-all-start.1) | async-done | bytes 1048608 | tf_op jit(solution)/shard_map/all_to_all | solution.py:526
  57.0 5.4 %main.1 = (s16[16,264,128]{2,1,0:T(8,128)(2,1)}, f32[8,128,256]{2,1,0:T(8,128)}) custom-call(s32[4,33]{1,0:T(4,128)S(1)} %get-tuple-element.16.lists, f32[8,128]{1,0:T(8,128)S(1)} %get-tuple-element.18.logs, bf16[16,128,256]{2,1,0:T(8,128)(2,1)S(1)} %bitcast.10, bf16[16,128,256]{2,1,0:T(8,128)(2,1)} %bitcast.8, f32[9,128,256]{2,1,0:T(8,128)} %get-tuple-element.20.own, ...), custom_call_target="tpu_custom_call" | custom-call | tf_op jit(solution)/shard_map/main/pallas_call | solution.py:569
  62.4 0.0 copy-start.7
  62.4 5.3 %all-to-all-start.2 = ((s16[16,264,128]{2,1,0:T(8,128)(2,1)}), s16[16,264,128]{2,1,0:T(8,128)(2,1)}, u32[]{:S(2)}, u32[]{:S(2)}) async-start(s16[16,264,128]{2,1,0:T(8,128)(2,1)} %get-tuple-element.26), calls=%async_computation.2 | async-start | bytes 2162688 | tf_op jit(solution)/shard_map/all_to_all | solution.py:596
  67.7 0.0 copy-done.7
  67.7 0.0 copy-start.3
  67.7 1.5 %copy-done.3 = f32[30,128,128]{2,1,0:T(8,128)S(1)} copy-done((f32[30,128,128]{2,1,0:T(8,128)S(1)}, f32[30,128,128]{2,1,0:T(8,128)}, u32[]{:S(2)}) %copy-start.3) | copy-done | bytes 1966104
  69.2 1.2 %copy-done.6 = f32[8,128,256]{2,1,0:T(8,128)S(1)} copy-done((f32[8,128,256]{2,1,0:T(8,128)S(1)}, f32[8,128,256]{2,1,0:T(8,128)}, u32[]{:S(2)}) %copy-start.6) | copy-done | bytes 1048600
  70.4 8.3 %side.1 = (f32[8,128,128]{2,1,0:T(8,128)}, f32[31,128,128]{2,1,0:T(8,128)}) custom-call(s32[4,33]{1,0:T(4,128)S(1)} %get-tuple-element.16.lists, bf16[8,128,256]{2,1,0:T(8,128)(2,1)S(1)} %bitcast.16, f32[8,128,128]{2,1,0:T(8,128)S(1)} %copy-done.5, f32[8,128]{1,0:T(8,128)S(1)} %bitcast.17, f32[8,128,256]{2,1,0:T(8,128)S(1)} %copy-done.6, ...), custom_call_target="tpu_custom_call" | custom-call | flops 402653184 | bytes 8388608 | tf_op jit(solution)/shard_map/side/pallas_call | solution.py:598
  78.8 14.8 %all-to-all-done.2.returned = s16[16,264,128]{2,1,0:T(8,128)(2,1)} async-done(((s16[16,264,128]{2,1,0:T(8,128)(2,1)}), s16[16,264,128]{2,1,0:T(8,128)(2,1)}, u32[]{:S(2)}, u32[]{:S(2)}) %all-to-all-start.2) | async-done | bytes 1081376 | tf_op jit(solution)/shard_map/all_to_all | solution.py:596
  93.6 5.0 %last.1 = (f32[30,128,128]{2,1,0:T(8,128)}, f32[1]{0:T(128)}) custom-call(s32[8]{0:T(128)} %count.3, s32[30]{0:T(128)} %copy-done.10, f32[31,128,128]{2,1,0:T(8,128)} %get-tuple-element.25.moved, s16[16,264,128]{2,1,0:T(8,128)(2,1)} %all-to-all-done.2.returned), custom_call_target="tpu_custom_call" | custom-call | tf_op jit(solution)/shard_map/last/pallas_call | solution.py:614
  (8 shorter events, 0.0 us)
Async XLA Ops:
  0.6 9.0 %copy-start.4 = (bf16[1024,256]{1,0:T(8,128)(2,1)S(1)}, bf16[1024,256]{1,0:T(8,128)(2,1)}, u32[]{:S(2)}) copy-start(bf16[1024,256]{1,0:T(8,128)(2,1)} %param.6) | copy-start | bytes 1572868
  0.6 0.7 copy-start.8
  1.4 0.7 copy-start.9
  5.3 0.5 copy-start.10
  5.8 33.2 %all-to-all-start = ((bf16[8,2,128,256]{3,2,1,0:T(8,128)(2,1)}), bf16[8,2,128,256]{3,2,1,0:T(8,128)(2,1)S(1)}, u32[]{:S(2)}, u32[]{:S(2)}) async-start(bf16[8,2,128,256]{3,2,1,0:T(8,128)(2,1)} %bitcast.20), calls=%async_computation | async-start | bytes 2097152 | tf_op jit(solution)/shard_map/all_to_all | solution.py:526
  9.7 27.6 %collective-permute-start.2 = (bf16[8,128,256]{2,1,0:T(8,128)(2,1)S(1)}, bf16[8,128,256]{2,1,0:T(8,128)(2,1)S(1)}, u32[]{:S(2)}, u32[]{:S(2)}) collective-permute-start(bf16[8,128,256]{2,1,0:T(8,128)(2,1)S(1)} %bitcast.13), channel_id=1, source_target_pairs={{4,8},{5,9},{6,10},{7,11},{8,4},{9,5},{10,6},{11,7},{20,24},{21,25... | collective-permute-start | bytes 1572872 | tf_op jit(solution)/shard_map/ppermute | solution.py:537
  12.5 24.8 %collective-permute-start.1 = (bf16[8,128,256]{2,1,0:T(8,128)(2,1)S(1)}, bf16[8,128,256]{2,1,0:T(8,128)(2,1)S(1)}, u32[]{:S(2)}, u32[]{:S(2)}) collective-permute-start(bf16[8,128,256]{2,1,0:T(8,128)(2,1)S(1)} %bitcast.14), channel_id=1, source_target_pairs={{0,12},{1,13},{2,14},{3,15},{12,0},{13,1},{14,2},{15,3},{16,28},{1... | collective-permute-start | bytes 1572872 | tf_op jit(solution)/shard_map/ppermute | solution.py:495
  13.2 29.4 %copy-start.5 = (f32[8,128,128]{2,1,0:T(8,128)S(1)}, f32[8,128,128]{2,1,0:T(8,128)}, u32[]{:S(2)}) copy-start(f32[8,128,128]{2,1,0:T(8,128)} %omega.3) | copy-start | bytes 1572868
  13.2 24.0 %collective-permute-start = (s32[17]{0:T(128)S(1)}, s32[17]{0:T(128)S(1)}, u32[]{:S(2)}, u32[]{:S(2)}) collective-permute-start(s32[17]{0:T(128)S(1)} %get-tuple-element.19), channel_id=1, source_target_pairs={{0,12},{1,13},{2,14},{3,15},{4,8},{5,9},{6,10},{7,11},{8,4},{9,5},... | collective-permute-start | bytes 212 | tf_op jit(solution)/shard_map/ppermute | solution.py:535
  39.0 10.0 %copy-start = (bf16[8,2,128,256]{3,2,1,0:T(8,128)(2,1)}, bf16[8,2,128,256]{3,2,1,0:T(8,128)(2,1)S(1)}, u32[]{:S(2)}) copy-start(bf16[8,2,128,256]{3,2,1,0:T(8,128)(2,1)S(1)} %all-to-all-done) | copy-start | bytes 3145732
  39.0 18.0 %all-to-all-start.1 = ((bf16[8,2,128,256]{3,2,1,0:T(8,128)(2,1)}), bf16[8,2,128,256]{3,2,1,0:T(8,128)(2,1)S(1)}, u32[]{:S(2)}, u32[]{:S(2)}) async-start(bf16[8,2,128,256]{3,2,1,0:T(8,128)(2,1)} %bitcast.19), calls=%async_computation.1 | async-start | bytes 2097152 | tf_op jit(solution)/shard_map/all_to_all | solution.py:526
  42.6 1.5 %copy-start.2 = (f32[30,128,128]{2,1,0:T(8,128)S(1)}, f32[30,128,128]{2,1,0:T(8,128)}, u32[]{:S(2)}) copy-start(f32[30,128,128]{2,1,0:T(8,128)} %off.3) | copy-start | bytes 5898244
  62.4 5.3 %copy-start.1 = (bf16[8,2,128,256]{3,2,1,0:T(8,128)(2,1)S(1)}, bf16[8,2,128,256]{3,2,1,0:T(8,128)(2,1)}, u32[]{:S(2)}) copy-start(bf16[8,2,128,256]{3,2,1,0:T(8,128)(2,1)} %copy-done) | copy-start | bytes 3145732
  62.4 5.3 %copy-start.7 = (f32[1024]{0:T(1024)S(1)}, f32[1024]{0:T(1024)}, u32[]{:S(2)}) copy-start(f32[1024]{0:T(1024)} %param.11) | copy-start | bytes 12292
  62.4 31.2 %all-to-all-start.2 = ((s16[16,264,128]{2,1,0:T(8,128)(2,1)}), s16[16,264,128]{2,1,0:T(8,128)(2,1)}, u32[]{:S(2)}, u32[]{:S(2)}) async-start(s16[16,264,128]{2,1,0:T(8,128)(2,1)} %get-tuple-element.26), calls=%async_computation.2 | async-start | bytes 2162688 | tf_op jit(solution)/shard_map/all_to_all | solution.py:596
  67.7 1.5 %copy-start.3 = (f32[30,128,128]{2,1,0:T(8,128)S(1)}, f32[30,128,128]{2,1,0:T(8,128)}, u32[]{:S(2)}) copy-start(f32[30,128,128]{2,1,0:T(8,128)} %off.3) | copy-start | bytes 5898244
  69.2 1.2 %copy-start.6 = (f32[8,128,256]{2,1,0:T(8,128)S(1)}, f32[8,128,256]{2,1,0:T(8,128)}, u32[]{:S(2)}) copy-start(f32[8,128,256]{2,1,0:T(8,128)} %get-tuple-element.22.projected) | copy-start | bytes 3145732

commit v7 on v6

--- a/solution.py
+++ b/solution.py
@@ -51,46 +51,11 @@
     return total
 
 
-def pack_kernel(
-    pattern,
-    count,
-    x,
-    send,
-    slots,
-    lists,
-    wanted,
-    sums,
-    keys,
-    held,
-    sem_x,
-    sems,
-    *,
-    rows_dev,
-    devices,
-    layer,
-    entries,
-    block_total,
-):
-    live = live_count(count, rows_dev)
-    half = devices // 2
-    far_limit, near_limit = limits(entries, devices)
+def place(pattern, keys, sums, visit, *, rows_dev, devices, entries):
     position = divide(pattern[0, 0], rows_dev)
-    base = position * rows_dev
-    side = divide(position, half)
-    spot = (position - side * half) * SLOTS
-
-    fetch = pltpu.make_async_copy(x, held, sem_x.at[0])
-    fetch.start()
-    spare = pltpu.make_async_copy(held.at[0], send.at[spot], sems.at[near_limit])
+    block_total = rows_dev * devices
     for o in range(devices):
         sums[o] = 0
-    for q in range(SLOTS * half):
-        wanted[q] = 0
-    for k in range(far_limit + near_limit):
-        lists[0, k] = entries
-        lists[1, k] = rows_dev
-        lists[2, k] = spot if k >= far_limit else 0
-        lists[3, k] = position * SLOTS
     for e in range(entries):
         i = pattern[0, e]
         j = pattern[1, e]
@@ -98,33 +63,35 @@
         key = jnp.minimum(i * block_total + j, j * block_total + i)
         keys[e] = key
         sums[owner] = sums[owner] + key
-    fars = jnp.int32(0)
-    nears = jnp.int32(far_limit)
     for e in range(entries):
-        row = pattern[0, e] - base
         owner = divide(pattern[1, e], rows_dev)
-        alive = e < live
-        later = jnp.where((2 * keys[e] > sums[owner]) & alive, 1, 0)
-        slot = owner * SLOTS + later
-        slots[e] = slot
-        away = divide(owner, half)
-        place = slot - away * (SLOTS * half)
-        near = away == side
-        wanted[jnp.where(alive & ~near, place, SLOTS * half)] = row
-        at = jnp.where(alive, jnp.where(near, nears, fars), far_limit + near_limit)
-        lists[0, at] = e
-        lists[1, at] = row
-        across = mirror(owner, devices, layer)
-        across = across - divide(across, half) * half
-        lists[2, at] = jnp.where(near, place, across * SLOTS + later)
-        lists[3, at] = slot
-        fars = fars + jnp.where(alive & ~near, 1, 0)
-        nears = nears + jnp.where(alive & near, 1, 0)
+        later = jnp.where(2 * keys[e] > sums[owner], 1, 0)
+        visit(e, pattern[0, e] - position * rows_dev, owner, later, owner != position)
+
+
+def pack_kernel(pattern, x, send, keys, sums, picks, held, sem_x, sems, *, rows_dev, devices, entries):
+    half = devices // 2
+    near_limit = limits(entries, devices)[1]
+    fetch = pltpu.make_async_copy(x, held, sem_x.at[0])
+    fetch.start()
+    position = divide(pattern[0, 0], rows_dev)
+    first = divide(position, half) * half
+    spare = pltpu.make_async_copy(
+        held.at[0], send.at[(position - first) * SLOTS], sems.at[near_limit]
+    )
+    total = [jnp.int32(0)]
+
+    def visit(e, row, owner, later, alive):
+        index = owner - first
+        wanted = alive & (index >= 0) & (index < half)
+        picks[0, total[0]] = row
+        picks[1, total[0]] = index * SLOTS + later
+        total[0] = total[0] + jnp.where(wanted, 1, 0)
+
+    place(pattern, keys, sums, visit, rows_dev=rows_dev, devices=devices, entries=entries)
 
     def copy(k):
-        return pltpu.make_async_copy(
-            held.at[lists[1, k]], send.at[lists[2, k]], sems.at[k - far_limit]
-        )
+        return pltpu.make_async_copy(held.at[picks[0, k]], send.at[picks[1, k]], sems.at[k])
 
     def begin(k, carry):
         copy(k).start()
@@ -136,11 +103,53 @@
 
     fetch.wait()
     spare.start()
-    lax.fori_loop(far_limit, nears, begin, 0)
-    lists[0, far_limit + near_limit + 1] = fars
-    lists[0, far_limit + near_limit + 2] = nears
+    lax.fori_loop(0, total[0], begin, 0)
     spare.wait()
-    lax.fori_loop(far_limit, nears, finish, 0)
+    lax.fori_loop(0, total[0], finish, 0)
+
+
+def plan_kernel(
+    pattern, other, slots, lists, wanted, keys, sums, *, rows_dev, devices, layer, entries
+):
+    half = devices // 2
+    far_limit, near_limit = limits(entries, devices)
+    limit = far_limit + near_limit
+    position = divide(pattern[0, 0], rows_dev)
+    first = divide(position, half) * half
+    for k in range(limit):
+        lists[0, k] = entries
+        lists[1, k] = rows_dev
+        lists[2, k] = (position - first) * SLOTS if k >= far_limit else 0
+        lists[3, k] = position * SLOTS
+    for q in range(SLOTS * half):
+        wanted[q] = 0
+    tops = [jnp.int32(0), jnp.int32(far_limit)]
+
+    def visit(e, row, owner, later, alive):
+        later = jnp.where(alive, later, 0)
+        slot = owner * SLOTS + later
+        slots[e] = slot
+        index = owner - first
+        near = (index >= 0) & (index < half)
+        across = mirror(owner, devices, layer) - first
+        at = jnp.where(alive, jnp.where(near, tops[1], tops[0]), limit)
+        lists[0, at] = e
+        lists[1, at] = row
+        lists[2, at] = jnp.where(near, index, across) * SLOTS + later
+        lists[3, at] = slot
+        tops[0] = tops[0] + jnp.where(alive & ~near, 1, 0)
+        tops[1] = tops[1] + jnp.where(alive & near, 1, 0)
+
+    place(pattern, keys, sums, visit, rows_dev=rows_dev, devices=devices, entries=entries)
+    lists[0, limit + 1] = tops[0]
+    lists[0, limit + 2] = tops[1]
+
+    def wish(e, row, owner, later, alive):
+        index = owner - first
+        ours = alive & (index >= 0) & (index < half)
+        wanted[jnp.where(ours, index * SLOTS + later, SLOTS * half)] = row
+
+    place(other, keys, sums, wish, rows_dev=rows_dev, devices=devices, entries=entries)
 
 
 def relay_kernel(wanted, outer, inner, send, x, sems, *, devices):
@@ -492,35 +501,40 @@
     inner = [pair for pair in across if pair not in outer]
     halves = [list(range(half)), list(range(half, devices))]
 
+    other_pattern = lax.ppermute(kept(pattern), "rows", across)
     from_outer = lax.ppermute(kept(x), "rows", outer)
 
-    send, slots, lists, wanted = pl.pallas_call(
-        functools.partial(
-            pack_kernel,
-            rows_dev=rows_dev,
-            devices=devices,
-            layer=layer,
-            entries=entries,
-            block_total=rows_dev * devices,
-        ),
-        out_shape=(
-            pltpu.HBM((SLOTS * half, edge, samples_dev), samples.dtype),
-            jax.ShapeDtypeStruct((entries,), jnp.int32),
-            jax.ShapeDtypeStruct((4, limit + 3), jnp.int32),
-            jax.ShapeDtypeStruct((SLOTS * half + 1,), jnp.int32),
-        ),
-        in_specs=[smem, smem, hbm],
-        out_specs=(hbm, smem, smem, smem),
+    ints = [pltpu.SMEM((entries,), jnp.int32), pltpu.SMEM((devices,), jnp.int32)]
+    places = dict(rows_dev=rows_dev, devices=devices, entries=entries)
+    send = pl.pallas_call(
+        functools.partial(pack_kernel, **places),
+        out_shape=pltpu.HBM((SLOTS * half, edge, samples_dev), samples.dtype),
+        in_specs=[smem, hbm],
+        out_specs=hbm,
         scratch_shapes=[
-            pltpu.SMEM((devices,), jnp.int32),
-            pltpu.SMEM((entries,), jnp.int32),
+            *ints,
+            pltpu.SMEM((2, entries + 1), jnp.int32),
             pltpu.VMEM((rows_dev, edge, samples_dev), samples.dtype),
             dma((1,)),
             dma((near_limit + 1,)),
         ],
+        compiler_params=alone,
+        name="pack",
+    )(pattern, kept(x))
+
+    slots, lists, wanted = pl.pallas_call(
+        functools.partial(plan_kernel, layer=layer, **places),
+        out_shape=(
+            jax.ShapeDtypeStruct((entries,), jnp.int32),
+            jax.ShapeDtypeStruct((4, limit + 3), jnp.int32),
+            jax.ShapeDtypeStruct((SLOTS * half + 1,), jnp.int32),
+        ),
+        in_specs=[smem, smem],
+        out_specs=(smem, smem, smem),
+        scratch_shapes=ints,
         compiler_params=params,
-        name="pack",
-    )(pattern, block_count, kept(x))
+        name="plan",
+    )(pattern, other_pattern)
 
     def within(blocks):
         return lax.all_to_all(
@@ -532,7 +546,6 @@
             tiled=True,
         ).reshape(SLOTS * half, edge, samples_dev)
 
-    wanted = lax.ppermute(wanted, "rows", across)
     near = within(send)
     from_inner = lax.ppermute(kept(x), "rows", inner)
 

time: 99.3 us -> 100 us (level)
  Pallas kernels: 28.5 us -> 30.5 us
    pallas_call x1 -> x2, Pallas kernels: 3.25 us -> 5.15 us  [the longest x1 2.89 us: shards(): pl.pallas_call(functools.partial(pack_kernel, **places), out_shape=pltpu....]
  transfers between devices with their start and end apart: 6 -> 6, of which waited for: 3 -> 3; matrix products, arithmetic and copies ran while one was open for 0% -> 0% of each run, Pallas kernels for 15% -> 17%
where the time goes in v7:
time: 100 us; the launch traced here: 99.6 us
  waiting for transfers between devices  45.6 us (46%)
  Pallas kernels  30.5 us (30%)
  starting transfers between devices  17.4 us (17%)
  local copies, waits for them, and re-layouts  5.39 us (5%)
    ppermute x1, waiting for transfers between devices, shards(): other_pattern = lax.ppermute(kept(pattern), 'rows', across)  22.8 us
    all_to_all x1, waiting for transfers between devices, shards(): lax.all_to_all(kept(payload), 'rows', split_axis=0, concat_axis=0, tiled=...  14.8 us
    pallas_call x1, Pallas kernels, shards(): pl.pallas_call(functools.partial(side_kernel, **every), out_shape=(jax.Sh...  8.32 us
    all_to_all x2, waiting for transfers between devices, within(): lax.all_to_all(blocks.reshape(half, SLOTS, edge, samples_dev), 'rows', sp...  7.95 us
    all_to_all x2, starting transfers between devices, within(): lax.all_to_all(blocks.reshape(half, SLOTS, edge, samples_dev), 'rows', sp...  7.43 us
    pallas_call x1, Pallas kernels, shards(): pl.pallas_call(functools.partial(main_kernel, **every), out_shape=(pltpu....  5.41 us
    unnamed x22, local copies, waits for them, and re-layouts  5.39 us
    all_to_all x1, starting transfers between devices, shards(): lax.all_to_all(kept(payload), 'rows', split_axis=0, concat_axis=0, tiled=...  5.25 us
  transfers between devices with their start and end apart: 6, of which 3 were waited for; matrix products, arithmetic and copies ran while one was open for 0% of the time, Pallas kernels for 17%

profile of v7, /device:TPU:16, one launch (start us, length us, event | category | flops | bytes accessed | tf_op | source)
XLA Modules:
  0.0 99.6 jit_solution(16127237993272082635)
XLA Ops:
  0.6 0.0 copy-start.8
  0.6 0.0 copy-start.4
  0.7 2.9 %pack.1 = bf16[16,128,256]{2,1,0:T(8,128)(2,1)} custom-call(s32[2,30]{1,0:T(2,128)} %bitcast.18, bf16[8,128,256]{2,1,0:T(8,128)(2,1)} %bitcast.12), custom_call_target="tpu_custom_call" | custom-call | tf_op jit(solution)/shard_map/pack/pallas_call | solution.py:509
  3.5 3.9 %all-to-all-start = ((bf16[8,2,128,256]{3,2,1,0:T(8,128)(2,1)}), bf16[8,2,128,256]{3,2,1,0:T(8,128)(2,1)S(1)}, u32[]{:S(2)}, u32[]{:S(2)}) async-start(bf16[8,2,128,256]{3,2,1,0:T(8,128)(2,1)} %bitcast.22), calls=%async_computation | async-start | bytes 2097152 | tf_op jit(solution)/shard_map/all_to_all | solution.py:540
  7.4 0.0 copy-done.4
  7.4 2.8 %collective-permute-start.2 = (bf16[8,128,256]{2,1,0:T(8,128)(2,1)S(1)}, bf16[8,128,256]{2,1,0:T(8,128)(2,1)S(1)}, u32[]{:S(2)}, u32[]{:S(2)}) collective-permute-start(bf16[8,128,256]{2,1,0:T(8,128)(2,1)S(1)} %bitcast.13), channel_id=1, source_target_pairs={{4,8},{5,9},{6,10},{7,11},{8,4},{9,5},{10,6},{11,7},{20,24},{21,25... | collective-permute-start | bytes 1572872 | tf_op jit(solution)/shard_map/ppermute | solution.py:550
  10.2 0.7 collective-permute-start.1
  10.9 0.0 copy-done.8
  10.9 1.2 %collective-permute-start = (s32[2,30]{1,0:T(2,128)S(1)}, s32[2,30]{1,0:T(2,128)S(1)}, u32[]{:S(2)}, u32[]{:S(2)}) collective-permute-start(s32[2,30]{1,0:T(2,128)S(1)} %bitcast.19), channel_id=1, source_target_pairs={{0,12},{1,13},{2,14},{3,15},{4,8},{5,9},{6,10},{7,11},{8,4},{9,5},... | collective-permute-start | bytes 728 | tf_op jit(solution)/shard_map/ppermute | solution.py:504
  12.1 22.8 %collective-permute-done.other = s32[2,30]{1,0:T(2,128)S(1)} collective-permute-done((s32[2,30]{1,0:T(2,128)S(1)}, s32[2,30]{1,0:T(2,128)S(1)}, u32[]{:S(2)}, u32[]{:S(2)}) %collective-permute-start) | collective-permute-done | bytes 272 | tf_op jit(solution)/shard_map/ppermute | solution.py:504
  35.0 0.6 copy-done.10
  35.5 2.3 %plan.1 = (s32[30]{0:T(128)S(1)}, s32[4,33]{1,0:T(4,128)S(1)}, s32[17]{0:T(128)S(1)}) custom-call(s32[2,30]{1,0:T(2,128)S(1)} %bitcast.20, s32[2,30]{1,0:T(2,128)} %copy-done.10), custom_call_target="tpu_custom_call" | custom-call | tf_op jit(solution)/shard_map/plan/pallas_call | solution.py:525
  37.8 0.5 copy-done.9
  38.3 0.0 collective-permute-done.2.inner
  38.3 0.0 collective-permute-done.1.outer
  38.3 1.7 %relay.1 = bf16[16,128,256]{2,1,0:T(8,128)(2,1)} custom-call(s32[17]{0:T(128)S(1)} %get-tuple-element.17.wanted, bf16[8,128,256]{2,1,0:T(8,128)(2,1)S(1)} %collective-permute-done.1.outer, bf16[8,128,256]{2,1,0:T(8,128)(2,1)S(1)} %collective-permute-done.2.inner), custom_call_target="tpu_custom_call" | custom-call | tf_op jit(solution)/shard_map/relay/pallas_call | solution.py:552
  40.0 0.0 all-to-all-done
  40.1 3.6 %all-to-all-start.1 = ((bf16[8,2,128,256]{3,2,1,0:T(8,128)(2,1)}), bf16[8,2,128,256]{3,2,1,0:T(8,128)(2,1)S(1)}, u32[]{:S(2)}, u32[]{:S(2)}) async-start(bf16[8,2,128,256]{3,2,1,0:T(8,128)(2,1)} %bitcast.21), calls=%async_computation.1 | async-start | bytes 2097152 | tf_op jit(solution)/shard_map/all_to_all | solution.py:540
  43.6 0.0 copy-start.2
  43.7 1.5 %copy-done.2 = f32[30,128,128]{2,1,0:T(8,128)S(1)} copy-done((f32[30,128,128]{2,1,0:T(8,128)S(1)}, f32[30,128,128]{2,1,0:T(8,128)}, u32[]{:S(2)}) %copy-start.2) | copy-done | bytes 1966104
  45.2 4.9 %own.1 = (f32[9,128,256]{2,1,0:T(8,128)}, f32[8,128]{1,0:T(8,128)S(1)}, bf16[16,128,256]{2,1,0:T(8,128)(2,1)}) custom-call(s32[4,33]{1,0:T(4,128)S(1)} %get-tuple-element.15.lists, bf16[8,128,256]{2,1,0:T(8,128)(2,1)S(1)} %bitcast.15, f32[8,128,128]{2,1,0:T(8,128)S(1)} %copy-done.5, f32[30,128,128]{2,1,0:T(8,128)S(1)} %copy-done.2, ...), custom_call_target="tpu_custom_call" | custom-call | flops 402653184 | bytes 8388608 | tf_op jit(solution)/shard_map/own/pallas_call | solution.py:566
  50.1 8.0 %all-to-all-done.1 = bf16[8,2,128,256]{3,2,1,0:T(8,128)(2,1)S(1)} async-done(((bf16[8,2,128,256]{3,2,1,0:T(8,128)(2,1)}), bf16[8,2,128,256]{3,2,1,0:T(8,128)(2,1)S(1)}, u32[]{:S(2)}, u32[]{:S(2)}) %all-to-all-start.1) | async-done | bytes 1048608 | tf_op jit(solution)/shard_map/all_to_all | solution.py:540
  58.0 5.4 %main.1 = (s16[16,264,128]{2,1,0:T(8,128)(2,1)}, f32[8,128,256]{2,1,0:T(8,128)}) custom-call(s32[4,33]{1,0:T(4,128)S(1)} %get-tuple-element.15.lists, f32[8,128]{1,0:T(8,128)S(1)} %get-tuple-element.16.logs, bf16[16,128,256]{2,1,0:T(8,128)(2,1)S(1)} %bitcast.10, bf16[16,128,256]{2,1,0:T(8,128)(2,1)} %bitcast.8, f32[9,128,256]{2,1,0:T(8,128)} %get-tuple-element.18.own, ...), custom_call_target="tpu_custom_call" | custom-call | tf_op jit(solution)/shard_map/main/pallas_call | solution.py:582
  63.5 0.0 copy-start.7
  63.5 5.3 %all-to-all-start.2 = ((s16[16,264,128]{2,1,0:T(8,128)(2,1)}), s16[16,264,128]{2,1,0:T(8,128)(2,1)}, u32[]{:S(2)}, u32[]{:S(2)}) async-start(s16[16,264,128]{2,1,0:T(8,128)(2,1)} %get-tuple-element.24), calls=%async_computation.2 | async-start | bytes 2162688 | tf_op jit(solution)/shard_map/all_to_all | solution.py:609
  68.7 0.0 copy-done.1
  68.7 0.0 copy-start.3
  68.8 1.5 %copy-done.3 = f32[30,128,128]{2,1,0:T(8,128)S(1)} copy-done((f32[30,128,128]{2,1,0:T(8,128)S(1)}, f32[30,128,128]{2,1,0:T(8,128)}, u32[]{:S(2)}) %copy-start.3) | copy-done | bytes 1966104
  70.3 1.2 %copy-done.6 = f32[8,128,256]{2,1,0:T(8,128)S(1)} copy-done((f32[8,128,256]{2,1,0:T(8,128)S(1)}, f32[8,128,256]{2,1,0:T(8,128)}, u32[]{:S(2)}) %copy-start.6) | copy-done | bytes 1048600
  71.5 8.3 %side.1 = (f32[8,128,128]{2,1,0:T(8,128)}, f32[31,128,128]{2,1,0:T(8,128)}) custom-call(s32[4,33]{1,0:T(4,128)S(1)} %get-tuple-element.15.lists, bf16[8,128,256]{2,1,0:T(8,128)(2,1)S(1)} %bitcast.16, f32[8,128,128]{2,1,0:T(8,128)S(1)} %copy-done.5, f32[8,128]{1,0:T(8,128)S(1)} %bitcast.17, f32[8,128,256]{2,1,0:T(8,128)S(1)} %copy-done.6, ...), custom_call_target="tpu_custom_call" | custom-call | flops 402653184 | bytes 8388608 | tf_op jit(solution)/shard_map/side/pallas_call | solution.py:611
  79.8 14.8 %all-to-all-done.2.returned = s16[16,264,128]{2,1,0:T(8,128)(2,1)} async-done(((s16[16,264,128]{2,1,0:T(8,128)(2,1)}), s16[16,264,128]{2,1,0:T(8,128)(2,1)}, u32[]{:S(2)}, u32[]{:S(2)}) %all-to-all-start.2) | async-done | bytes 1081376 | tf_op jit(solution)/shard_map/all_to_all | solution.py:609
  94.7 5.0 %last.1 = (f32[30,128,128]{2,1,0:T(8,128)}, f32[1]{0:T(128)}) custom-call(s32[8]{0:T(128)} %count.1, s32[30]{0:T(128)} %copy-done.9, f32[31,128,128]{2,1,0:T(8,128)} %get-tuple-element.23.moved, s16[16,264,128]{2,1,0:T(8,128)(2,1)} %all-to-all-done.2.returned), custom_call_target="tpu_custom_call" | custom-call | tf_op jit(solution)/shard_map/last/pallas_call | solution.py:627
  (9 shorter events, 0.0 us)
Async XLA Ops:
  0.6 10.3 %copy-start.8 = (s32[30,2]{0,1:T(2,128)S(1)}, s32[30,2]{0,1:T(2,128)}, u32[]{:S(2)}) copy-start(s32[30,2]{0,1:T(2,128)} %param.9) | copy-start | bytes 724
  0.6 6.8 %copy-start.4 = (bf16[1024,256]{1,0:T(8,128)(2,1)S(1)}, bf16[1024,256]{1,0:T(8,128)(2,1)}, u32[]{:S(2)}) copy-start(bf16[1024,256]{1,0:T(8,128)(2,1)} %param.6) | copy-start | bytes 1572868
  3.5 36.5 %all-to-all-start = ((bf16[8,2,128,256]{3,2,1,0:T(8,128)(2,1)}), bf16[8,2,128,256]{3,2,1,0:T(8,128)(2,1)S(1)}, u32[]{:S(2)}, u32[]{:S(2)}) async-start(bf16[8,2,128,256]{3,2,1,0:T(8,128)(2,1)} %bitcast.22), calls=%async_computation | async-start | bytes 2097152 | tf_op jit(solution)/shard_map/all_to_all | solution.py:540
  7.4 30.9 %collective-permute-start.2 = (bf16[8,128,256]{2,1,0:T(8,128)(2,1)S(1)}, bf16[8,128,256]{2,1,0:T(8,128)(2,1)S(1)}, u32[]{:S(2)}, u32[]{:S(2)}) collective-permute-start(bf16[8,128,256]{2,1,0:T(8,128)(2,1)S(1)} %bitcast.13), channel_id=1, source_target_pairs={{4,8},{5,9},{6,10},{7,11},{8,4},{9,5},{10,6},{11,7},{20,24},{21,25... | collective-permute-start | bytes 1572872 | tf_op jit(solution)/shard_map/ppermute | solution.py:550
  10.2 28.1 %collective-permute-start.1 = (bf16[8,128,256]{2,1,0:T(8,128)(2,1)S(1)}, bf16[8,128,256]{2,1,0:T(8,128)(2,1)S(1)}, u32[]{:S(2)}, u32[]{:S(2)}) collective-permute-start(bf16[8,128,256]{2,1,0:T(8,128)(2,1)S(1)} %bitcast.14), channel_id=1, source_target_pairs={{0,12},{1,13},{2,14},{3,15},{12,0},{13,1},{14,2},{15,3},{16,28},{1... | collective-permute-start | bytes 1572872 | tf_op jit(solution)/shard_map/ppermute | solution.py:505
  10.9 24.0 %collective-permute-start = (s32[2,30]{1,0:T(2,128)S(1)}, s32[2,30]{1,0:T(2,128)S(1)}, u32[]{:S(2)}, u32[]{:S(2)}) collective-permute-start(s32[2,30]{1,0:T(2,128)S(1)} %bitcast.19), channel_id=1, source_target_pairs={{0,12},{1,13},{2,14},{3,15},{4,8},{5,9},{6,10},{7,11},{8,4},{9,5},... | collective-permute-start | bytes 728 | tf_op jit(solution)/shard_map/ppermute | solution.py:504
  34.9 0.6 copy-start.10
  37.8 0.5 copy-start.9
  38.3 5.3 %copy-start.5 = (f32[8,128,128]{2,1,0:T(8,128)S(1)}, f32[8,128,128]{2,1,0:T(8,128)}, u32[]{:S(2)}) copy-start(f32[8,128,128]{2,1,0:T(8,128)} %omega.3) | copy-start | bytes 1572868
  40.0 10.0 %copy-start = (bf16[8,2,128,256]{3,2,1,0:T(8,128)(2,1)}, bf16[8,2,128,256]{3,2,1,0:T(8,128)(2,1)S(1)}, u32[]{:S(2)}) copy-start(bf16[8,2,128,256]{3,2,1,0:T(8,128)(2,1)S(1)} %all-to-all-done) | copy-start | bytes 3145732
  40.1 18.0 %all-to-all-start.1 = ((bf16[8,2,128,256]{3,2,1,0:T(8,128)(2,1)}), bf16[8,2,128,256]{3,2,1,0:T(8,128)(2,1)S(1)}, u32[]{:S(2)}, u32[]{:S(2)}) async-start(bf16[8,2,128,256]{3,2,1,0:T(8,128)(2,1)} %bitcast.21), calls=%async_computation.1 | async-start | bytes 2097152 | tf_op jit(solution)/shard_map/all_to_all | solution.py:540
  43.6 1.5 %copy-start.2 = (f32[30,128,128]{2,1,0:T(8,128)S(1)}, f32[30,128,128]{2,1,0:T(8,128)}, u32[]{:S(2)}) copy-start(f32[30,128,128]{2,1,0:T(8,128)} %off.3) | copy-start | bytes 5898244
  63.5 5.3 %copy-start.1 = (bf16[8,2,128,256]{3,2,1,0:T(8,128)(2,1)S(1)}, bf16[8,2,128,256]{3,2,1,0:T(8,128)(2,1)}, u32[]{:S(2)}) copy-start(bf16[8,2,128,256]{3,2,1,0:T(8,128)(2,1)} %copy-done) | copy-start | bytes 3145732
  63.5 5.3 %copy-start.7 = (f32[1024]{0:T(1024)S(1)}, f32[1024]{0:T(1024)}, u32[]{:S(2)}) copy-start(f32[1024]{0:T(1024)} %param.11) | copy-start | bytes 12292
  63.5 31.2 %all-to-all-start.2 = ((s16[16,264,128]{2,1,0:T(8,128)(2,1)}), s16[16,264,128]{2,1,0:T(8,128)(2,1)}, u32[]{:S(2)}, u32[]{:S(2)}) async-start(s16[16,264,128]{2,1,0:T(8,128)(2,1)} %get-tuple-element.24), calls=%async_computation.2 | async-start | bytes 2162688 | tf_op jit(solution)/shard_map/all_to_all | solution.py:609
  68.7 1.5 %copy-start.3 = (f32[30,128,128]{2,1,0:T(8,128)S(1)}, f32[30,128,128]{2,1,0:T(8,128)}, u32[]{:S(2)}) copy-start(f32[30,128,128]{2,1,0:T(8,128)} %off.3) | copy-start | bytes 5898244
  70.3 1.2 %copy-start.6 = (f32[8,128,256]{2,1,0:T(8,128)S(1)}, f32[8,128,256]{2,1,0:T(8,128)}, u32[]{:S(2)}) copy-start(f32[8,128,256]{2,1,0:T(8,128)} %get-tuple-element.20.projected) | copy-start | bytes 3145732

commit v8 on v7

--- a/solution.py
+++ b/solution.py
@@ -69,7 +69,25 @@
         visit(e, pattern[0, e] - position * rows_dev, owner, later, owner != position)
 
 
-def pack_kernel(pattern, x, send, keys, sums, picks, held, sem_x, sems, *, rows_dev, devices, entries):
+def pack_kernel(
+    pattern,
+    x,
+    send,
+    keys,
+    sums,
+    picks,
+    asked,
+    held,
+    tiles,
+    sem_x,
+    sems,
+    *,
+    rows_dev,
+    devices,
+    layer,
+    entries,
+    edge,
+):
     half = devices // 2
     near_limit = limits(entries, devices)[1]
     fetch = pltpu.make_async_copy(x, held, sem_x.at[0])
@@ -77,21 +95,39 @@
     position = divide(pattern[0, 0], rows_dev)
     first = divide(position, half) * half
     spare = pltpu.make_async_copy(
-        held.at[0], send.at[(position - first) * SLOTS], sems.at[near_limit]
+        held.at[0], send.at[position - first, pl.ds(0, edge)], sems.at[near_limit]
     )
     total = [jnp.int32(0)]
+    for q in range(SLOTS * half):
+        asked[q] = 0
 
     def visit(e, row, owner, later, alive):
         index = owner - first
-        wanted = alive & (index >= 0) & (index < half)
+        near = (index >= 0) & (index < half)
         picks[0, total[0]] = row
-        picks[1, total[0]] = index * SLOTS + later
-        total[0] = total[0] + jnp.where(wanted, 1, 0)
+        picks[1, total[0]] = index
+        picks[2, total[0]] = later
+        total[0] = total[0] + jnp.where(alive & near, 1, 0)
+        relay = (mirror(owner, devices, layer) - first) * SLOTS + later
+        asked[jnp.where(near, SLOTS * half, relay)] = pattern[1, e] - owner * rows_dev
 
     place(pattern, keys, sums, visit, rows_dev=rows_dev, devices=devices, entries=entries)
+    at = lax.broadcasted_iota(jnp.int32, tiles.shape[1:], 0)
+    for q in range(half):
+        tile = jnp.zeros(at.shape, jnp.int32)
+        for rank in range(SLOTS):
+            tile = jnp.where(at == rank, asked[q * SLOTS + rank], tile)
+        tiles[q] = tile.astype(jnp.float32).astype(jnp.bfloat16)
+    tell = pltpu.make_async_copy(
+        tiles, send.at[:, pl.ds(SLOTS * edge, STAT_ROWS), :], sems.at[near_limit + 1]
+    )
+    tell.start()
 
     def copy(k):
-        return pltpu.make_async_copy(held.at[picks[0, k]], send.at[picks[1, k]], sems.at[k])
+        rank = pl.multiple_of(picks[2, k] * edge, edge)
+        return pltpu.make_async_copy(
+            held.at[picks[0, k]], send.at[picks[1, k], pl.ds(rank, edge)], sems.at[k]
+        )
 
     def begin(k, carry):
         copy(k).start()
@@ -105,12 +141,16 @@
     spare.start()
     lax.fori_loop(0, total[0], begin, 0)
     spare.wait()
+    tell.wait()
     lax.fori_loop(0, total[0], finish, 0)
 
 
-def plan_kernel(
-    pattern, other, slots, lists, wanted, keys, sums, *, rows_dev, devices, layer, entries
-):
+def near_block(near, at, edge):
+    peer = divide(at, SLOTS)
+    return near[peer, pl.ds(pl.multiple_of((at - peer * SLOTS) * edge, edge), edge), :]
+
+
+def plan_kernel(pattern, slots, lists, keys, sums, *, rows_dev, devices, layer, entries):
     half = devices // 2
     far_limit, near_limit = limits(entries, devices)
     limit = far_limit + near_limit
@@ -121,8 +161,6 @@
         lists[1, k] = rows_dev
         lists[2, k] = (position - first) * SLOTS if k >= far_limit else 0
         lists[3, k] = position * SLOTS
-    for q in range(SLOTS * half):
-        wanted[q] = 0
     tops = [jnp.int32(0), jnp.int32(far_limit)]
 
     def visit(e, row, owner, later, alive):
@@ -144,22 +182,18 @@
     lists[0, limit + 1] = tops[0]
     lists[0, limit + 2] = tops[1]
 
-    def wish(e, row, owner, later, alive):
-        index = owner - first
-        ours = alive & (index >= 0) & (index < half)
-        wanted[jnp.where(ours, index * SLOTS + later, SLOTS * half)] = row
-
-    place(other, keys, sums, wish, rows_dev=rows_dev, devices=devices, entries=entries)
-
-
-def relay_kernel(wanted, outer, inner, send, x, sems, *, devices):
+
+def relay_kernel(near, outer, inner, send, x, sems, *, devices, edge):
     x[...] = outer[...] + inner[...]
-    copies = [
-        pltpu.make_async_copy(x.at[wanted[q]], send.at[q], sems.at[q])
-        for q in range(SLOTS * (devices // 2))
-    ]
-    for copy in copies:
-        copy.start()
+    copies = []
+    for q in range(devices // 2):
+        tile = near[q, SLOTS * edge :, :].astype(jnp.float32)
+        for rank in range(SLOTS):
+            row = jnp.max(tile[rank : rank + 1, :128]).astype(jnp.int32)
+            row = jnp.clip(row, 0, x.shape[0] - 1)
+            at = q * SLOTS + rank
+            copies.append(pltpu.make_async_copy(x.at[row], send.at[at], sems.at[at]))
+            copies[-1].start()
     for copy in copies:
         copy.wait()
 
@@ -190,7 +224,7 @@
     def add(k, carry):
         row = lists[1, k]
         block = off[jnp.minimum(lists[0, k], entries - 1)]
-        projected[row] = projected[row] + apply(block, near[lists[2, k]])
+        projected[row] = projected[row] + apply(block, near_block(near, lists[2, k], edge))
         return carry
 
     lax.fori_loop(far_limit, far_limit + near_limit, add, 0)
@@ -318,7 +352,7 @@
         encode(k, far[lists[2, k]])
     lax.fori_loop(0, fars, begin, 0)
     for k in range(far_limit, limit):
-        encode(k, held_near[lists[2, k]])
+        encode(k, near_block(held_near, lists[2, k], edge))
     lax.fori_loop(far_limit, nears, begin, 0)
 
     term = jnp.sum(squares) * (1.0 / (2.0 * samples_dev)) - jnp.sum(logs[0:1, :])
@@ -389,14 +423,19 @@
         value = omega[k] - STEP_SIZE * gradient
         result[k] = jnp.where(on_diagonal, value, soften(value, STEP_SIZE * PENALTY))
 
-    def move(source, k, carry):
+    def move(block, k, carry):
         e = lists[0, k]
-        product = against(lists[1, k], source[lists[2, k]])
+        product = against(lists[1, k], block(lists[2, k]))
         moved[e] = off[jnp.minimum(e, entries - 1)] - product * (STEP_SIZE / (2.0 * samples_dev))
         return carry
 
-    lax.fori_loop(0, far_limit, functools.partial(move, far), 0)
-    lax.fori_loop(far_limit, far_limit + near_limit, functools.partial(move, near), 0)
+    lax.fori_loop(0, far_limit, functools.partial(move, lambda at: far[at]), 0)
+    lax.fori_loop(
+        far_limit,
+        far_limit + near_limit,
+        functools.partial(move, lambda at: near_block(near, at, edge)),
+        0,
+    )
 
 
 def last_kernel(
@@ -501,58 +540,54 @@
     inner = [pair for pair in across if pair not in outer]
     halves = [list(range(half)), list(range(half, devices))]
 
-    other_pattern = lax.ppermute(kept(pattern), "rows", across)
     from_outer = lax.ppermute(kept(x), "rows", outer)
 
     ints = [pltpu.SMEM((entries,), jnp.int32), pltpu.SMEM((devices,), jnp.int32)]
     places = dict(rows_dev=rows_dev, devices=devices, entries=entries)
+    near_rows = SLOTS * edge + STAT_ROWS
     send = pl.pallas_call(
-        functools.partial(pack_kernel, **places),
-        out_shape=pltpu.HBM((SLOTS * half, edge, samples_dev), samples.dtype),
+        functools.partial(pack_kernel, layer=layer, edge=edge, **places),
+        out_shape=pltpu.HBM((half, near_rows, samples_dev), samples.dtype),
         in_specs=[smem, hbm],
         out_specs=hbm,
         scratch_shapes=[
             *ints,
-            pltpu.SMEM((2, entries + 1), jnp.int32),
+            pltpu.SMEM((3, entries + 1), jnp.int32),
+            pltpu.SMEM((SLOTS * half + 1,), jnp.int32),
             pltpu.VMEM((rows_dev, edge, samples_dev), samples.dtype),
+            pltpu.VMEM((half, STAT_ROWS, samples_dev), samples.dtype),
             dma((1,)),
-            dma((near_limit + 1,)),
+            dma((near_limit + 2,)),
         ],
         compiler_params=alone,
         name="pack",
     )(pattern, kept(x))
 
-    slots, lists, wanted = pl.pallas_call(
+    slots, lists = pl.pallas_call(
         functools.partial(plan_kernel, layer=layer, **places),
         out_shape=(
             jax.ShapeDtypeStruct((entries,), jnp.int32),
             jax.ShapeDtypeStruct((4, limit + 3), jnp.int32),
-            jax.ShapeDtypeStruct((SLOTS * half + 1,), jnp.int32),
-        ),
-        in_specs=[smem, smem],
-        out_specs=(smem, smem, smem),
+        ),
+        in_specs=[smem],
+        out_specs=(smem, smem),
         scratch_shapes=ints,
         compiler_params=params,
         name="plan",
-    )(pattern, other_pattern)
+    )(pattern)
 
     def within(blocks):
         return lax.all_to_all(
-            blocks.reshape(half, SLOTS, edge, samples_dev),
-            "rows",
-            split_axis=0,
-            concat_axis=0,
-            axis_index_groups=halves,
-            tiled=True,
-        ).reshape(SLOTS * half, edge, samples_dev)
+            blocks, "rows", split_axis=0, concat_axis=0, axis_index_groups=halves, tiled=True
+        )
 
     near = within(send)
     from_inner = lax.ppermute(kept(x), "rows", inner)
 
     passed = pl.pallas_call(
-        functools.partial(relay_kernel, devices=devices),
+        functools.partial(relay_kernel, devices=devices, edge=edge),
         out_shape=pltpu.HBM((SLOTS * half, edge, samples_dev), samples.dtype),
-        in_specs=[smem, vmem, vmem],
+        in_specs=[vmem, vmem, vmem],
         out_specs=hbm,
         scratch_shapes=[
             pltpu.VMEM((rows_dev, edge, samples_dev), samples.dtype),
@@ -560,8 +595,9 @@
         ],
         compiler_params=params,
         name="relay",
-    )(wanted, held(from_outer), held(from_inner))
-    far = within(passed)
+    )(held(near), held(from_outer), held(from_inner))
+    far = within(passed.reshape(half, SLOTS, edge, samples_dev))
+    far = far.reshape(SLOTS * half, edge, samples_dev)
 
     own, logs, wide = pl.pallas_call(
         functools.partial(own_kernel, devices=devices, **sizes),
@@ -588,7 +624,7 @@
         in_specs=[smem, vmem, vmem, hbm, hbm, hbm],
         out_specs=(hbm, hbm),
         scratch_shapes=[
-            pltpu.VMEM((SLOTS * half, edge, samples_dev), samples.dtype),
+            pltpu.VMEM((half, near_rows, samples_dev), samples.dtype),
             pltpu.VMEM((far_limit, edge, 2 * edge), jnp.bfloat16),
             pltpu.VMEM((rows_dev, edge, samples_dev), f32),
             pltpu.VMEM((rows_dev + 1, edge, samples_dev), f32),

time: 100 us -> 97.4 us (0.974)
  waiting for transfers between devices: 45.6 us -> 44.4 us
    ppermute x1, waiting for transfers between devices: 0.01 us -> 23.9 us  [shards(): from_inner = lax.ppermute(kept(x), 'rows', inner)]
    ppermute x1 -> x0, waiting for transfers between devices: 22.8 us -> none  [shards(): other_pattern = lax.ppermute(kept(pattern), 'rows', across)]
    all_to_all x2, waiting for transfers between devices: 7.95 us -> 5.62 us  [within(): lax.all_to_all(blocks, 'rows', split_axis=0, concat_axis=0, axis_index_gr...]
    ppermute x1 -> x0, starting transfers between devices: 1.21 us -> none  [shards(): other_pattern = lax.ppermute(kept(pattern), 'rows', across)]
    unnamed x22 -> x20, local copies, waits for them, and re-layouts: 5.39 us -> 4.85 us
  transfers between devices with their start and end apart: 6 -> 5, of which waited for: 3 -> 3; matrix products, arithmetic and copies ran while one was open for 0% -> 0% of each run, Pallas kernels for 17% -> 16%
where the time goes in v8:
time: 97.4 us; the launch traced here: 96.6 us
  waiting for transfers between devices  44.4 us (46%)
  Pallas kernels  30.1 us (31%)
  starting transfers between devices  16.5 us (17%)
  local copies, waits for them, and re-layouts  4.85 us (5%)
    ppermute x1, waiting for transfers between devices, shards(): from_inner = lax.ppermute(kept(x), 'rows', inner)  23.9 us
    all_to_all x1, waiting for transfers between devices, shards(): lax.all_to_all(kept(payload), 'rows', split_axis=0, concat_axis=0, tiled=...  14.8 us
    pallas_call x1, Pallas kernels, shards(): pl.pallas_call(functools.partial(side_kernel, **every), out_shape=(jax.Sh...  8.37 us
    all_to_all x2, starting transfers between devices, within(): lax.all_to_all(blocks, 'rows', split_axis=0, concat_axis=0, axis_index_gr...  7.69 us
    all_to_all x2, waiting for transfers between devices, within(): lax.all_to_all(blocks, 'rows', split_axis=0, concat_axis=0, axis_index_gr...  5.62 us
    pallas_call x1, Pallas kernels, shards(): pl.pallas_call(functools.partial(main_kernel, **every), out_shape=(pltpu....  5.43 us
    all_to_all x1, starting transfers between devices, shards(): lax.all_to_all(kept(payload), 'rows', split_axis=0, concat_axis=0, tiled=...  5.37 us
    pallas_call x1, Pallas kernels, shards(): pl.pallas_call(functools.partial(last_kernel, **every), out_shape=(jax.Sh...  4.95 us
  transfers between devices with their start and end apart: 5, of which 3 were waited for; matrix products, arithmetic and copies ran while one was open for 0% of the time, Pallas kernels for 16%

profile of v8, /device:TPU:16, one launch (start us, length us, event | category | flops | bytes accessed | tf_op | source)
XLA Modules:
  0.0 96.6 jit_solution(16819139936562671609)
XLA Ops:
  0.6 3.3 %pack.1 = bf16[8,264,256]{2,1,0:T(8,128)(2,1)} custom-call(s32[2,30]{1,0:T(2,128)} %bitcast.13, bf16[8,128,256]{2,1,0:T(8,128)(2,1)} %bitcast.7), custom_call_target="tpu_custom_call" | custom-call | tf_op jit(solution)/shard_map/pack/pallas_call | solution.py:548
  3.9 0.0 copy-start.4
  3.9 4.0 %all-to-all-start = ((bf16[8,264,256]{2,1,0:T(8,128)(2,1)}), bf16[8,264,256]{2,1,0:T(8,128)(2,1)S(1)}, u32[]{:S(2)}, u32[]{:S(2)}) async-start(bf16[8,264,256]{2,1,0:T(8,128)(2,1)} %pack.1), calls=%async_computation | async-start | bytes 2162688 | tf_op jit(solution)/shard_map/all_to_all | solution.py:580
  7.9 0.0 copy-done.4
  7.9 2.8 %collective-permute-start.1 = (bf16[8,128,256]{2,1,0:T(8,128)(2,1)S(1)}, bf16[8,128,256]{2,1,0:T(8,128)(2,1)S(1)}, u32[]{:S(2)}, u32[]{:S(2)}) collective-permute-start(bf16[8,128,256]{2,1,0:T(8,128)(2,1)S(1)} %bitcast.8), channel_id=1, source_target_pairs={{4,8},{5,9},{6,10},{7,11},{8,4},{9,5},{10,6},{11,7},{20,24},{21,25... | collective-permute-start | bytes 1572872 | tf_op jit(solution)/shard_map/ppermute | solution.py:585
  10.7 0.7 collective-permute-start
  11.4 23.9 %collective-permute-done.1.inner = bf16[8,128,256]{2,1,0:T(8,128)(2,1)S(1)} collective-permute-done((bf16[8,128,256]{2,1,0:T(8,128)(2,1)S(1)}, bf16[8,128,256]{2,1,0:T(8,128)(2,1)S(1)}, u32[]{:S(2)}, u32[]{:S(2)}) %collective-permute-start.1) | collective-permute-done | bytes 524320 | tf_op jit(solution)/shard_map/ppermute | solution.py:585
  35.4 0.0 collective-permute-done.outer
  35.4 0.0 all-to-all-done.near
  35.4 1.4 %relay.1 = bf16[16,128,256]{2,1,0:T(8,128)(2,1)} custom-call(bf16[8,264,256]{2,1,0:T(8,128)(2,1)S(1)} %all-to-all-done.near, bf16[8,128,256]{2,1,0:T(8,128)(2,1)S(1)} %collective-permute-done.outer, bf16[8,128,256]{2,1,0:T(8,128)(2,1)S(1)} %collective-permute-done.1.inner), custom_call_target="tpu_custom_call" | custom-call | tf_op jit(solution)/shard_map/relay/pallas_call | solution.py:587
  36.8 0.0 copy-start.8
  36.8 0.0 copy-start.5
  36.8 3.7 %all-to-all-start.1 = ((bf16[8,2,128,256]{3,2,1,0:T(8,128)(2,1)}), bf16[8,2,128,256]{3,2,1,0:T(8,128)(2,1)S(1)}, u32[]{:S(2)}, u32[]{:S(2)}) async-start(bf16[8,2,128,256]{3,2,1,0:T(8,128)(2,1)} %bitcast.15), calls=%async_computation.1 | async-start | bytes 2097152 | tf_op jit(solution)/shard_map/all_to_all | solution.py:580
  40.5 0.0 copy-done.8
  40.5 1.8 %plan.1 = (s32[30]{0:T(128)S(1)}, s32[4,33]{1,0:T(4,128)S(1)}) custom-call(s32[2,30]{1,0:T(2,128)S(1)} %bitcast.14), custom_call_target="tpu_custom_call" | custom-call | tf_op jit(solution)/shard_map/plan/pallas_call | solution.py:566
  42.3 0.0 copy-start.9
  42.4 0.0 copy-done
  42.4 0.5 copy-done.9
  42.9 0.0 copy-done.5
  42.9 1.5 %copy-done.2 = f32[30,128,128]{2,1,0:T(8,128)S(1)} copy-done((f32[30,128,128]{2,1,0:T(8,128)S(1)}, f32[30,128,128]{2,1,0:T(8,128)}, u32[]{:S(2)}) %copy-start.2) | copy-done | bytes 1966104
  44.4 4.9 %own.1 = (f32[9,128,256]{2,1,0:T(8,128)}, f32[8,128]{1,0:T(8,128)S(1)}, bf16[16,128,256]{2,1,0:T(8,128)(2,1)}) custom-call(s32[4,33]{1,0:T(4,128)S(1)} %get-tuple-element.14.lists, bf16[8,128,256]{2,1,0:T(8,128)(2,1)S(1)} %bitcast.10, f32[8,128,128]{2,1,0:T(8,128)S(1)} %copy-done.5, f32[30,128,128]{2,1,0:T(8,128)S(1)} %copy-done.2, ...), custom_call_target="tpu_custom_call" | custom-call | flops 402653184 | bytes 8388608 | tf_op jit(solution)/shard_map/own/pallas_call | solution.py:602
  49.3 5.6 %all-to-all-done.1 = bf16[8,2,128,256]{3,2,1,0:T(8,128)(2,1)S(1)} async-done(((bf16[8,2,128,256]{3,2,1,0:T(8,128)(2,1)}), bf16[8,2,128,256]{3,2,1,0:T(8,128)(2,1)S(1)}, u32[]{:S(2)}, u32[]{:S(2)}) %all-to-all-start.1) | async-done | bytes 1048608 | tf_op jit(solution)/shard_map/all_to_all | solution.py:580
  54.9 5.4 %main.1 = (s16[16,264,128]{2,1,0:T(8,128)(2,1)}, f32[8,128,256]{2,1,0:T(8,128)}) custom-call(s32[4,33]{1,0:T(4,128)S(1)} %get-tuple-element.14.lists, f32[8,128]{1,0:T(8,128)S(1)} %get-tuple-element.15.logs, bf16[16,128,256]{2,1,0:T(8,128)(2,1)S(1)} %bitcast.5, bf16[8,264,256]{2,1,0:T(8,128)(2,1)} %copy-done, f32[9,128,256]{2,1,0:T(8,128)} %get-tuple-element.16.own, ...), custom_call_target="tpu_custom_call" | custom-call | tf_op jit(solution)/shard_map/main/pallas_call | solution.py:618
  60.4 0.0 copy-start.1
  60.4 0.0 copy-start.7
  60.4 5.4 %all-to-all-start.2 = ((s16[16,264,128]{2,1,0:T(8,128)(2,1)}), s16[16,264,128]{2,1,0:T(8,128)(2,1)}, u32[]{:S(2)}, u32[]{:S(2)}) async-start(s16[16,264,128]{2,1,0:T(8,128)(2,1)} %get-tuple-element.22), calls=%async_computation.2 | async-start | bytes 2162688 | tf_op jit(solution)/shard_map/all_to_all | solution.py:645
  65.8 0.0 copy-start.3
  65.8 1.5 %copy-done.3 = f32[30,128,128]{2,1,0:T(8,128)S(1)} copy-done((f32[30,128,128]{2,1,0:T(8,128)S(1)}, f32[30,128,128]{2,1,0:T(8,128)}, u32[]{:S(2)}) %copy-start.3) | copy-done | bytes 1966104
  67.3 1.2 %copy-done.6 = f32[8,128,256]{2,1,0:T(8,128)S(1)} copy-done((f32[8,128,256]{2,1,0:T(8,128)S(1)}, f32[8,128,256]{2,1,0:T(8,128)}, u32[]{:S(2)}) %copy-start.6) | copy-done | bytes 1048600
  68.5 8.4 %side.1 = (f32[8,128,128]{2,1,0:T(8,128)}, f32[31,128,128]{2,1,0:T(8,128)}) custom-call(s32[4,33]{1,0:T(4,128)S(1)} %get-tuple-element.14.lists, bf16[8,128,256]{2,1,0:T(8,128)(2,1)S(1)} %bitcast.11, f32[8,128,128]{2,1,0:T(8,128)S(1)} %copy-done.5, f32[8,128]{1,0:T(8,128)S(1)} %bitcast.12, f32[8,128,256]{2,1,0:T(8,128)S(1)} %copy-done.6, ...), custom_call_target="tpu_custom_call" | custom-call | flops 402653184 | bytes 8388608 | tf_op jit(solution)/shard_map/side/pallas_call | solution.py:647
  76.9 14.8 %all-to-all-done.2.returned = s16[16,264,128]{2,1,0:T(8,128)(2,1)} async-done(((s16[16,264,128]{2,1,0:T(8,128)(2,1)}), s16[16,264,128]{2,1,0:T(8,128)(2,1)}, u32[]{:S(2)}, u32[]{:S(2)}) %all-to-all-start.2) | async-done | bytes 1081376 | tf_op jit(solution)/shard_map/all_to_all | solution.py:645
  91.7 4.9 %last.1 = (f32[30,128,128]{2,1,0:T(8,128)}, f32[1]{0:T(128)}) custom-call(s32[8]{0:T(128)} %count.1, s32[30]{0:T(128)} %copy-done.9, f32[31,128,128]{2,1,0:T(8,128)} %get-tuple-element.21.moved, s16[16,264,128]{2,1,0:T(8,128)(2,1)} %all-to-all-done.2.returned), custom_call_target="tpu_custom_call" | custom-call | tf_op jit(solution)/shard_map/last/pallas_call | solution.py:663
  (5 shorter events, 0.0 us)
Async XLA Ops:
  3.9 4.0 %copy-start.4 = (bf16[1024,256]{1,0:T(8,128)(2,1)S(1)}, bf16[1024,256]{1,0:T(8,128)(2,1)}, u32[]{:S(2)}) copy-start(bf16[1024,256]{1,0:T(8,128)(2,1)} %param.6) | copy-start | bytes 1572868
  3.9 31.5 %all-to-all-start = ((bf16[8,264,256]{2,1,0:T(8,128)(2,1)}), bf16[8,264,256]{2,1,0:T(8,128)(2,1)S(1)}, u32[]{:S(2)}, u32[]{:S(2)}) async-start(bf16[8,264,256]{2,1,0:T(8,128)(2,1)} %pack.1), calls=%async_computation | async-start | bytes 2162688 | tf_op jit(solution)/shard_map/all_to_all | solution.py:580
  7.9 27.4 %collective-permute-start.1 = (bf16[8,128,256]{2,1,0:T(8,128)(2,1)S(1)}, bf16[8,128,256]{2,1,0:T(8,128)(2,1)S(1)}, u32[]{:S(2)}, u32[]{:S(2)}) collective-permute-start(bf16[8,128,256]{2,1,0:T(8,128)(2,1)S(1)} %bitcast.8), channel_id=1, source_target_pairs={{4,8},{5,9},{6,10},{7,11},{8,4},{9,5},{10,6},{11,7},{20,24},{21,25... | collective-permute-start | bytes 1572872 | tf_op jit(solution)/shard_map/ppermute | solution.py:585
  10.7 24.7 %collective-permute-start = (bf16[8,128,256]{2,1,0:T(8,128)(2,1)S(1)}, bf16[8,128,256]{2,1,0:T(8,128)(2,1)S(1)}, u32[]{:S(2)}, u32[]{:S(2)}) collective-permute-start(bf16[8,128,256]{2,1,0:T(8,128)(2,1)S(1)} %bitcast.9), channel_id=1, source_target_pairs={{0,12},{1,13},{2,14},{3,15},{12,0},{13,1},{14,2},{15,3},{16,28},{1... | collective-permute-start | bytes 1572872 | tf_op jit(solution)/shard_map/ppermute | solution.py:543
  35.4 7.0 %copy-start = (bf16[8,264,256]{2,1,0:T(8,128)(2,1)}, bf16[8,264,256]{2,1,0:T(8,128)(2,1)S(1)}, u32[]{:S(2)}) copy-start(bf16[8,264,256]{2,1,0:T(8,128)(2,1)S(1)} %all-to-all-done.near) | copy-start | bytes 3244036
  36.8 3.7 %copy-start.8 = (s32[30,2]{0,1:T(2,128)S(1)}, s32[30,2]{0,1:T(2,128)}, u32[]{:S(2)}) copy-start(s32[30,2]{0,1:T(2,128)} %param.9) | copy-start | bytes 724
  36.8 6.1 %copy-start.5 = (f32[8,128,128]{2,1,0:T(8,128)S(1)}, f32[8,128,128]{2,1,0:T(8,128)}, u32[]{:S(2)}) copy-start(f32[8,128,128]{2,1,0:T(8,128)} %omega.3) | copy-start | bytes 1572868
  36.8 18.1 %all-to-all-start.1 = ((bf16[8,2,128,256]{3,2,1,0:T(8,128)(2,1)}), bf16[8,2,128,256]{3,2,1,0:T(8,128)(2,1)S(1)}, u32[]{:S(2)}, u32[]{:S(2)}) async-start(bf16[8,2,128,256]{3,2,1,0:T(8,128)(2,1)} %bitcast.15), calls=%async_computation.1 | async-start | bytes 2097152 | tf_op jit(solution)/shard_map/all_to_all | solution.py:580
  42.3 0.5 copy-start.9
  42.9 1.5 %copy-start.2 = (f32[30,128,128]{2,1,0:T(8,128)S(1)}, f32[30,128,128]{2,1,0:T(8,128)}, u32[]{:S(2)}) copy-start(f32[30,128,128]{2,1,0:T(8,128)} %off.3) | copy-start | bytes 5898244
  60.4 5.4 %copy-start.1 = (bf16[8,264,256]{2,1,0:T(8,128)(2,1)S(1)}, bf16[8,264,256]{2,1,0:T(8,128)(2,1)}, u32[]{:S(2)}) copy-start(bf16[8,264,256]{2,1,0:T(8,128)(2,1)} %copy-done) | copy-start | bytes 3244036
  60.4 5.4 %copy-start.7 = (f32[1024]{0:T(1024)S(1)}, f32[1024]{0:T(1024)}, u32[]{:S(2)}) copy-start(f32[1024]{0:T(1024)} %param.11) | copy-start | bytes 12292
  60.4 31.3 %all-to-all-start.2 = ((s16[16,264,128]{2,1,0:T(8,128)(2,1)}), s16[16,264,128]{2,1,0:T(8,128)(2,1)}, u32[]{:S(2)}, u32[]{:S(2)}) async-start(s16[16,264,128]{2,1,0:T(8,128)(2,1)} %get-tuple-element.22), calls=%async_computation.2 | async-start | bytes 2162688 | tf_op jit(solution)/shard_map/all_to_all | solution.py:645
  65.8 1.5 %copy-start.3 = (f32[30,128,128]{2,1,0:T(8,128)S(1)}, f32[30,128,128]{2,1,0:T(8,128)}, u32[]{:S(2)}) copy-start(f32[30,128,128]{2,1,0:T(8,128)} %off.3) | copy-start | bytes 5898244
  67.3 1.2 %copy-start.6 = (f32[8,128,256]{2,1,0:T(8,128)S(1)}, f32[8,128,256]{2,1,0:T(8,128)}, u32[]{:S(2)}) copy-start(f32[8,128,256]{2,1,0:T(8,128)} %get-tuple-element.18.projected) | copy-start | bytes 3145732

commit v9 on v8

--- a/solution.py
+++ b/solution.py
@@ -42,13 +42,6 @@
 def limits(entries, devices):
     half = devices // 2
     return min(entries, SLOTS * half), min(entries, SLOTS * (half - 1))
-
-
-def live_count(count, rows_dev):
-    total = count[0]
-    for k in range(1, rows_dev):
-        total = total + count[k]
-    return total
 
 
 def place(pattern, keys, sums, visit, *, rows_dev, devices, entries):
@@ -166,7 +159,7 @@
     def visit(e, row, owner, later, alive):
         later = jnp.where(alive, later, 0)
         slot = owner * SLOTS + later
-        slots[e] = slot
+        slots[e] = jnp.where(alive, slot, -1)
         index = owner - first
         near = (index >= 0) & (index < half)
         across = mirror(owner, devices, layer) - first
@@ -439,7 +432,6 @@
 
 
 def last_kernel(
-    count,
     slots,
     moved,
     returned,
@@ -458,21 +450,24 @@
     edge,
     samples_dev,
 ):
-    live = live_count(count, rows_dev)
-
     def fetch(at, part):
         return pltpu.make_async_copy(moved.at[part], held.at[part], sem_in.at[at])
 
     def store(at, part):
         return pltpu.make_async_copy(rs.at[part], result.at[part], sem_out.at[at])
 
-    width = max(k for k in range(1, 11) if entries % k == 0)
+    width = max(k for k in range(1, 7) if entries % k == 0)
     parts = [(at, pl.ds(at * width, width)) for at in range(entries // width)]
-    whole = pltpu.make_async_copy(returned, rt, sem_rt.at[0])
-    whole.start()
+    pieces = [
+        pltpu.make_async_copy(returned.at[piece], rt.at[piece], sem_rt.at[at])
+        for at, piece in enumerate(pl.ds(q, devices // 4) for q in range(0, devices, devices // 4))
+    ]
+    for piece in pieces:
+        piece.start()
     for at, part in parts:
         fetch(at, part).start()
-    whole.wait()
+    for piece in pieces:
+        piece.wait()
     codes = rt[:, SLOTS * edge :, :].astype(jnp.int32).astype(jnp.float32)
     power = codes[:, SLOTS : SLOTS + 1]
     digits = codes[:, SLOTS + 1 : SLOTS + 2] + codes[:, SLOTS + 2 : SLOTS + 3] * (1.0 / FRACTION)
@@ -481,7 +476,7 @@
     for at, part in parts:
         fetch(at, part).wait()
         for e in range(at * width, (at + 1) * width):
-            slot = slots[e]
+            slot = jnp.maximum(slots[e], 0)
             owner = divide(slot, SLOTS)
             rank = slot - owner * SLOTS
             codes = rt[owner, SLOTS * edge :, :].astype(jnp.int32).astype(jnp.float32)
@@ -489,7 +484,7 @@
             weight = jnp.exp2(code * (1.0 / LOG_STEPS) - (15.0 - HEADROOM)) * (
                 STEP_SIZE / (2.0 * samples_dev)
             )
-            weight = jnp.where(e < live, weight, 0.0)
+            weight = jnp.where(slots[e] >= 0, weight, 0.0)
             digits = rt[owner, pl.ds(pl.multiple_of(rank * edge, edge), edge), :]
             value = held[e] - digits.astype(jnp.int32).astype(jnp.float32) * weight
             rs[e] = soften(value, STEP_SIZE * PENALTY)
@@ -666,19 +661,19 @@
             jax.ShapeDtypeStruct((entries, edge, edge), f32),
             jax.ShapeDtypeStruct((1,), f32),
         ),
-        in_specs=[smem, smem, hbm, hbm],
+        in_specs=[smem, hbm, hbm],
         out_specs=(hbm, smem),
         scratch_shapes=[
             pltpu.VMEM((entries, edge, edge), f32),
             pltpu.VMEM((devices, SLOTS * edge + STAT_ROWS, edge), jnp.int16),
             pltpu.VMEM((entries, edge, edge), f32),
             dma((entries,)),
-            dma((1,)),
+            dma((4,)),
             dma((entries,)),
         ],
         compiler_params=alone,
         name="last",
-    )(block_count, slots, kept(moved), kept(returned))
+    )(slots, kept(moved), kept(returned))
     return diag_next, off_next, objective
 
 

time: 97.4 us -> 97.4 us (level)
  no operation moved by 1% of the time
where the time goes in v9:
time: 97.4 us; the launch traced here: 96.6 us
  waiting for transfers between devices  44.3 us (45%)
  Pallas kernels  30.1 us (31%)
  starting transfers between devices  16.5 us (17%)
  local copies, waits for them, and re-layouts  4.85 us (5%)
    ppermute x1, waiting for transfers between devices, shards(): from_inner = lax.ppermute(kept(x), 'rows', inner)  23.9 us
    all_to_all x1, waiting for transfers between devices, shards(): lax.all_to_all(kept(payload), 'rows', split_axis=0, concat_axis=0, tiled=...  14.8 us
    pallas_call x1, Pallas kernels, shards(): pl.pallas_call(functools.partial(side_kernel, **every), out_shape=(jax.Sh...  8.37 us
    all_to_all x2, starting transfers between devices, within(): lax.all_to_all(blocks, 'rows', split_axis=0, concat_axis=0, axis_index_gr...  7.69 us
    all_to_all x2, waiting for transfers between devices, within(): lax.all_to_all(blocks, 'rows', split_axis=0, concat_axis=0, axis_index_gr...  5.6 us
    pallas_call x1, Pallas kernels, shards(): pl.pallas_call(functools.partial(main_kernel, **every), out_shape=(pltpu....  5.43 us
    all_to_all x1, starting transfers between devices, shards(): lax.all_to_all(kept(payload), 'rows', split_axis=0, concat_axis=0, tiled=...  5.37 us
    pallas_call x1, Pallas kernels, shards(): pl.pallas_call(functools.partial(last_kernel, **every), out_shape=(jax.Sh...  4.93 us
  transfers between devices with their start and end apart: 5, of which 3 were waited for; matrix products, arithmetic and copies ran while one was open for 0% of the time, Pallas kernels for 16%

profile of v9, /device:TPU:16, one launch (start us, length us, event | category | flops | bytes accessed | tf_op | source)
XLA Modules:
  0.0 96.6 jit_solution(9151008746728520525)
XLA Ops:
  0.6 3.3 %pack.1 = bf16[8,264,256]{2,1,0:T(8,128)(2,1)} custom-call(s32[2,30]{1,0:T(2,128)} %bitcast.13, bf16[8,128,256]{2,1,0:T(8,128)(2,1)} %bitcast.7), custom_call_target="tpu_custom_call" | custom-call | tf_op jit(solution)/shard_map/pack/pallas_call | solution.py:543
  3.9 0.0 copy-start.4
  3.9 4.0 %all-to-all-start = ((bf16[8,264,256]{2,1,0:T(8,128)(2,1)}), bf16[8,264,256]{2,1,0:T(8,128)(2,1)S(1)}, u32[]{:S(2)}, u32[]{:S(2)}) async-start(bf16[8,264,256]{2,1,0:T(8,128)(2,1)} %pack.1), calls=%async_computation | async-start | bytes 2162688 | tf_op jit(solution)/shard_map/all_to_all | solution.py:575
  7.9 0.0 copy-done.4
  7.9 2.8 %collective-permute-start.1 = (bf16[8,128,256]{2,1,0:T(8,128)(2,1)S(1)}, bf16[8,128,256]{2,1,0:T(8,128)(2,1)S(1)}, u32[]{:S(2)}, u32[]{:S(2)}) collective-permute-start(bf16[8,128,256]{2,1,0:T(8,128)(2,1)S(1)} %bitcast.8), channel_id=1, source_target_pairs={{4,8},{5,9},{6,10},{7,11},{8,4},{9,5},{10,6},{11,7},{20,24},{21,25... | collective-permute-start | bytes 1572872 | tf_op jit(solution)/shard_map/ppermute | solution.py:580
  10.7 0.7 collective-permute-start
  11.4 23.9 %collective-permute-done.1.inner = bf16[8,128,256]{2,1,0:T(8,128)(2,1)S(1)} collective-permute-done((bf16[8,128,256]{2,1,0:T(8,128)(2,1)S(1)}, bf16[8,128,256]{2,1,0:T(8,128)(2,1)S(1)}, u32[]{:S(2)}, u32[]{:S(2)}) %collective-permute-start.1) | collective-permute-done | bytes 524320 | tf_op jit(solution)/shard_map/ppermute | solution.py:580
  35.4 0.0 collective-permute-done.outer
  35.4 0.0 all-to-all-done.near
  35.4 1.4 %relay.1 = bf16[16,128,256]{2,1,0:T(8,128)(2,1)} custom-call(bf16[8,264,256]{2,1,0:T(8,128)(2,1)S(1)} %all-to-all-done.near, bf16[8,128,256]{2,1,0:T(8,128)(2,1)S(1)} %collective-permute-done.outer, bf16[8,128,256]{2,1,0:T(8,128)(2,1)S(1)} %collective-permute-done.1.inner), custom_call_target="tpu_custom_call" | custom-call | tf_op jit(solution)/shard_map/relay/pallas_call | solution.py:582
  36.8 0.0 copy-start.8
  36.8 0.0 copy-start.5
  36.8 3.7 %all-to-all-start.1 = ((bf16[8,2,128,256]{3,2,1,0:T(8,128)(2,1)}), bf16[8,2,128,256]{3,2,1,0:T(8,128)(2,1)S(1)}, u32[]{:S(2)}, u32[]{:S(2)}) async-start(bf16[8,2,128,256]{3,2,1,0:T(8,128)(2,1)} %bitcast.15), calls=%async_computation.1 | async-start | bytes 2097152 | tf_op jit(solution)/shard_map/all_to_all | solution.py:575
  40.5 0.0 copy-done.8
  40.5 1.8 %plan.1 = (s32[30]{0:T(128)S(1)}, s32[4,33]{1,0:T(4,128)S(1)}) custom-call(s32[2,30]{1,0:T(2,128)S(1)} %bitcast.14), custom_call_target="tpu_custom_call" | custom-call | tf_op jit(solution)/shard_map/plan/pallas_call | solution.py:561
  42.4 0.0 copy-start.9
  42.4 0.0 copy-done
  42.4 0.5 copy-done.9
  42.9 0.0 copy-done.5
  42.9 1.5 %copy-done.2 = f32[30,128,128]{2,1,0:T(8,128)S(1)} copy-done((f32[30,128,128]{2,1,0:T(8,128)S(1)}, f32[30,128,128]{2,1,0:T(8,128)}, u32[]{:S(2)}) %copy-start.2) | copy-done | bytes 1966104
  44.4 4.9 %own.1 = (f32[9,128,256]{2,1,0:T(8,128)}, f32[8,128]{1,0:T(8,128)S(1)}, bf16[16,128,256]{2,1,0:T(8,128)(2,1)}) custom-call(s32[4,33]{1,0:T(4,128)S(1)} %get-tuple-element.14.lists, bf16[8,128,256]{2,1,0:T(8,128)(2,1)S(1)} %bitcast.10, f32[8,128,128]{2,1,0:T(8,128)S(1)} %copy-done.5, f32[30,128,128]{2,1,0:T(8,128)S(1)} %copy-done.2, ...), custom_call_target="tpu_custom_call" | custom-call | flops 402653184 | bytes 8388608 | tf_op jit(solution)/shard_map/own/pallas_call | solution.py:597
  49.3 5.6 %all-to-all-done.1 = bf16[8,2,128,256]{3,2,1,0:T(8,128)(2,1)S(1)} async-done(((bf16[8,2,128,256]{3,2,1,0:T(8,128)(2,1)}), bf16[8,2,128,256]{3,2,1,0:T(8,128)(2,1)S(1)}, u32[]{:S(2)}, u32[]{:S(2)}) %all-to-all-start.1) | async-done | bytes 1048608 | tf_op jit(solution)/shard_map/all_to_all | solution.py:575
  54.9 5.4 %main.1 = (s16[16,264,128]{2,1,0:T(8,128)(2,1)}, f32[8,128,256]{2,1,0:T(8,128)}) custom-call(s32[4,33]{1,0:T(4,128)S(1)} %get-tuple-element.14.lists, f32[8,128]{1,0:T(8,128)S(1)} %get-tuple-element.15.logs, bf16[16,128,256]{2,1,0:T(8,128)(2,1)S(1)} %bitcast.5, bf16[8,264,256]{2,1,0:T(8,128)(2,1)} %copy-done, f32[9,128,256]{2,1,0:T(8,128)} %get-tuple-element.16.own, ...), custom_call_target="tpu_custom_call" | custom-call | tf_op jit(solution)/shard_map/main/pallas_call | solution.py:613
  60.4 0.0 copy-start.1
  60.4 0.0 copy-start.7
  60.4 5.4 %all-to-all-start.2 = ((s16[16,264,128]{2,1,0:T(8,128)(2,1)}), s16[16,264,128]{2,1,0:T(8,128)(2,1)}, u32[]{:S(2)}, u32[]{:S(2)}) async-start(s16[16,264,128]{2,1,0:T(8,128)(2,1)} %get-tuple-element.22), calls=%async_computation.2 | async-start | bytes 2162688 | tf_op jit(solution)/shard_map/all_to_all | solution.py:640
  65.8 0.0 copy-start.3
  65.8 1.5 %copy-done.3 = f32[30,128,128]{2,1,0:T(8,128)S(1)} copy-done((f32[30,128,128]{2,1,0:T(8,128)S(1)}, f32[30,128,128]{2,1,0:T(8,128)}, u32[]{:S(2)}) %copy-start.3) | copy-done | bytes 1966104
  67.3 1.2 %copy-done.6 = f32[8,128,256]{2,1,0:T(8,128)S(1)} copy-done((f32[8,128,256]{2,1,0:T(8,128)S(1)}, f32[8,128,256]{2,1,0:T(8,128)}, u32[]{:S(2)}) %copy-start.6) | copy-done | bytes 1048600
  68.5 8.4 %side.1 = (f32[8,128,128]{2,1,0:T(8,128)}, f32[31,128,128]{2,1,0:T(8,128)}) custom-call(s32[4,33]{1,0:T(4,128)S(1)} %get-tuple-element.14.lists, bf16[8,128,256]{2,1,0:T(8,128)(2,1)S(1)} %bitcast.11, f32[8,128,128]{2,1,0:T(8,128)S(1)} %copy-done.5, f32[8,128]{1,0:T(8,128)S(1)} %bitcast.12, f32[8,128,256]{2,1,0:T(8,128)S(1)} %copy-done.6, ...), custom_call_target="tpu_custom_call" | custom-call | flops 402653184 | bytes 8388608 | tf_op jit(solution)/shard_map/side/pallas_call | solution.py:642
  76.9 14.8 %all-to-all-done.2.returned = s16[16,264,128]{2,1,0:T(8,128)(2,1)} async-done(((s16[16,264,128]{2,1,0:T(8,128)(2,1)}), s16[16,264,128]{2,1,0:T(8,128)(2,1)}, u32[]{:S(2)}, u32[]{:S(2)}) %all-to-all-start.2) | async-done | bytes 1081376 | tf_op jit(solution)/shard_map/all_to_all | solution.py:640
  91.7 4.9 %last.1 = (f32[30,128,128]{2,1,0:T(8,128)}, f32[1]{0:T(128)}) custom-call(s32[30]{0:T(128)} %copy-done.9, f32[31,128,128]{2,1,0:T(8,128)} %get-tuple-element.21.moved, s16[16,264,128]{2,1,0:T(8,128)(2,1)} %all-to-all-done.2.returned), custom_call_target="tpu_custom_call" | custom-call | tf_op jit(solution)/shard_map/last/pallas_call | solution.py:658
  (5 shorter events, 0.0 us)
Async XLA Ops:
  3.9 4.0 %copy-start.4 = (bf16[1024,256]{1,0:T(8,128)(2,1)S(1)}, bf16[1024,256]{1,0:T(8,128)(2,1)}, u32[]{:S(2)}) copy-start(bf16[1024,256]{1,0:T(8,128)(2,1)} %param.6) | copy-start | bytes 1572868
  3.9 31.5 %all-to-all-start = ((bf16[8,264,256]{2,1,0:T(8,128)(2,1)}), bf16[8,264,256]{2,1,0:T(8,128)(2,1)S(1)}, u32[]{:S(2)}, u32[]{:S(2)}) async-start(bf16[8,264,256]{2,1,0:T(8,128)(2,1)} %pack.1), calls=%async_computation | async-start | bytes 2162688 | tf_op jit(solution)/shard_map/all_to_all | solution.py:575
  7.9 27.4 %collective-permute-start.1 = (bf16[8,128,256]{2,1,0:T(8,128)(2,1)S(1)}, bf16[8,128,256]{2,1,0:T(8,128)(2,1)S(1)}, u32[]{:S(2)}, u32[]{:S(2)}) collective-permute-start(bf16[8,128,256]{2,1,0:T(8,128)(2,1)S(1)} %bitcast.8), channel_id=1, source_target_pairs={{4,8},{5,9},{6,10},{7,11},{8,4},{9,5},{10,6},{11,7},{20,24},{21,25... | collective-permute-start | bytes 1572872 | tf_op jit(solution)/shard_map/ppermute | solution.py:580
  10.7 24.7 %collective-permute-start = (bf16[8,128,256]{2,1,0:T(8,128)(2,1)S(1)}, bf16[8,128,256]{2,1,0:T(8,128)(2,1)S(1)}, u32[]{:S(2)}, u32[]{:S(2)}) collective-permute-start(bf16[8,128,256]{2,1,0:T(8,128)(2,1)S(1)} %bitcast.9), channel_id=1, source_target_pairs={{0,12},{1,13},{2,14},{3,15},{12,0},{13,1},{14,2},{15,3},{16,28},{1... | collective-permute-start | bytes 1572872 | tf_op jit(solution)/shard_map/ppermute | solution.py:538
  35.4 7.0 %copy-start = (bf16[8,264,256]{2,1,0:T(8,128)(2,1)}, bf16[8,264,256]{2,1,0:T(8,128)(2,1)S(1)}, u32[]{:S(2)}) copy-start(bf16[8,264,256]{2,1,0:T(8,128)(2,1)S(1)} %all-to-all-done.near) | copy-start | bytes 3244036
  36.8 3.7 %copy-start.8 = (s32[30,2]{0,1:T(2,128)S(1)}, s32[30,2]{0,1:T(2,128)}, u32[]{:S(2)}) copy-start(s32[30,2]{0,1:T(2,128)} %param.9) | copy-start | bytes 724
  36.8 6.1 %copy-start.5 = (f32[8,128,128]{2,1,0:T(8,128)S(1)}, f32[8,128,128]{2,1,0:T(8,128)}, u32[]{:S(2)}) copy-start(f32[8,128,128]{2,1,0:T(8,128)} %omega.3) | copy-start | bytes 1572868
  36.8 18.1 %all-to-all-start.1 = ((bf16[8,2,128,256]{3,2,1,0:T(8,128)(2,1)}), bf16[8,2,128,256]{3,2,1,0:T(8,128)(2,1)S(1)}, u32[]{:S(2)}, u32[]{:S(2)}) async-start(bf16[8,2,128,256]{3,2,1,0:T(8,128)(2,1)} %bitcast.15), calls=%async_computation.1 | async-start | bytes 2097152 | tf_op jit(solution)/shard_map/all_to_all | solution.py:575
  42.4 0.5 copy-start.9
  42.9 1.5 %copy-start.2 = (f32[30,128,128]{2,1,0:T(8,128)S(1)}, f32[30,128,128]{2,1,0:T(8,128)}, u32[]{:S(2)}) copy-start(f32[30,128,128]{2,1,0:T(8,128)} %off.3) | copy-start | bytes 5898244
  60.4 5.4 %copy-start.1 = (bf16[8,264,256]{2,1,0:T(8,128)(2,1)S(1)}, bf16[8,264,256]{2,1,0:T(8,128)(2,1)}, u32[]{:S(2)}) copy-start(bf16[8,264,256]{2,1,0:T(8,128)(2,1)} %copy-done) | copy-start | bytes 3244036
  60.4 5.4 %copy-start.7 = (f32[1024]{0:T(1024)S(1)}, f32[1024]{0:T(1024)}, u32[]{:S(2)}) copy-start(f32[1024]{0:T(1024)} %param.10) | copy-start | bytes 12292
  60.4 31.3 %all-to-all-start.2 = ((s16[16,264,128]{2,1,0:T(8,128)(2,1)}), s16[16,264,128]{2,1,0:T(8,128)(2,1)}, u32[]{:S(2)}, u32[]{:S(2)}) async-start(s16[16,264,128]{2,1,0:T(8,128)(2,1)} %get-tuple-element.22), calls=%async_computation.2 | async-start | bytes 2162688 | tf_op jit(solution)/shard_map/all_to_all | solution.py:640
  65.8 1.5 %copy-start.3 = (f32[30,128,128]{2,1,0:T(8,128)S(1)}, f32[30,128,128]{2,1,0:T(8,128)}, u32[]{:S(2)}) copy-start(f32[30,128,128]{2,1,0:T(8,128)} %off.3) | copy-start | bytes 5898244
  67.3 1.2 %copy-start.6 = (f32[8,128,256]{2,1,0:T(8,128)S(1)}, f32[8,128,256]{2,1,0:T(8,128)}, u32[]{:S(2)}) copy-start(f32[8,128,256]{2,1,0:T(8,128)} %get-tuple-element.18.projected) | copy-start | bytes 3145732
